TPU v7x, 32 devices: a whole 2x2x4 slice. The times are simulated.
32 devices in a mesh: dp: 8 (over y, x, core), expert: 4 (over z).
Axes of the slice: x: 2, y: 2, z: 4, core: 2. Of those that a mesh axis runs over, the one named last changes fastest.
Arguments:
- tokens: bfloat16 [4096, 2048], P(('dp', 'expert')), may hold values from -6 to 6
- w_qkv: bfloat16 [3, 2048, 2048], P(None, 'dp', 'expert'), may hold values from -0.125 to 0.125
- w_out: bfloat16 [2048, 2048], P('expert', 'dp'), may hold values from -0.5 to 0.5
- attention_norm_gain: bfloat16 [2048], P('dp'), may hold values from 0.5 to 1.5
- gain_ffn: bfloat16 [2048], P('dp'), may hold values from 0.5 to 1.5
- w_router: bfloat16 [2048, 4], P('dp'), may hold values from -0.09375 to 0.09375
- w_gate_up: bfloat16 [4, 2048, 11264], P('expert', 'dp'), may hold values from -0.125 to 0.125
- w_down: bfloat16 [4, 5632, 2048], P('expert', 'dp'), may hold values from -0.15625 to 0.15625
- lengths: int32 [8], P('dp'), may hold values from 128 to 512, as said below
- routes: int32 [4096, 2], P(('dp', 'expert')), may hold values from 0 to 3, all different within a row
- order: int32 [4096], P(('dp', 'expert')), may hold values from 0 to 127, as said below
- cotangent: bfloat16 [4096, 2048], P(('dp', 'expert')), may hold values from -6 to 6
Outputs:
- output: bfloat16 [4096, 2048], P(('dp', 'expert'))
- grad_tokens: bfloat16 [4096, 2048], P(('dp', 'expert'))
- grad_qkv: float32 [3, 2048, 2048], P(None, 'dp', 'expert')
- grad_out: float32 [2048, 2048], P('expert', 'dp')
- grad_gain_attn: float32 [2048], P('dp')
- grad_gain_ffn: float32 [2048], P('dp')
- grad_router: float32 [2048, 4], P('dp')
- grad_gate_up: float32 [4, 2048, 11264], P('expert', 'dp')
- grad_down: float32 [4, 5632, 2048], P('expert', 'dp')
Inputs may be any that keep to these rules, and one draw needn't show every extreme that they name: `lengths`: one sequence of every draw has exactly 512 live tokens. `routes`: each token slot names 2 different experts, and every expert is named somewhere. `order`: each aligned block of 128 entries holds every number of 0 to 127 once.
All inputs are finite; a program needn't handle non-finite values.
Results may differ from a plain program's by a relative error of at most 0.023.
Values may be sent and summed in bfloat16 or wider, within the bound.
A program may use at most 384 MiB of HBM per device.

v0:
```python
import jax
import jax.numpy as jnp
from jax import lax
from jax.sharding import PartitionSpec as P

HEAD_DIM = 128
FF = 5632


NORM_EPSILON = 1e-05
NEGATIVE = -1e30
THETA = 10000.0
HIGH = lax.Precision.HIGHEST


def rotary_tables(length_total, head_size):
    position = jnp.arange(length_total, dtype=jnp.float32)
    frequency = THETA ** (-(jnp.arange(head_size // 2, dtype=jnp.float32) * 2.0 / head_size))
    angles = position[:, None] * frequency[None, :]
    return (jnp.cos(angles)[:, None, :], jnp.sin(angles)[:, None, :])


def rotate(values, cosine, sine):
    half_size = values.shape[-1] // 2
    first = values[..., :half_size]
    second = values[..., half_size:]
    return jnp.concatenate(
        [first * cosine - second * sine, second * cosine + first * sine], axis=-1
    )


def rotate_back(grad_rows, cosine, sine):
    half_size = grad_rows.shape[-1] // 2
    first = grad_rows[..., :half_size]
    second = grad_rows[..., half_size:]
    return jnp.concatenate(
        [first * cosine + second * sine, second * cosine - first * sine], axis=-1
    )


def slot_table(routes, order, valid, capacity):
    row_count = routes.shape[0]
    top_count = routes.shape[1]
    pair_rank = order[:, None] + row_count * jnp.arange(top_count, dtype=jnp.int32)[None, :]
    flat_rank = pair_rank.reshape(-1)
    flat_expert = routes.reshape(-1)
    flat_valid = jnp.broadcast_to(valid[:, None], routes.shape).reshape(-1)
    earlier = (
        (flat_rank[None, :] < flat_rank[:, None])
        & (flat_expert[None, :] == flat_expert[:, None])
        & flat_valid[None, :]
    )
    slot_index = jnp.sum(earlier.astype(jnp.int32), axis=1).reshape(row_count, top_count)
    kept_pair = valid[:, None] & (slot_index < capacity)
    target = routes * capacity + jnp.minimum(slot_index, capacity - 1)
    return (target, kept_pair)


def masked_scores(query, key_rows, allowed):
    scale = query.shape[-1] ** (-0.5)
    raw = jnp.einsum("qhd,khd->hqk", query, key_rows, preferred_element_type=jnp.float32) * scale
    return jnp.where(allowed[None], raw, NEGATIVE)


def fetch_expert(w_gate_up, w_down):
    gate_up_full, down_full = (
        lax.all_gather(w_gate_up, "dp", axis=1, tiled=True),
        lax.all_gather(w_down, "dp", axis=1, tiled=True),
    )
    return (gate_up_full[0], down_full[0])


def contract_first(left, right):
    return lax.dot_general(
        left, right, (((0,), (0,)), ((), ())), preferred_element_type=jnp.float32
    )


def contract_last(left, right):
    return lax.dot_general(
        left, right, (((1,), (1,)), ((), ())), preferred_element_type=jnp.float32
    )


def on_device(
    tokens,
    w_qkv,
    w_out,
    attention_norm_gain,
    gain_ffn,
    w_router,
    w_gate_up,
    w_down,
    lengths,
    routes,
    order,
    cotangent,
):
    group_size = lax.axis_size("expert")
    tok_dev = tokens.shape[0]
    seq_len = tok_dev * group_size
    width = tokens.shape[1]
    top_count = routes.shape[1]
    capacity = tok_dev * top_count // group_size
    head_size = HEAD_DIM
    local_width = w_qkv.shape[2]
    heads_local = local_width // head_size
    ff_width = FF
    qkv_full, out_full, first_norm_gain, gain_two, router_full = (
        lax.all_gather(w_qkv, "dp", axis=1, tiled=True),
        lax.all_gather(w_out, "dp", axis=1, tiled=True),
        lax.all_gather(attention_norm_gain, "dp", axis=0, tiled=True),
        lax.all_gather(gain_ffn, "dp", axis=0, tiled=True),
        lax.all_gather(w_router, "dp", axis=0, tiled=True),
    )
    first_norm_gain = first_norm_gain.astype(jnp.float32)
    gain_two = gain_two.astype(jnp.float32)
    own_start = lax.axis_index("expert") * tok_dev
    own_position = own_start + jnp.arange(tok_dev, dtype=jnp.int32)
    live_own = own_position < lengths[0]
    live_rows = live_own.astype(jnp.float32)[:, None]
    inputs_float = tokens.astype(jnp.float32)
    first_inverse_rms = lax.rsqrt(
        jnp.mean(inputs_float * inputs_float, axis=-1, keepdims=True) + NORM_EPSILON
    )
    input_normalized_hat = inputs_float * first_inverse_rms
    normalized_input = (input_normalized_hat * first_norm_gain).astype(jnp.bfloat16)
    whole = lax.all_gather(normalized_input, "expert", axis=0, tiled=True)
    cosine, sine = rotary_tables(seq_len, head_size)
    projected = jnp.einsum("td,cde->cte", whole, qkv_full, preferred_element_type=jnp.float32)
    query = rotate(projected[0].reshape(seq_len, heads_local, head_size), cosine, sine).astype(
        jnp.bfloat16
    )
    key_rows = rotate(projected[1].reshape(seq_len, heads_local, head_size), cosine, sine).astype(
        jnp.bfloat16
    )
    value = projected[2].astype(jnp.bfloat16).reshape(seq_len, heads_local, head_size)
    position = jnp.arange(seq_len, dtype=jnp.int32)
    live_all = position < lengths[0]
    allowed = (position[None, :] <= position[:, None]) & live_all[None, :]
    scores = masked_scores(query, key_rows, allowed)
    top_score = jnp.max(scores, axis=-1, keepdims=True)
    exponent = jnp.exp(scores - top_score)
    row_total = jnp.sum(exponent, axis=-1, keepdims=True)
    probs = exponent / row_total
    log_total = top_score + jnp.log(row_total)
    probs_low = probs.astype(jnp.bfloat16)
    attended = jnp.einsum("hqk,khd->qhd", probs_low, value, preferred_element_type=jnp.float32)
    attended = attended.reshape(seq_len, local_width).astype(jnp.bfloat16)
    attn_part = jnp.dot(attended, out_full, preferred_element_type=jnp.float32)
    attn_own = lax.psum_scatter(
        attn_part.astype(jnp.bfloat16), "expert", scatter_dimension=0, tiled=True
    ).astype(jnp.float32)
    resid = inputs_float + attn_own
    inverse_two = lax.rsqrt(jnp.mean(resid * resid, axis=-1, keepdims=True) + NORM_EPSILON)
    hhat = resid * inverse_two
    hidden_in = (hhat * gain_two).astype(jnp.bfloat16)
    logits = jnp.dot(hidden_in, router_full, preferred_element_type=jnp.float32)
    chosen = jnp.take_along_axis(logits, routes, axis=1)
    gates = jax.nn.softmax(chosen, axis=1)
    target, kept_pair = slot_table(routes, order, live_own, capacity)
    slot_ids = jnp.arange(group_size * capacity, dtype=jnp.int32)
    pair_hits = (slot_ids[:, None, None] == target[None]) & kept_pair[None]
    select = jnp.sum(pair_hits.astype(jnp.float32), axis=2).astype(jnp.bfloat16)
    sent = jnp.dot(select, hidden_in, preferred_element_type=jnp.float32).astype(jnp.bfloat16)
    received = lax.all_to_all(
        sent.reshape(group_size, capacity, width), "expert", split_axis=0, concat_axis=0, tiled=True
    )
    dispatched = received.reshape(group_size * capacity, width)
    gate_up_full, down_full = fetch_expert(w_gate_up, w_down)
    gate_up = jnp.dot(dispatched, gate_up_full, preferred_element_type=jnp.float32)
    gate = gate_up[:, :ff_width]
    upward = gate_up[:, ff_width:]
    sigmoid = jax.nn.sigmoid(gate)
    activated = (gate * sigmoid * upward).astype(jnp.bfloat16)
    expert_out = jnp.dot(activated, down_full, preferred_element_type=jnp.float32).astype(
        jnp.bfloat16
    )
    returned = lax.all_to_all(
        expert_out.reshape(group_size, capacity, width),
        "expert",
        split_axis=0,
        concat_axis=0,
        tiled=True,
    )
    returned = returned.reshape(group_size * capacity, width)
    moe = jnp.zeros_like(resid)
    picked_rows = []
    for index in range(top_count):
        one_hot = pair_hits[:, :, index].astype(jnp.bfloat16)
        picked = contract_first(one_hot, returned)
        picked_rows.append(picked)
        moe = moe + gates[:, index : index + 1] * picked
    output = (live_rows * (resid + moe)).astype(jnp.bfloat16)
    d_out = live_rows * cotangent.astype(jnp.float32)
    d_gates_list = []
    d_back = jnp.zeros((group_size * capacity, width), jnp.float32)
    for index in range(top_count):
        d_gates_list.append(jnp.sum(d_out * picked_rows[index], axis=-1))
        weighted = (gates[:, index : index + 1] * d_out).astype(jnp.bfloat16)
        d_back = d_back + jnp.dot(
            pair_hits[:, :, index].astype(jnp.bfloat16),
            weighted,
            preferred_element_type=jnp.float32,
        )
    d_gates = jnp.stack(d_gates_list, axis=1)
    d_back = d_back.astype(jnp.bfloat16)
    d_out_rows = lax.all_to_all(
        d_back.reshape(group_size, capacity, width),
        "expert",
        split_axis=0,
        concat_axis=0,
        tiled=True,
    )
    d_out_rows = d_out_rows.reshape(group_size * capacity, width)
    gate_up_back, down_back = fetch_expert(w_gate_up, w_down)
    d_activated = contract_last(d_out_rows, down_back)
    columns = activated
    grad_down = lax.psum_scatter(
        contract_first(columns, d_out_rows), "dp", scatter_dimension=0, tiled=True
    )
    silu_gate = gate * sigmoid
    d_gate = d_activated * upward * sigmoid * (1.0 + gate * (1.0 - sigmoid))
    d_up = d_activated * silu_gate
    d_gate_up = jnp.concatenate([d_gate, d_up], axis=1).astype(jnp.bfloat16)
    columns = dispatched
    grad_gate_up = lax.psum_scatter(
        contract_first(columns, d_gate_up), "dp", scatter_dimension=0, tiled=True
    )
    d_rows = contract_last(d_gate_up, gate_up_back).astype(jnp.bfloat16)
    d_sent = lax.all_to_all(
        d_rows.reshape(group_size, capacity, width),
        "expert",
        split_axis=0,
        concat_axis=0,
        tiled=True,
    )
    d_hidden = contract_first(select, d_sent.reshape(group_size * capacity, width))
    d_chosen = gates * (d_gates - jnp.sum(gates * d_gates, axis=1, keepdims=True))
    expert_ids = jnp.arange(group_size, dtype=jnp.int32)
    route_hits = (routes[:, :, None] == expert_ids[None, None, :]).astype(jnp.float32)
    d_logits = jnp.sum(route_hits * d_chosen[:, :, None], axis=1)
    router_f = router_full.astype(jnp.float32)
    d_hidden = d_hidden + jnp.dot(
        d_logits, router_f.T, precision=HIGH, preferred_element_type=jnp.float32
    )
    router_part = jnp.dot(
        hidden_in.astype(jnp.float32).T,
        d_logits,
        precision=HIGH,
        preferred_element_type=jnp.float32,
    )
    gain_two_part = jnp.sum(d_hidden * hhat, axis=0)
    scaled_two = d_hidden * gain_two
    d_resid = d_out + inverse_two * (
        scaled_two - hhat * jnp.mean(scaled_two * hhat, axis=-1, keepdims=True)
    )
    d_attn = d_resid.astype(jnp.bfloat16)
    whole_grad = lax.all_gather(d_attn, "expert", axis=0, tiled=True)
    out_part = contract_first(attended, whole_grad)
    d_attended = contract_last(whole_grad, out_full).astype(jnp.bfloat16)
    d_heads = d_attended.reshape(seq_len, heads_local, head_size)
    probs = jnp.exp(masked_scores(query, key_rows, allowed) - log_total)
    probs_low = probs.astype(jnp.bfloat16)
    d_value = jnp.einsum(
        "hqk,qhd->khd", probs_low, d_heads, preferred_element_type=jnp.float32
    ).astype(jnp.bfloat16)
    d_probs = jnp.einsum("qhd,khd->hqk", d_heads, value, preferred_element_type=jnp.float32)
    row_delta = jnp.sum(probs * d_probs, axis=-1, keepdims=True)
    d_scores = (probs * (d_probs - row_delta)).astype(jnp.bfloat16)
    scale = head_size ** (-0.5)
    d_query = (
        jnp.einsum("hqk,khd->qhd", d_scores, key_rows, preferred_element_type=jnp.float32) * scale
    )
    d_key = jnp.einsum("hqk,qhd->khd", d_scores, query, preferred_element_type=jnp.float32) * scale
    d_query_pre = (
        rotate_back(d_query, cosine, sine).reshape(seq_len, local_width).astype(jnp.bfloat16)
    )
    d_key_pre = rotate_back(d_key, cosine, sine).reshape(seq_len, local_width).astype(jnp.bfloat16)
    d_projected = jnp.stack([d_query_pre, d_key_pre, d_value.reshape(seq_len, local_width)])
    qkv_part = jnp.einsum("td,cte->cde", whole, d_projected, preferred_element_type=jnp.float32)
    d_normed_part = jnp.einsum(
        "cte,cde->td", d_projected, qkv_full, preferred_element_type=jnp.float32
    )
    grad_normalized = lax.psum_scatter(
        d_normed_part.astype(jnp.bfloat16), "expert", scatter_dimension=0, tiled=True
    ).astype(jnp.float32)
    first_gain_piece = jnp.sum(grad_normalized * input_normalized_hat, axis=0)
    first_scaled_input = grad_normalized * first_norm_gain
    grad_tokens = d_resid + first_inverse_rms * (
        first_scaled_input
        - input_normalized_hat
        * jnp.mean(first_scaled_input * input_normalized_hat, axis=-1, keepdims=True)
    )
    gain_one_sum, gain_two_sum, router_sum = (
        lax.psum(first_gain_piece.astype(jnp.bfloat16), "expert").astype(jnp.float32),
        lax.psum(gain_two_part.astype(jnp.bfloat16), "expert").astype(jnp.float32),
        lax.psum(router_part.astype(jnp.bfloat16), "expert").astype(jnp.float32),
    )
    grad_qkv, grad_out, grad_gain_attn, grad_gain_ffn, grad_router = (
        lax.psum_scatter(qkv_part, "dp", scatter_dimension=1, tiled=True),
        lax.psum_scatter(out_part, "dp", scatter_dimension=1, tiled=True),
        lax.psum_scatter(gain_one_sum, "dp", scatter_dimension=0, tiled=True),
        lax.psum_scatter(gain_two_sum, "dp", scatter_dimension=0, tiled=True),
        lax.psum_scatter(router_sum, "dp", scatter_dimension=0, tiled=True),
    )
    return (
        output,
        grad_tokens.astype(jnp.bfloat16),
        grad_qkv,
        grad_out,
        grad_gain_attn,
        grad_gain_ffn,
        grad_router,
        grad_gate_up[None],
        grad_down[None],
    )


def solution(mesh):
    placed = (
        P(("dp", "expert"), None),
        P(None, "dp", "expert"),
        P("expert", "dp"),
        P("dp"),
        P("dp"),
        P("dp", None),
        P("expert", "dp", None),
        P("expert", "dp", None),
        P("dp"),
        P(("dp", "expert"), None),
        P(("dp", "expert")),
        P(("dp", "expert"), None),
    )
    return jax.shard_map(
        on_device,
        mesh=mesh,
        in_specs=placed,
        out_specs=(
            P(("dp", "expert"), None),
            P(("dp", "expert"), None),
            P(None, "dp", "expert"),
            P("expert", "dp"),
            P("dp"),
            P("dp"),
            P("dp", None),
            P("expert", "dp", None),
            P("expert", "dp", None),
        ),
        check_vma=False,
    )
```

profile of v0, /device:TPU:0, one launch (start us, length us, event | category | flops | bytes accessed | tf_op | source)
XLA Modules:
  0.0 1797.3 jit_solution(4819094658459941075)
XLA Ops:
  9.1 10.3 all-gather
  19.5 2.0 fusion.43
  21.6 2.3 copy.189
  26.2 1.7 fusion.55
  27.9 40.1 %all-gather.9.cloned.1.call-done = bf16[512,2048]{1,0:T(8,128)(2,1)} async-done(((bf16[128,2048]{1,0:T(8,128)(2,1)}), bf16[512,2048]{1,0:T(8,128)(2,1)}) %all-gather.9.cloned.1.call-update) | async-done | bytes 2097168 | tf_op jit(solution)/shard_map/all_gather | solution.py:128
  67.9 47.9 %all-gather.11.cloned.1.call-done = bf16[3,2048,512]{1,2,0:T(8,128)(2,1)} async-done(((bf16[3,256,512]{1,2,0:T(8,128)(2,1)}), bf16[3,2048,512]{1,2,0:T(8,128)(2,1)}) %all-gather.11.cloned.1.call-update) | async-done | bytes 6291472 | tf_op jit(solution)/shard_map/all_gather | solution.py:110
  115.8 6.2 fusion.26
  124.1 1.4 copy.232
  126.4 2.4 copy.234
  131.4 2.6 subtract_convert_fusion.3
  136.1 1.4 copy-done
  138.4 7.5 all-gather.13.cloned.1.call-done
  145.9 4.2 convolution_convert_fusion
  151.4 8.8 all-gather.1
  162.4 31.7 %reduce-scatter.12.cloned.1.call-done = bf16[128,2048]{1,0:T(8,128)(2,1)} async-done(((bf16[512,2048]{1,0:T(8,128)(2,1)}), bf16[128,2048]{1,0:T(8,128)(2,1)}) %reduce-scatter.12.cloned.1.call-update) | async-done | bytes 524304 | tf_op jit(solution)/shard_map/reduce_scatter | solution.py:151
  197.2 29.1 %all_to_all.20 = bf16[4,64,2048]{2,1,0:T(8,128)(2,1)S(1)} all-to-all(bf16[4,64,2048]{2,1,0:T(8,128)(2,1)S(1)} %bitcast.116), channel_id=1, replica_groups=mesh['dp'=8,'expert'=4] {'expert'}, dimensions={0} | all-to-all | bytes 2097152 | tf_op jit(solution)/shard_map/all_to_all | solution.py:166
  226.2 183.9 %all-gather.15.cloned.1.call-done = bf16[1,2048,11264]{2,1,0:T(8,128)(2,1)} async-done(((bf16[1,256,11264]{2,1,0:T(8,128)(2,1)}), bf16[1,2048,11264]{2,1,0:T(8,128)(2,1)}) %all-gather.15.cloned.1.call-update) | async-done | bytes 46137360 | tf_op jit(solution)/shard_map/all_gather | solution.py:67
  410.1 25.8 %fusion.2 = f32[256,11264]{1,0:T(8,128)} fusion(bf16[256,2048]{1,0:T(8,128)(2,1)S(1)} %bitcast.114, bf16[1,2048,11264]{2,1,0:T(8,128)(2,1)} %all-gather.15.cloned.1.call-done), kind=kOutput, calls=%fused_computation.3 | convolution fusion | flops 11811160064 | bytes 58720256 | tf_op jit(solution)/shard_map/dot_general | solution.py:171
  436.0 5.2 multiply_convert_fusion.2
  441.2 87.4 %all-gather.17.cloned.1.call-done = bf16[1,5632,2048]{2,1,0:T(8,128)(2,1)} async-done(((bf16[1,704,2048]{2,1,0:T(8,128)(2,1)}), bf16[1,5632,2048]{2,1,0:T(8,128)(2,1)}) %all-gather.17.cloned.1.call-update) | async-done | bytes 23068688 | tf_op jit(solution)/shard_map/all_gather | solution.py:68
  528.5 12.0 fusion.12
  540.6 4.6 all-to-all-start.1
  545.5 8.9 all_gather.34
  556.4 2.4 gather_fusion
  559.5 1.5 copy.196
  562.2 9.2 all-to-all-done.1
  571.4 1.6 fusion.58
  574.1 2.8 multiply_reduce_fusion.4
  579.3 27.9 %all_to_all.21 = bf16[4,64,2048]{2,1,0:T(8,128)(2,1)S(1)} all-to-all(bf16[4,64,2048]{2,1,0:T(8,128)(2,1)S(1)} %bitcast.119), channel_id=1, replica_groups=mesh['dp'=8,'expert'=4] {'expert'}, dimensions={0} | all-to-all | bytes 2097152 | tf_op jit(solution)/shard_map/all_to_all | solution.py:208
  607.2 25.1 %multiply_convert_fusion.1 = (bf16[256,5632]{1,0:T(8,128)(2,1)}, bf16[256,5632]{1,0:T(8,128)(2,1)}) fusion(f32[256,11264]{1,0:T(8,128)} %fusion.2, bf16[256,2048]{1,0:T(8,128)(2,1)S(1)} %bitcast.120, bf16[1,5632,2048]{2,1,0:T(8,128)(2,1)} %all-gather.17.cloned.1.call-done), kind=kOutput, calls=%fused_computation.11 | convolution fusion | flops 5924323328 | bytes 41418752 | tf_op jit(solution)/shard_map/dot_general | solution.py:80
  632.4 21.1 %fusion.16 = bf16[256,2048]{1,0:T(8,128)(2,1)} fusion(bf16[1,2048,11264]{2,1,0:T(8,128)(2,1)} %all-gather.15.cloned.1.call-done, bf16[256,5632]{1,0:T(8,128)(2,1)} %get-tuple-element.81, bf16[256,5632]{1,0:T(8,128)(2,1)} %get-tuple-element.80), kind=kOutput, calls=%fused_computation.31 | convolution fusion | flops 11823218688 | bytes 52953088 | tf_op jit(solution)/shard_map/dot_general | solution.py:80
  653.5 4.4 all-to-all-start.3
  658.1 24.7 %all-to-all-done.3 = bf16[4,64,2048]{2,1,0:T(8,128)(2,1)} async-done(((bf16[4,64,2048]{2,1,0:T(8,128)(2,1)}), bf16[4,64,2048]{2,1,0:T(8,128)(2,1)}, u32[]{:S(2)}, u32[]{:S(2)}) %all-to-all-start.3) | async-done | bytes 1048608 | tf_op jit(solution)/shard_map/all_to_all | solution.py:231
  682.8 1.6 fusion.82
  684.5 2.0 multiply_reduce_fusion.1
  689.1 43.9 %all-gather.19.cloned.1.call-done = bf16[512,2048]{1,0:T(8,128)(2,1)} async-done(((bf16[128,2048]{1,0:T(8,128)(2,1)}), bf16[512,2048]{1,0:T(8,128)(2,1)}) %all-gather.19.cloned.1.call-update) | async-done | bytes 2097168 | tf_op jit(solution)/shard_map/all_gather | solution.py:259
  733.0 3.7 convolution_convert_fusion.3
  736.7 1.6 fusion.35
  740.6 1.8 fusion.33
  742.3 2.0 fusion.34
  744.4 2.0 copy.213
  746.4 3.3 add_convert_fusion.1
  749.7 1.5 pad_maximum_fusion.10
  751.3 2.0 copy.205
  753.3 2.0 copy.211
  755.3 2.0 copy.209
  757.4 2.0 copy.212
  759.4 8.0 bitcast_convert_fusion
  767.5 1.4 convolution_convert_fusion.2
  768.9 41.3 %reduce-scatter.14.cloned.1.call-done = bf16[128,2048]{1,0:T(8,128)(2,1)} async-done(((bf16[512,2048]{1,0:T(8,128)(2,1)}), bf16[128,2048]{1,0:T(8,128)(2,1)}) %reduce-scatter.14.cloned.1.call-update) | async-done | bytes 524304 | tf_op jit(solution)/shard_map/reduce_scatter | solution.py:285
  810.2 1.5 fusion.45
  811.7 17.1 all-reduce.4
  830.4 10.1 convolution_bitcast_fusion
  840.5 5.0 fusion.80
  845.6 19.3 %fusion.81 = f32[5632,2048]{1,0:T(8,128)} fusion(bf16[256,5632]{1,0:T(8,128)(2,1)S(1)} %multiply_convert_fusion.2, bf16[256,2048]{1,0:T(8,128)(2,1)} %bitcast.121), kind=kOutput, calls=%fused_computation.154 | convolution fusion | flops 5905580032 | bytes 50069504 | tf_op jit(solution)/shard_map/dot_general | solution.py:74
  866.1 43.1 %fusion.9 = f32[2048,11264]{1,0:T(8,128)} fusion(bf16[256,2048]{1,0:T(8,128)(2,1)S(1)} %bitcast.115, bf16[256,5632]{1,0:T(8,128)(2,1)} %get-tuple-element.81, bf16[256,5632]{1,0:T(8,128)(2,1)} %get-tuple-element.80), kind=kOutput, calls=%fused_computation.23 | convolution fusion | flops 11822694400 | bytes 99090432 | tf_op jit(solution)/shard_map/dot_general | solution.py:74
  911.1 23.6 %all-reduce.3 = (f32[2048]{0:T(1024)S(1)}, f32[2048]{0:T(1024)S(1)}) all-reduce(bf16[2048]{0:T(1024)(128)(2,1)S(1)} %get-tuple-element.71, bf16[2048]{0:T(1024)(128)(2,1)S(1)} %get-tuple-element.72), channel_id=6, replica_groups=mesh['dp'=8,'expert'=4] {'dp'}, use_global_device_ids=true, to_apply=%region_21.22.clone | all-reduce | flops 4096 | bytes 24576
  936.0 3.5 fusion.42
  939.5 1.6 copy.230
  941.1 19.7 %reduce-scatter.16.cloned.1.call-done = f32[3,256,512]{1,2,0:T(8,128)} async-done(((f32[3,2048,512]{1,2,0:T(8,128)}), f32[3,256,512]{1,2,0:T(8,128)}) %reduce-scatter.16.cloned.1.call-update) | async-done | bytes 1572880 | tf_op jit(solution)/shard_map/reduce_scatter | solution.py:301
  960.8 3.0 copy.216
  963.9 52.3 %reduce-scatter.18.cloned.1.call-done = f32[512,256]{1,0:T(8,128)} async-done(((f32[512,2048]{1,0:T(8,128)}), f32[512,256]{1,0:T(8,128)}) %reduce-scatter.18.cloned.1.call-update) | async-done | bytes 524304 | tf_op jit(solution)/shard_map/reduce_scatter | solution.py:302
  1016.1 268.9 %reduce-scatter.20.cloned.1.call-done = f32[704,2048]{1,0:T(8,128)} async-done(((f32[5632,2048]{1,0:T(8,128)}), f32[704,2048]{1,0:T(8,128)}) %reduce-scatter.20.cloned.1.call-update) | async-done | bytes 5767184 | tf_op jit(solution)/shard_map/reduce_scatter | solution.py:219
  1285.0 505.4 %reduce-scatter.24.cloned.1.call-done = f32[256,11264]{1,0:T(8,128)} async-done(((f32[2048,11264]{1,0:T(8,128)}), f32[256,11264]{1,0:T(8,128)}) %reduce-scatter.24.cloned.1.call-update) | async-done | bytes 11534352
  (222 shorter events, 36.3 us)
Async XLA Ops:
  7.2 60.7 %all-gather.9.cloned.1.call-start = ((), (), s32[]{:S(2)}) async-start(), calls=%async_computation.11 | async-start | bytes 2621440 | tf_op jit(solution)/shard_map/all_gather | solution.py:128
  8.5 113.6 %copy-start.48 = (f32[128]{0:T(128)}, f32[128]{0:T(128)S(1)}, u32[]{:S(2)}) copy-start(f32[128]{0:T(128)S(1)} %add_rsqrt_fusion.1) | copy-start | bytes 1540
  19.5 102.6 %copy-start.34 = (f32[8,1,256]{2,1,0:T(1,128)}, f32[8,1,256]{2,1,0:T(1,128)S(1)}, u32[]{:S(2)}) copy-start(f32[8,1,256]{2,1,0:T(1,128)S(1)} %convert_element_type.200) | copy-start | bytes 24580
  21.5 94.3 %all-gather.11.cloned.1.call-start = ((), (), s32[]{:S(2)}) async-start(), calls=%async_computation.12 | async-start | bytes 7077888 | tf_op jit(solution)/shard_map/all_gather | solution.py:110
  23.9 122.0 %all-gather.13.cloned.1.call-start = ((), (), s32[]{:S(2)}) async-start(), calls=%async_computation.13 | async-start | bytes 2359296 | tf_op jit(solution)/shard_map/all_gather | solution.py:111
  24.6 169.5 %reduce-scatter.12.cloned.1.call-start = ((), (), s32[]{:S(2)}) async-start(), calls=%async_computation.14 | async-start | bytes 2621440 | tf_op jit(solution)/shard_map/reduce_scatter | solution.py:151
  27.9 103.6 %copy-start.23 = (f32[512,64]{1,0:T(8,128)}, f32[512,64]{1,0:T(8,128)S(1)}, u32[]{:S(2)}) copy-start(f32[512,64]{1,0:T(8,128)S(1)} %get-tuple-element.104) | copy-start | bytes 393220
  124.1 4.7 copy-start.27
  131.4 2.6 copy-start.28
  134.0 2.0 copy-start.12
  134.0 3.4 copy-start.25
  135.4 3.0 copy-start.36
  136.1 2.3 copy-start.38
  138.4 12.4 copy-start.29
  150.1 10.9 copy-start.63
  150.2 11.1 copy-start.40
  150.2 44.0 %copy-start.2 = (bf16[128,2048]{1,0:T(8,128)(2,1)S(1)}, bf16[128,2048]{1,0:T(8,128)(2,1)}, u32[]{:S(2)}) copy-start(bf16[128,2048]{1,0:T(8,128)(2,1)} %param.12) | copy-start | bytes 1572868
  150.2 259.9 %all-gather.15.cloned.1.call-start = ((), (), s32[]{:S(2)}) async-start(), calls=%async_computation.15 | async-start | bytes 51904512 | tf_op jit(solution)/shard_map/all_gather | solution.py:67
  150.8 377.8 %all-gather.17.cloned.1.call-start = ((), (), s32[]{:S(2)}) async-start(), calls=%async_computation.16 | async-start | bytes 25952256 | tf_op jit(solution)/shard_map/all_gather | solution.py:68
  160.2 275.7 %copy-start.30 = (f32[8,1,256]{2,1,0:T(1,128)}, f32[8,1,256]{2,1,0:T(1,128)S(1)}, u32[]{:S(2)}) copy-start(f32[8,1,256]{2,1,0:T(1,128)S(1)} %convert_element_type.201) | copy-start | bytes 24580
  162.1 32.1 %copy-start.50 = (pred[128,2]{0,1:T(4,128)(4,1)}, pred[128,2]{0,1:T(4,128)(4,1)S(1)}, u32[]{:S(2)}) copy-start(pred[128,2]{0,1:T(4,128)(4,1)S(1)} %copy.199) | copy-start | bytes 772
  162.3 273.6 %copy-start.43 = (s32[128,2]{0,1:T(2,128)}, s32[128,2]{0,1:T(2,128)S(1)}, u32[]{:S(2)}) copy-start(s32[128,2]{0,1:T(2,128)S(1)} %multiply_add_fusion.1) | copy-start | bytes 3076
  195.4 240.5 %copy-start.46 = (f32[128]{0:T(128)}, f32[128]{0:T(128)S(1)}, u32[]{:S(2)}) copy-start(f32[128]{0:T(128)S(1)} %add_rsqrt_fusion) | copy-start | bytes 1540
  196.7 213.4 %copy-start.11 = (bf16[128,2048]{1,0:T(8,128)(2,1)}, bf16[128,2048]{1,0:T(8,128)(2,1)S(1)}, u32[]{:S(2)}) copy-start(bf16[128,2048]{1,0:T(8,128)(2,1)S(1)} %multiply_convert_fusion.7) | copy-start | bytes 1572868
  226.2 183.9 %copy-start.20 = (bf16[4,64,2048]{2,1,0:T(8,128)(2,1)}, bf16[4,64,2048]{2,1,0:T(8,128)(2,1)S(1)}, u32[]{:S(2)}) copy-start(bf16[4,64,2048]{2,1,0:T(8,128)(2,1)S(1)} %all_to_all.20) | copy-start | bytes 3145732
  441.2 104.3 %copy-start.60 = (bf16[256,4]{0,1:T(4,128)(2,1)S(1)}, bf16[256,4]{0,1:T(4,128)(2,1)}, u32[]{:S(2)}) copy-start(bf16[256,4]{0,1:T(4,128)(2,1)} %param.17) | copy-start | bytes 6148
  540.6 30.9 %all-to-all-start.1 = ((bf16[4,64,2048]{2,1,0:T(8,128)(2,1)}), bf16[4,64,2048]{2,1,0:T(8,128)(2,1)}, u32[]{:S(2)}, u32[]{:S(2)}) async-start(bf16[4,64,2048]{2,1,0:T(8,128)(2,1)} %bitcast.129), calls=%async_computation.2 | async-start | bytes 2097152 | tf_op jit(solution)/shard_map/all_to_all | solution.py:179
  558.7 19.4 %copy-start.41 = (f32[128]{0:T(128)S(1)}, f32[128]{0:T(128)}, u32[]{:S(2)}) copy-start(f32[128]{0:T(128)} %get-tuple-element.76) | copy-start | bytes 1540
  561.7 15.2 copy-start.59
  571.4 5.5 copy-start.62
  571.4 6.8 copy-start.5
  578.2 29.0 %copy-start.44 = (f32[128,2]{0,1:T(2,128)}, f32[128,2]{0,1:T(2,128)S(1)}, u32[]{:S(2)}) copy-start(f32[128,2]{0,1:T(2,128)S(1)} %get-tuple-element.75) | copy-start | bytes 3076
  578.2 29.0 %copy-start.51 = (f32[128]{0:T(128)}, f32[128]{0:T(128)S(1)}, u32[]{:S(2)}) copy-start(f32[128]{0:T(128)S(1)} %get-tuple-element.102) | copy-start | bytes 1540
  578.2 29.0 %copy-start.53 = (f32[128]{0:T(128)}, f32[128]{0:T(128)S(1)}, u32[]{:S(2)}) copy-start(f32[128]{0:T(128)S(1)} %get-tuple-element.103) | copy-start | bytes 1540
  607.2 25.1 %copy-start.22 = (bf16[4,64,2048]{2,1,0:T(8,128)(2,1)}, bf16[4,64,2048]{2,1,0:T(8,128)(2,1)S(1)}, u32[]{:S(2)}) copy-start(bf16[4,64,2048]{2,1,0:T(8,128)(2,1)S(1)} %all_to_all.21) | copy-start | bytes 3145732
  632.3 25.6 %copy-start.45 = (f32[128,2]{0,1:T(2,128)S(1)}, f32[128,2]{0,1:T(2,128)}, u32[]{:S(2)}) copy-start(f32[128,2]{0,1:T(2,128)} %copy-done.44) | copy-start | bytes 3076
  632.3 25.6 %copy-start.56 = (f32[128]{0:T(128)S(1)}, f32[128]{0:T(128)}, u32[]{:S(2)}) copy-start(f32[128]{0:T(128)} %copy-done.55) | copy-start | bytes 1540
  632.4 25.6 %copy-start.58 = (f32[128]{0:T(128)S(1)}, f32[128]{0:T(128)}, u32[]{:S(2)}) copy-start(f32[128]{0:T(128)} %copy-done.57) | copy-start | bytes 1540
  632.4 25.6 %copy-start.61 = (f32[128]{0:T(128)S(1)}, f32[128]{0:T(128)}, u32[]{:S(2)}) copy-start(f32[128]{0:T(128)} %get-tuple-element.74) | copy-start | bytes 1540
  653.5 30.9 %copy-start.31 = (f32[8,1,256]{2,1,0:T(1,128)S(1)}, f32[8,1,256]{2,1,0:T(1,128)}, u32[]{:S(2)}) copy-start(f32[8,1,256]{2,1,0:T(1,128)} %copy-done.30) | copy-start | bytes 24580
  653.5 30.9 %copy-start.33 = (bf16[2048,4]{0,1:T(4,128)(2,1)S(1)}, bf16[2048,4]{0,1:T(4,128)(2,1)}, u32[]{:S(2)}) copy-start(bf16[2048,4]{0,1:T(4,128)(2,1)} %copy-done.32) | copy-start | bytes 49156
  653.5 30.9 %copy-start.47 = (f32[128]{0:T(128)S(1)}, f32[128]{0:T(128)}, u32[]{:S(2)}) copy-start(f32[128]{0:T(128)} %copy-done.46) | copy-start | bytes 1540
  653.5 34.0 %copy-start.42 = (f32[128]{0:T(128)S(1)}, f32[128]{0:T(128)}, u32[]{:S(2)}) copy-start(f32[128]{0:T(128)} %get-tuple-element.76) | copy-start | bytes 1540
  653.5 29.2 %all-to-all-start.3 = ((bf16[4,64,2048]{2,1,0:T(8,128)(2,1)}), bf16[4,64,2048]{2,1,0:T(8,128)(2,1)}, u32[]{:S(2)}, u32[]{:S(2)}) async-start(bf16[4,64,2048]{2,1,0:T(8,128)(2,1)} %bitcast.130), calls=%async_computation.4 | async-start | bytes 2097152 | tf_op jit(solution)/shard_map/all_to_all | solution.py:231
  657.9 75.1 %all-gather.19.cloned.1.call-start = ((), (), s32[]{:S(2)}) async-start(), calls=%async_computation.17 | async-start | bytes 2621440 | tf_op jit(solution)/shard_map/all_gather | solution.py:259
  682.8 4.7 copy-start.3
  682.8 4.7 copy-start.6
  682.8 6.3 copy-start.37
  682.8 6.3 copy-start.39
  688.8 121.4 %reduce-scatter.14.cloned.1.call-start = ((), (), s32[]{:S(2)}) async-start(), calls=%async_computation.18 | async-start | bytes 2621440 | tf_op jit(solution)/shard_map/reduce_scatter | solution.py:285
  733.0 3.7 copy-start.1
  759.4 50.8 %copy-start.35 = (f32[8,1,256]{2,1,0:T(1,128)S(1)}, f32[8,1,256]{2,1,0:T(1,128)}, u32[]{:S(2)}) copy-start(f32[8,1,256]{2,1,0:T(1,128)} %copy-done.34) | copy-start | bytes 24580
  759.4 50.8 %copy-start.49 = (f32[128]{0:T(128)S(1)}, f32[128]{0:T(128)}, u32[]{:S(2)}) copy-start(f32[128]{0:T(128)} %copy-done.48) | copy-start | bytes 1540
  767.5 172.0 %reduce-scatter.22.cloned.1.call-start = ((), (), s32[]{:S(2)}) async-start(), calls=%async_computation.22 | async-start | bytes 1179648
  830.1 130.8 %reduce-scatter.16.cloned.1.call-start = ((), (), s32[]{:S(2)}) async-start(), calls=%async_computation.19 | async-start | bytes 14155776 | tf_op jit(solution)/shard_map/reduce_scatter | solution.py:301
  840.5 175.7 %reduce-scatter.18.cloned.1.call-start = ((), (), s32[]{:S(2)}) async-start(), calls=%async_computation.20 | async-start | bytes 4718592 | tf_op jit(solution)/shard_map/reduce_scatter | solution.py:302
  845.6 439.4 %reduce-scatter.20.cloned.1.call-start = ((), (), s32[]{:S(2)}) async-start(), calls=%async_computation.21 | async-start | bytes 51904512 | tf_op jit(solution)/shard_map/reduce_scatter | solution.py:219
  864.9 925.5 %reduce-scatter.24.cloned.1.call-start = ((), (), s32[]{:S(2)}) async-start(), calls=%async_computation.23 | async-start | bytes 103809024
  909.2 26.7 %copy-start.4 = (bf16[128,2048]{1,0:T(8,128)(2,1)S(1)}, bf16[128,2048]{1,0:T(8,128)(2,1)}, u32[]{:S(2)}) copy-start(bf16[128,2048]{1,0:T(8,128)(2,1)} %reduce-scatter.12.cloned.1.call-done) | copy-start | bytes 1572868
  909.2 26.7 %copy-start.7 = (bf16[128,2048]{1,0:T(8,128)(2,1)S(1)}, bf16[128,2048]{1,0:T(8,128)(2,1)}, u32[]{:S(2)}) copy-start(bf16[128,2048]{1,0:T(8,128)(2,1)} %param.23) | copy-start | bytes 1572868
  909.2 26.7 %copy-start.9 = (f32[128,2048]{1,0:T(8,128)S(1)}, f32[128,2048]{1,0:T(8,128)}, u32[]{:S(2)}) copy-start(f32[128,2048]{1,0:T(8,128)} %copy-done.8) | copy-start | bytes 3145732
  909.2 26.7 %copy-start.24 = (bf16[128,2048]{1,0:T(8,128)(2,1)S(1)}, bf16[128,2048]{1,0:T(8,128)(2,1)}, u32[]{:S(2)}) copy-start(bf16[128,2048]{1,0:T(8,128)(2,1)} %reduce-scatter.14.cloned.1.call-done) | copy-start | bytes 1572868
  909.2 26.7 %copy-start.52 = (f32[128]{0:T(128)S(1)}, f32[128]{0:T(128)}, u32[]{:S(2)}) copy-start(f32[128]{0:T(128)} %copy-done.51) | copy-start | bytes 1540
  909.3 26.7 %copy-start.54 = (f32[128]{0:T(128)S(1)}, f32[128]{0:T(128)}, u32[]{:S(2)}) copy-start(f32[128]{0:T(128)} %copy-done.53) | copy-start | bytes 1540
  (17 other events, 25.4 us)
Sparse Core Ops, SparseCore 0:
  21.7 46.2 all-gather.8
  70.4 45.3 all-gather.10
  117.7 28.1 all-gather.12
  150.2 43.8 reduce-scatter.11
  196.1 214.0 all-gather.14
  412.0 116.4 all-gather.16
  688.9 44.0 all-gather.18
  767.6 42.5 reduce-scatter.13
  830.2 34.3 reduce-scatter.21
  868.0 92.8 reduce-scatter.15
  964.8 51.3 reduce-scatter.17
  1020.6 264.3 reduce-scatter.19
  1289.2 501.1 reduce-scatter.23
where the time goes:
time: 1810 us; the launch traced here: 1800 us
  waiting for transfers between devices  1370 us (76%)
  matrix products  205 us (11%)
  blocking collectives  126 us (7%)
  local copies, waits for them, and re-layouts  41.6 us (2%)
  other arithmetic  33.2 us (2%)
    unnamed x15, waiting for transfers between devices  507 us
    reduce_scatter x1, waiting for transfers between devices, on_device(): lax.psum_scatter(contract_first(columns, d_out_rows), 'dp', scatter_dimen...  269 us
    all_gather x1, waiting for transfers between devices, fetch_expert(): lax.all_gather(w_gate_up, 'dp', axis=1, tiled=True)  184 us
    all_gather x1, waiting for transfers between devices, fetch_expert(): lax.all_gather(w_down, 'dp', axis=1, tiled=True)  87.4 us
    dot_general x6, matrix products, contract_first(): lax.dot_general(left, right, (((0,), (0,)), ((), ())), preferred_element_...  73.5 us
    reduce_scatter x1, waiting for transfers between devices, on_device(): lax.psum_scatter(out_part, 'dp', scatter_dimension=1, tiled=True)  52.3 us
    dot_general x3, matrix products, contract_last(): lax.dot_general(left, right, (((1,), (1,)), ((), ())), preferred_element_...  49.9 us
    all_gather x1, waiting for transfers between devices, on_device(): lax.all_gather(w_qkv, 'dp', axis=1, tiled=True)  47.9 us
  transfers between devices with their start and end apart: 15, of which 14 were waited for; matrix products, arithmetic and copies ran while one was open for 9% of the time, Pallas kernels for 0%

commit v1 on v0

v1 whole, which is shorter than its diff:
```python
import jax
import jax.numpy as jnp
from jax import lax
from jax.sharding import PartitionSpec as P

HEAD_DIM = 128
FF = 5632


NORM_EPSILON = 1e-05
NEGATIVE = -1e30
THETA = 10000.0
HIGH = lax.Precision.HIGHEST


def rotary_tables(length_total, head_size):
    position = jnp.arange(length_total, dtype=jnp.float32)
    frequency = THETA ** (-(jnp.arange(head_size // 2, dtype=jnp.float32) * 2.0 / head_size))
    angles = position[:, None] * frequency[None, :]
    return (jnp.cos(angles)[:, None, :], jnp.sin(angles)[:, None, :])


def rotate(values, cosine, sine):
    half_size = values.shape[-1] // 2
    first = values[..., :half_size]
    second = values[..., half_size:]
    return jnp.concatenate(
        [first * cosine - second * sine, second * cosine + first * sine], axis=-1
    )


def rotate_back(grad_rows, cosine, sine):
    half_size = grad_rows.shape[-1] // 2
    first = grad_rows[..., :half_size]
    second = grad_rows[..., half_size:]
    return jnp.concatenate(
        [first * cosine + second * sine, second * cosine - first * sine], axis=-1
    )


def slot_table(routes, order, valid, capacity):
    row_count = routes.shape[0]
    top_count = routes.shape[1]
    pair_rank = order[:, None] + row_count * jnp.arange(top_count, dtype=jnp.int32)[None, :]
    flat_rank = pair_rank.reshape(-1)
    flat_expert = routes.reshape(-1)
    flat_valid = jnp.broadcast_to(valid[:, None], routes.shape).reshape(-1)
    earlier = (
        (flat_rank[None, :] < flat_rank[:, None])
        & (flat_expert[None, :] == flat_expert[:, None])
        & flat_valid[None, :]
    )
    slot_index = jnp.sum(earlier.astype(jnp.int32), axis=1).reshape(row_count, top_count)
    kept_pair = valid[:, None] & (slot_index < capacity)
    target = routes * capacity + jnp.minimum(slot_index, capacity - 1)
    return (target, kept_pair)


def masked_scores(query, key_rows, allowed):
    scale = query.shape[-1] ** (-0.5)
    raw = jnp.einsum("qhd,khd->hqk", query, key_rows, preferred_element_type=jnp.float32) * scale
    return jnp.where(allowed[None], raw, NEGATIVE)


def contract_first(left, right):
    return lax.dot_general(
        left, right, (((0,), (0,)), ((), ())), preferred_element_type=jnp.float32
    )


def contract_last(left, right):
    return lax.dot_general(
        left, right, (((1,), (1,)), ((), ())), preferred_element_type=jnp.float32
    )


def normalize(rows):
    inverse = lax.rsqrt(jnp.mean(rows * rows, axis=-1, keepdims=True) + NORM_EPSILON)
    return rows * inverse, inverse


def exchange_experts(blocks):
    return lax.all_to_all(blocks, "expert", split_axis=0, concat_axis=0, tiled=True)


def by_hidden(w_gate_up):
    parts = lax.axis_size("dp")
    rows = w_gate_up.shape[1]
    ff_part = w_gate_up.shape[2] // 2 // parts
    pieces = w_gate_up[0].reshape(rows, 2, parts, ff_part).transpose(2, 0, 1, 3)
    pieces = pieces.reshape(parts, rows, 2 * ff_part)
    got = lax.all_to_all(pieces, "dp", split_axis=0, concat_axis=0, tiled=True)
    return got.reshape(parts * rows, 2 * ff_part)


def by_rows(grad):
    parts = lax.axis_size("dp")
    rows = grad.shape[0] // parts
    ff_part = grad.shape[1] // 2
    pieces = grad.astype(jnp.bfloat16).reshape(parts, rows, 2 * ff_part)
    got = lax.all_to_all(pieces, "dp", split_axis=0, concat_axis=0, tiled=True)
    got = got.reshape(parts, rows, 2, ff_part).transpose(1, 2, 0, 3)
    return got.reshape(1, rows, 2 * parts * ff_part).astype(jnp.float32)


def expert_step(gate_up_w, down_w, rows, d_rows_out):
    ff = down_w.shape[0]
    gate_up = jnp.dot(rows, gate_up_w, preferred_element_type=jnp.float32)
    gate = gate_up[:, :ff]
    upward = gate_up[:, ff:]
    sigmoid = jax.nn.sigmoid(gate)
    activated = (gate * sigmoid * upward).astype(jnp.bfloat16)
    out = jnp.dot(activated, down_w, preferred_element_type=jnp.float32).astype(jnp.bfloat16)
    d_activated = contract_last(d_rows_out, down_w)
    grad_down = contract_first(activated, d_rows_out)
    d_gate = d_activated * upward * sigmoid * (1.0 + gate * (1.0 - sigmoid))
    d_up = d_activated * gate * sigmoid
    d_gate_up = jnp.concatenate([d_gate, d_up], axis=1).astype(jnp.bfloat16)
    d_rows = contract_last(d_gate_up, gate_up_w).astype(jnp.bfloat16)
    grad_gate_up = contract_first(rows, d_gate_up)
    return out, d_rows, grad_gate_up, grad_down


def experts_split_hidden(w_gate_up, w_down, rows, d_rows_out):
    gate_up_w = by_hidden(w_gate_up)
    all_rows = lax.all_gather(rows, "dp", axis=0, tiled=True)
    all_d_out = lax.all_gather(d_rows_out, "dp", axis=0, tiled=True)
    out, d_rows, grad_gate_up, grad_down = expert_step(
        gate_up_w, w_down[0], all_rows, all_d_out
    )
    out = lax.psum_scatter(out, "dp", scatter_dimension=0, tiled=True)
    d_rows = lax.psum_scatter(d_rows, "dp", scatter_dimension=0, tiled=True)
    return out, d_rows, by_rows(grad_gate_up), grad_down[None]


def experts_gather_weights(w_gate_up, w_down, rows, d_rows_out):
    gate_up_w = lax.all_gather(w_gate_up, "dp", axis=1, tiled=True)[0]
    down_w = lax.all_gather(w_down, "dp", axis=1, tiled=True)[0]
    out, d_rows, grad_gate_up, grad_down = expert_step(gate_up_w, down_w, rows, d_rows_out)
    grad_gate_up = lax.psum_scatter(
        grad_gate_up.astype(jnp.bfloat16), "dp", scatter_dimension=0, tiled=True
    )
    grad_down = lax.psum_scatter(
        grad_down.astype(jnp.bfloat16), "dp", scatter_dimension=0, tiled=True
    )
    return (
        out,
        d_rows,
        grad_gate_up.astype(jnp.float32)[None],
        grad_down.astype(jnp.float32)[None],
    )


def on_device(
    tokens,
    w_qkv,
    w_out,
    attention_norm_gain,
    gain_ffn,
    w_router,
    w_gate_up,
    w_down,
    lengths,
    routes,
    order,
    cotangent,
):
    group_size = lax.axis_size("expert")
    dp_size = lax.axis_size("dp")
    tok_dev = tokens.shape[0]
    seq_len = tok_dev * group_size
    width = tokens.shape[1]
    top_count = routes.shape[1]
    capacity = tok_dev * top_count // group_size
    slots = group_size * capacity
    head_size = HEAD_DIM
    local_width = w_qkv.shape[2]
    heads_local = local_width // head_size
    tokens_all = lax.all_gather(tokens, "expert", axis=0, tiled=True)
    small = jnp.concatenate(
        [attention_norm_gain[:, None], gain_ffn[:, None], w_router], axis=1
    )
    small_full = lax.all_gather(small, "dp", axis=0, tiled=True)
    qkv_full = lax.all_gather(w_qkv, "dp", axis=1, tiled=True)
    out_full = lax.all_gather(w_out, "dp", axis=1, tiled=True)
    first_norm_gain = small_full[:, 0].astype(jnp.float32)
    gain_two = small_full[:, 1].astype(jnp.float32)
    router_full = small_full[:, 2:]

    own_start = lax.axis_index("expert") * tok_dev
    own_position = own_start + jnp.arange(tok_dev, dtype=jnp.int32)
    live_own = own_position < lengths[0]
    live_rows = live_own.astype(jnp.float32)[:, None]
    target, kept_pair = slot_table(routes, order, live_own, capacity)
    slot_ids = jnp.arange(slots, dtype=jnp.int32)
    pair_hits = (slot_ids[:, None, None] == target[None]) & kept_pair[None]
    select = jnp.sum(pair_hits.astype(jnp.float32), axis=2).astype(jnp.bfloat16)

    inputs_float = tokens.astype(jnp.float32)
    input_normalized_hat, first_inverse_rms = normalize(inputs_float)
    hat_all, _ = normalize(tokens_all.astype(jnp.float32))
    whole = (hat_all * first_norm_gain).astype(jnp.bfloat16)
    cosine, sine = rotary_tables(seq_len, head_size)
    projected = jnp.einsum("td,cde->cte", whole, qkv_full, preferred_element_type=jnp.float32)
    query = rotate(projected[0].reshape(seq_len, heads_local, head_size), cosine, sine).astype(
        jnp.bfloat16
    )
    key_rows = rotate(projected[1].reshape(seq_len, heads_local, head_size), cosine, sine).astype(
        jnp.bfloat16
    )
    value = projected[2].astype(jnp.bfloat16).reshape(seq_len, heads_local, head_size)
    position = jnp.arange(seq_len, dtype=jnp.int32)
    live_all = position < lengths[0]
    allowed = (position[None, :] <= position[:, None]) & live_all[None, :]
    scores = masked_scores(query, key_rows, allowed)
    top_score = jnp.max(scores, axis=-1, keepdims=True)
    exponent = jnp.exp(scores - top_score)
    row_total = jnp.sum(exponent, axis=-1, keepdims=True)
    probs = exponent / row_total
    log_total = top_score + jnp.log(row_total)
    probs_low = probs.astype(jnp.bfloat16)
    attended = jnp.einsum("hqk,khd->qhd", probs_low, value, preferred_element_type=jnp.float32)
    attended = attended.reshape(seq_len, local_width).astype(jnp.bfloat16)
    attn_part = jnp.dot(attended, out_full, preferred_element_type=jnp.float32)
    attn_own = lax.psum_scatter(
        attn_part.astype(jnp.bfloat16), "expert", scatter_dimension=0, tiled=True
    ).astype(jnp.float32)
    resid = inputs_float + attn_own
    hhat, inverse_two = normalize(resid)
    hidden_in = (hhat * gain_two).astype(jnp.bfloat16)
    sent = jnp.dot(select, hidden_in, preferred_element_type=jnp.float32).astype(jnp.bfloat16)
    dispatched = exchange_experts(sent.reshape(group_size, capacity, width)).reshape(slots, width)

    logits = jnp.dot(hidden_in, router_full, preferred_element_type=jnp.float32)
    chosen = jnp.take_along_axis(logits, routes, axis=1)
    gates = jax.nn.softmax(chosen, axis=1)
    d_out = live_rows * cotangent.astype(jnp.float32)
    d_back = jnp.zeros((slots, width), jnp.float32)
    for index in range(top_count):
        weighted = (gates[:, index : index + 1] * d_out).astype(jnp.bfloat16)
        d_back = d_back + jnp.dot(
            pair_hits[:, :, index].astype(jnp.bfloat16),
            weighted,
            preferred_element_type=jnp.float32,
        )
    d_back = d_back.astype(jnp.bfloat16)
    d_out_rows = exchange_experts(d_back.reshape(group_size, capacity, width)).reshape(
        slots, width
    )

    split_cost = 4 * dp_size * slots * width + 2 * 2 * FF * width // dp_size
    gather_cost = 2 * 3 * FF * width
    experts = experts_split_hidden if split_cost < gather_cost else experts_gather_weights
    expert_out, d_rows, grad_gate_up, grad_down = experts(
        w_gate_up, w_down, dispatched, d_out_rows
    )
    d_sent = exchange_experts(d_rows.reshape(group_size, capacity, width)).reshape(slots, width)
    returned = exchange_experts(expert_out.reshape(group_size, capacity, width)).reshape(
        slots, width
    )

    moe = jnp.zeros_like(resid)
    d_gates_list = []
    for index in range(top_count):
        one_hot = pair_hits[:, :, index].astype(jnp.bfloat16)
        picked = contract_first(one_hot, returned)
        d_gates_list.append(jnp.sum(d_out * picked, axis=-1))
        moe = moe + gates[:, index : index + 1] * picked
    output = (live_rows * (resid + moe)).astype(jnp.bfloat16)
    d_gates = jnp.stack(d_gates_list, axis=1)
    d_hidden = contract_first(select, d_sent)
    d_chosen = gates * (d_gates - jnp.sum(gates * d_gates, axis=1, keepdims=True))
    expert_ids = jnp.arange(group_size, dtype=jnp.int32)
    route_hits = (routes[:, :, None] == expert_ids[None, None, :]).astype(jnp.float32)
    d_logits = jnp.sum(route_hits * d_chosen[:, :, None], axis=1)
    router_f = router_full.astype(jnp.float32)
    d_hidden = d_hidden + jnp.dot(
        d_logits, router_f.T, precision=HIGH, preferred_element_type=jnp.float32
    )
    router_part = jnp.dot(
        hidden_in.astype(jnp.float32).T,
        d_logits,
        precision=HIGH,
        preferred_element_type=jnp.float32,
    )
    gain_two_part = jnp.sum(d_hidden * hhat, axis=0)
    scaled_two = d_hidden * gain_two
    d_resid = d_out + inverse_two * (
        scaled_two - hhat * jnp.mean(scaled_two * hhat, axis=-1, keepdims=True)
    )
    d_attn = d_resid.astype(jnp.bfloat16)
    whole_grad = lax.all_gather(d_attn, "expert", axis=0, tiled=True)
    d_attended = contract_last(whole_grad, out_full).astype(jnp.bfloat16)
    out_part = contract_first(attended, whole_grad)
    grad_out = lax.psum_scatter(
        out_part.astype(jnp.bfloat16), "dp", scatter_dimension=1, tiled=True
    ).astype(jnp.float32)
    d_heads = d_attended.reshape(seq_len, heads_local, head_size)
    probs = jnp.exp(masked_scores(query, key_rows, allowed) - log_total)
    probs_low = probs.astype(jnp.bfloat16)
    d_value = jnp.einsum(
        "hqk,qhd->khd", probs_low, d_heads, preferred_element_type=jnp.float32
    ).astype(jnp.bfloat16)
    d_probs = jnp.einsum("qhd,khd->hqk", d_heads, value, preferred_element_type=jnp.float32)
    row_delta = jnp.sum(probs * d_probs, axis=-1, keepdims=True)
    d_scores = (probs * (d_probs - row_delta)).astype(jnp.bfloat16)
    scale = head_size ** (-0.5)
    d_query = (
        jnp.einsum("hqk,khd->qhd", d_scores, key_rows, preferred_element_type=jnp.float32) * scale
    )
    d_key = jnp.einsum("hqk,qhd->khd", d_scores, query, preferred_element_type=jnp.float32) * scale
    d_query_pre = (
        rotate_back(d_query, cosine, sine).reshape(seq_len, local_width).astype(jnp.bfloat16)
    )
    d_key_pre = rotate_back(d_key, cosine, sine).reshape(seq_len, local_width).astype(jnp.bfloat16)
    d_projected = jnp.stack([d_query_pre, d_key_pre, d_value.reshape(seq_len, local_width)])
    d_normed_part = jnp.einsum(
        "cte,cde->td", d_projected, qkv_full, preferred_element_type=jnp.float32
    )
    grad_normalized = lax.psum_scatter(
        d_normed_part.astype(jnp.bfloat16), "expert", scatter_dimension=0, tiled=True
    ).astype(jnp.float32)
    qkv_part = jnp.einsum("td,cte->cde", whole, d_projected, preferred_element_type=jnp.float32)
    grad_qkv = lax.psum_scatter(
        qkv_part.astype(jnp.bfloat16), "dp", scatter_dimension=1, tiled=True
    ).astype(jnp.float32)
    first_gain_part = jnp.sum(d_normed_part * hat_all, axis=0)
    first_scaled_input = grad_normalized * first_norm_gain
    grad_tokens = d_resid + first_inverse_rms * (
        first_scaled_input
        - input_normalized_hat
        * jnp.mean(first_scaled_input * input_normalized_hat, axis=-1, keepdims=True)
    )
    small_part = jnp.concatenate(
        [first_gain_part[None], gain_two_part[None], router_part.T], axis=0
    )
    small_sum = lax.psum(small_part, ("dp", "expert"))
    own_rows = width // dp_size
    small_own = lax.dynamic_slice_in_dim(
        small_sum, lax.axis_index("dp") * own_rows, own_rows, axis=1
    )
    return (
        output,
        grad_tokens.astype(jnp.bfloat16),
        grad_qkv,
        grad_out,
        small_own[0],
        small_own[1],
        small_own[2:].T,
        grad_gate_up,
        grad_down,
    )


def solution(mesh):
    placed = (
        P(("dp", "expert"), None),
        P(None, "dp", "expert"),
        P("expert", "dp"),
        P("dp"),
        P("dp"),
        P("dp", None),
        P("expert", "dp", None),
        P("expert", "dp", None),
        P("dp"),
        P(("dp", "expert"), None),
        P(("dp", "expert")),
        P(("dp", "expert"), None),
    )
    return jax.shard_map(
        on_device,
        mesh=mesh,
        in_specs=placed,
        out_specs=(
            P(("dp", "expert"), None),
            P(("dp", "expert"), None),
            P(None, "dp", "expert"),
            P("expert", "dp"),
            P("dp"),
            P("dp"),
            P("dp", None),
            P("expert", "dp", None),
            P("expert", "dp", None),
        ),
        check_vma=False,
    )
```

time: 1810 us -> 991 us (0.55)
  waiting for transfers between devices: 1370 us -> 466 us
  blocking collectives: 126 us -> 199 us
  matrix products: 205 us -> 142 us
  local copies, waits for them, and re-layouts: 41.6 us -> 88.3 us
    unnamed x15 -> x12, waiting for transfers between devices: 507 us -> 1.53 us
    all_gather x5, waiting for transfers between devices: 367 us -> 132 us  [the longest x1 52.6 us: experts_split_hidden(): all_d_out = lax.all_gather(d_rows_out, 'dp', axis=0, tiled=True)]
    reduce_scatter x3 -> x4, waiting for transfers between devices: 341 us -> 142 us  [the longest x1 71.3 us: experts_split_hidden(): d_rows = lax.psum_scatter(d_rows, 'dp', scatter_dimension=0, tiled=True)]
    all_to_all x2 -> x3, blocking collectives: 57 us -> 152 us  [the longest x1 94.4 us: by_hidden(): got = lax.all_to_all(pieces, 'dp', split_axis=0, concat_axis=0, tiled=True)]
    all_to_all x2 -> x3, waiting for transfers between devices: 33.9 us -> 105 us  [the longest x1 70.9 us: by_rows(): got = lax.all_to_all(pieces, 'dp', split_axis=0, concat_axis=0, tiled=True)]
    reduce_scatter x1, waiting for transfers between devices: 41.3 us -> 0.01 us  [on_device(): lax.psum_scatter(d_normed_part.astype(jnp.bfloat16), 'expert', scatter_di...]
    dot_general x6, matrix products: 73.5 us -> 38.9 us  [contract_first(): lax.dot_general(left, right, (((0,), (0,)), ((), ())), preferred_element_...]
    unnamed x1 -> x0, blocking collectives: 23.6 us -> none
  transfers between devices with their start and end apart: 15 -> 15, of which waited for: 14 -> 11; matrix products, arithmetic and copies ran while one was open for 9% -> 18% of each run, Pallas kernels for 0% -> 0%
where the time goes in v1:
time: 991 us; the launch traced here: 980 us
  waiting for transfers between devices  466 us (47%)
  blocking collectives  199 us (20%)
  matrix products  142 us (14%)
  local copies, waits for them, and re-layouts  88.3 us (9%)
  other arithmetic  43.5 us (4%)
  starting transfers between devices  24.9 us (3%)
  between operations  16 us (2%)
    all_to_all x1, blocking collectives, by_hidden(): got = lax.all_to_all(pieces, 'dp', split_axis=0, concat_axis=0, tiled=True)  94.4 us
    reduce_scatter x1, waiting for transfers between devices, experts_split_hidden(): d_rows = lax.psum_scatter(d_rows, 'dp', scatter_dimension=0, tiled=True)  71.3 us
    all_to_all x1, waiting for transfers between devices, by_rows(): got = lax.all_to_all(pieces, 'dp', split_axis=0, concat_axis=0, tiled=True)  70.9 us
    reduce_scatter x1, waiting for transfers between devices, experts_split_hidden(): out = lax.psum_scatter(out, 'dp', scatter_dimension=0, tiled=True)  70.9 us
    all_to_all x2, blocking collectives, exchange_experts(): lax.all_to_all(blocks, 'expert', split_axis=0, concat_axis=0, tiled=True)  57.3 us
    all_gather x1, waiting for transfers between devices, experts_split_hidden(): all_d_out = lax.all_gather(d_rows_out, 'dp', axis=0, tiled=True)  52.6 us
    all_gather x1, waiting for transfers between devices, on_device(): qkv_full = lax.all_gather(w_qkv, 'dp', axis=1, tiled=True)  45.8 us
    all_gather x1, waiting for transfers between devices, on_device(): whole_grad = lax.all_gather(d_attn, 'expert', axis=0, tiled=True)  44.1 us
  transfers between devices with their start and end apart: 15, of which 11 were waited for; matrix products, arithmetic and copies ran while one was open for 18% of the time, Pallas kernels for 0%

profile of v1, /device:TPU:0, one launch (start us, length us, event | category | flops | bytes accessed | tf_op | source)
XLA Modules:
  0.0 980.1 jit_solution(3513390332413267402)
XLA Ops:
  8.0 2.4 copy.213
  13.8 10.5 %all_gather.22 = bf16[2048,6]{0,1:T(8,128)(2,1)S(1)} all-gather(bf16[256,6]{0,1:T(8,128)(2,1)S(1)} %pad_maximum_fusion.15), channel_id=1, replica_groups=mesh['dp'=8,'expert'=4] {'dp'}, dimensions={0}, use_global_device_ids=true | all-gather | bytes 27648 | tf_op jit(solution)/shard_map/all_gather | solution.py:183
  25.2 1.7 fusion.41
  26.9 31.3 %all-gather.7.cloned.1.call-done = bf16[512,2048]{1,0:T(8,128)(2,1)} async-done(((bf16[128,2048]{1,0:T(8,128)(2,1)}), bf16[512,2048]{1,0:T(8,128)(2,1)}) %all-gather.7.cloned.1.call-update) | async-done | bytes 2097168 | tf_op jit(solution)/shard_map/all_gather | solution.py:179
  58.3 2.1 fusion.4
  60.4 45.8 %all-gather.9.cloned.1.call-done = bf16[3,2048,512]{1,2,0:T(8,128)(2,1)} async-done(((bf16[3,256,512]{1,2,0:T(8,128)(2,1)}), bf16[3,2048,512]{1,2,0:T(8,128)(2,1)}) %all-gather.9.cloned.1.call-update) | async-done | bytes 6291472 | tf_op jit(solution)/shard_map/all_gather | solution.py:184
  106.1 6.4 convolution_bitcast_fusion.1
  115.4 2.4 copy.260
  117.8 2.2 fusion.66
  120.1 2.4 copy.262
  122.4 1.3 copy.259
  123.7 2.4 copy.261
  126.1 3.1 subtract_convert_fusion.3
  129.2 1.4 fusion.68
  131.2 1.4 copy-done.2
  132.6 1.7 fusion.21
  134.4 1.9 all-gather.11.cloned.1.call-done
  136.2 4.4 convolution_convert_fusion.4
  142.9 41.9 %reduce-scatter.7.cloned.1.call-done = bf16[128,2048]{1,0:T(8,128)(2,1)} async-done(((bf16[512,2048]{1,0:T(8,128)(2,1)}), bf16[128,2048]{1,0:T(8,128)(2,1)}) %reduce-scatter.7.cloned.1.call-update) | async-done | bytes 524304 | tf_op jit(solution)/shard_map/reduce_scatter | solution.py:225
  188.6 29.0 %all_to_all.30 = bf16[4,64,2048]{2,1,0:T(8,128)(2,1)} all-to-all(bf16[4,64,2048]{2,1,0:T(8,128)(2,1)S(1)} %bitcast.127), channel_id=1, replica_groups=mesh['dp'=8,'expert'=4] {'expert'}, dimensions={0} | all-to-all | bytes 2097152 | tf_op jit(solution)/shard_map/all_to_all | solution.py:83
  217.9 8.4 copy.224
  226.3 3.0 copy.225
  229.3 94.4 %all_to_all.31 = bf16[8,256,1408]{1,2,0:T(8,128)(2,1)} all-to-all(bf16[8,256,1408]{1,2,0:T(8,128)(2,1)S(1)} %bitcast.119), channel_id=1, replica_groups=mesh['dp'=8,'expert'=4] {'dp'}, dimensions={0} | all-to-all | bytes 11534336 | tf_op jit(solution)/shard_map/all_to_all | solution.py:92
  323.8 8.2 copy.226
  332.0 18.8 %fusion.69 = f32[2048,1408]{0,1:T(8,128)} fusion(bf16[2048,2048]{1,0:T(8,128)(2,1)} %all-gather.13.cloned.1.call-done, bf16[2048,1408]{1,0:T(8,128)(2,1)} %bitcast.121), kind=kOutput, calls=%fused_computation.161 | convolution fusion | flops 11811160064 | bytes 25690112 | tf_op jit(solution)/shard_map/dot_general | solution.py:108
  350.8 5.2 multiply_convert_fusion.2
  356.1 1.7 copy-done.22
  357.8 9.1 convolution_convert_fusion.1
  366.9 70.9 %reduce-scatter.9.cloned.1.call-done = bf16[256,2048]{1,0:T(8,128)(2,1)} async-done(((bf16[2048,2048]{1,0:T(8,128)(2,1)}), bf16[256,2048]{1,0:T(8,128)(2,1)}) %reduce-scatter.9.cloned.1.call-update) | async-done | bytes 1048592 | tf_op jit(solution)/shard_map/reduce_scatter | solution.py:131
  437.7 4.6 all-to-all-start.2
  442.3 9.3 all-gather.15.cloned.1.call-start
  454.0 2.4 gather_fusion
  457.1 1.5 copy.220
  459.8 8.3 all-to-all-done.2
  468.2 1.6 fusion.44
  470.8 2.8 multiply_reduce_fusion.4
  475.8 28.4 %all_to_all.32 = bf16[4,64,2048]{2,1,0:T(8,128)(2,1)} all-to-all(bf16[4,64,2048]{2,1,0:T(8,128)(2,1)S(1)} %bitcast.130), channel_id=1, replica_groups=mesh['dp'=8,'expert'=4] {'expert'}, dimensions={0} | all-to-all | bytes 2097152 | tf_op jit(solution)/shard_map/all_to_all | solution.py:83
  504.3 52.6 %all-gather.15.cloned.1.call-done = bf16[2048,2048]{1,0:T(8,128)(2,1)} async-done(((bf16[256,2048]{1,0:T(8,128)(2,1)}), bf16[2048,2048]{1,0:T(8,128)(2,1)}) %all-gather.15.cloned.1.call-update) | async-done | bytes 8388624 | tf_op jit(solution)/shard_map/all_gather | solution.py:127
  556.9 13.1 %multiply_convert_fusion.1 = (bf16[2048,704]{0,1:T(8,128)(2,1)S(1)}, bf16[2048,704]{0,1:T(8,128)(2,1)S(1)}) fusion(f32[2048,1408]{0,1:T(8,128)} %fusion.69, bf16[2048,2048]{1,0:T(8,128)(2,1)} %all-gather.15.cloned.1.call-done, bf16[1,704,2048]{2,1,0:T(8,128)(2,1)S(1)} %copy-done), kind=kOutput, calls=%fused_computation.8 | convolution fusion | flops 5924323328 | bytes 28573696 | tf_op jit(solution)/shard_map/dot_general | solution.py:72
  570.0 1.5 copy-done.62
  572.5 17.7 %convolution_convert_fusion = bf16[2048,2048]{1,0:T(8,128)(2,1)} fusion(bf16[2048,1408]{1,0:T(8,128)(2,1)} %bitcast.122, bf16[2048,704]{0,1:T(8,128)(2,1)S(1)} %get-tuple-element.75, bf16[2048,704]{0,1:T(8,128)(2,1)S(1)} %get-tuple-element.74), kind=kOutput, calls=%fused_computation.2 | convolution fusion | flops 11826888704 | bytes 19922944 | tf_op jit(solution)/shard_map/dot_general | solution.py:72
  590.3 71.3 %reduce-scatter.11.cloned.1.call-done = bf16[256,2048]{1,0:T(8,128)(2,1)} async-done(((bf16[2048,2048]{1,0:T(8,128)(2,1)}), bf16[256,2048]{1,0:T(8,128)(2,1)}) %reduce-scatter.11.cloned.1.call-update) | async-done | bytes 1048592 | tf_op jit(solution)/shard_map/reduce_scatter | solution.py:132
  661.6 4.6 all-to-all-start.4
  666.7 25.2 %all-to-all-done.4 = bf16[4,64,2048]{2,1,0:T(8,128)(2,1)S(1)} async-done(((bf16[4,64,2048]{2,1,0:T(8,128)(2,1)}), bf16[4,64,2048]{2,1,0:T(8,128)(2,1)S(1)}, u32[]{:S(2)}, u32[]{:S(2)}) %all-to-all-start.4) | async-done | bytes 1048608 | tf_op jit(solution)/shard_map/all_to_all | solution.py:83
  694.7 44.1 %all-gather.17.cloned.1.call-done = bf16[512,2048]{1,0:T(8,128)(2,1)} async-done(((bf16[128,2048]{1,0:T(8,128)(2,1)}), bf16[512,2048]{1,0:T(8,128)(2,1)}) %all-gather.17.cloned.1.call-update) | async-done | bytes 2097168 | tf_op jit(solution)/shard_map/all_gather | solution.py:292
  738.9 4.2 convolution_convert_fusion.3
  743.1 3.7 convolution_convert_fusion.6
  748.7 3.5 multiply_reduce_fusion
  759.9 9.7 bitcast_convert_fusion
  769.9 6.9 convert_bitcast_fusion.1
  776.8 19.0 %convolution_convert_fusion.2 = bf16[2048,1408]{1,0:T(8,128)(2,1)} fusion(bf16[2048,2048]{1,0:T(8,128)(2,1)} %all-gather.13.cloned.1.call-done, bf16[2048,704]{0,1:T(8,128)(2,1)} %copy-done.63, bf16[2048,704]{0,1:T(8,128)(2,1)} %copy-done.62), kind=kOutput, calls=%fused_computation.4 | convolution fusion | flops 11825577984 | bytes 19922944 | tf_op jit(solution)/shard_map/dot_general | solution.py:66
  795.8 8.3 copy.243
  804.1 5.1 all-to-all-start.5
  809.5 11.0 %convolution_bitcast_fusion = f32[1,704,2048]{2,1,0:T(8,128)} fusion(bf16[2048,704]{0,1:T(8,128)(2,1)} %copy-done.22, bf16[2048,2048]{1,0:T(8,128)(2,1)} %all-gather.15.cloned.1.call-done), kind=kOutput, calls=%fused_computation.26 | convolution fusion | flops 5905580032 | bytes 17039360 | tf_op jit(solution)/shard_map/dot_general | solution.py:66
  820.5 70.9 %all-to-all-done.5 = bf16[8,256,1408]{1,2,0:T(8,128)(2,1)} async-done(((bf16[8,256,1408]{1,2,0:T(8,128)(2,1)}), bf16[8,256,1408]{1,2,0:T(8,128)(2,1)}, u32[]{:S(2)}, u32[]{:S(2)}) %all-to-all-start.5) | async-done | bytes 5767200 | tf_op jit(solution)/shard_map/all_to_all | solution.py:101
  891.4 8.4 convert_bitcast_fusion
  899.9 9.7 copy.244
  909.5 11.9 %copy.246 = f32[1,256,11264]{2,1,0:T(8,128)} copy(f32[1,256,11264]{1,2,0:T(8,128)} %bitcast.118) | data formatting | bytes 23068672
  921.5 2.8 fusion.3
  924.3 37.2 %psum.7 = f32[6,2048]{1,0:T(8,128)S(1)} all-reduce(f32[6,2048]{1,0:T(8,128)S(1)} %pad_maximum_fusion.14), channel_id=1, replica_groups=mesh['dp'=8,'expert'=4] {'dp','expert'}, use_global_device_ids=true, to_apply=%region_24.25 | all-reduce | flops 12288 | bytes 98304 | tf_op jit(solution)/shard_map/psum | solution.py:337
  962.8 1.8 convert_element_type.238
  964.6 1.4 fusion.26
  966.0 4.4 fusion.30
  970.4 2.6 copy.245
  (222 shorter events, 37.3 us)
Async XLA Ops:
  7.2 350.6 %copy-start = (bf16[1,704,2048]{2,1,0:T(8,128)(2,1)S(1)}, bf16[1,704,2048]{2,1,0:T(8,128)(2,1)}, u32[]{:S(2)}) copy-start(bf16[1,704,2048]{2,1,0:T(8,128)(2,1)} %param.19) | copy-start | bytes 8650756
  7.2 51.1 %all-gather.7.cloned.1.call-start = ((), (), s32[]{:S(2)}) async-start(), calls=%async_computation.12 | async-start | bytes 2621440 | tf_op jit(solution)/shard_map/all_gather | solution.py:179
  7.9 98.2 %all-gather.9.cloned.1.call-start = ((), (), s32[]{:S(2)}) async-start(), calls=%async_computation.13 | async-start | bytes 7077888 | tf_op jit(solution)/shard_map/all_gather | solution.py:184
  10.4 125.9 %all-gather.11.cloned.1.call-start = ((), (), s32[]{:S(2)}) async-start(), calls=%async_computation.14 | async-start | bytes 2359296 | tf_op jit(solution)/shard_map/all_gather | solution.py:185
  11.1 173.6 %reduce-scatter.7.cloned.1.call-start = ((), (), s32[]{:S(2)}) async-start(), calls=%async_computation.15 | async-start | bytes 2621440 | tf_op jit(solution)/shard_map/reduce_scatter | solution.py:225
  24.3 88.2 %copy-start.29 = (bf16[2048,6]{0,1:T(8,128)(2,1)}, bf16[2048,6]{0,1:T(8,128)(2,1)S(1)}, u32[]{:S(2)}) copy-start(bf16[2048,6]{0,1:T(8,128)(2,1)S(1)} %all_gather.22) | copy-start | bytes 73732
  24.4 88.2 %copy-start.35 = (f32[2048,1]{0,1:T(1,128)}, f32[2048,1]{0,1:T(1,128)S(1)}, u32[]{:S(2)}) copy-start(f32[2048,1]{0,1:T(1,128)S(1)} %get-tuple-element.99) | copy-start | bytes 24580
  24.4 161.7 %copy-start.31 = (f32[2048,1]{0,1:T(1,128)}, f32[2048,1]{0,1:T(1,128)S(1)}, u32[]{:S(2)}) copy-start(f32[2048,1]{0,1:T(1,128)S(1)} %get-tuple-element.98) | copy-start | bytes 24580
  60.4 52.2 %copy-start.44 = (f32[512]{0:T(512)}, f32[512]{0:T(512)S(1)}, u32[]{:S(2)}) copy-start(f32[512]{0:T(512)S(1)} %add_rsqrt_fusion) | copy-start | bytes 6148
  126.1 3.1 copy-start.27
  129.1 2.0 copy-start.14
  129.2 3.5 copy-start.25
  130.6 2.1 copy-start.2
  130.6 2.1 copy-start.33
  134.4 7.1 copy-start.60
  134.4 7.4 copy-start.39
  136.2 48.5 %copy-start.5 = (bf16[128,2048]{1,0:T(8,128)(2,1)S(1)}, bf16[128,2048]{1,0:T(8,128)(2,1)}, u32[]{:S(2)}) copy-start(bf16[128,2048]{1,0:T(8,128)(2,1)} %param.12) | copy-start | bytes 1572868
  140.7 191.3 %all-gather.13.cloned.1.call-start = ((), (), s32[]{:S(2)}) async-start(), calls=%async_computation.16 | async-start | bytes 9437184 | tf_op jit(solution)/shard_map/all_gather | solution.py:126
  142.6 42.2 %copy-start.48 = (pred[128,2]{0,1:T(4,128)(4,1)}, pred[128,2]{0,1:T(4,128)(4,1)S(1)}, u32[]{:S(2)}) copy-start(pred[128,2]{0,1:T(4,128)(4,1)S(1)} %copy.223) | copy-start | bytes 772
  186.1 40.2 %copy-start.46 = (f32[128]{0:T(128)}, f32[128]{0:T(128)S(1)}, u32[]{:S(2)}) copy-start(f32[128]{0:T(128)S(1)} %add_rsqrt_fusion.2) | copy-start | bytes 1540
  217.6 220.2 %reduce-scatter.9.cloned.1.call-start = ((), (), s32[]{:S(2)}) async-start(), calls=%async_computation.17 | async-start | bytes 9437184 | tf_op jit(solution)/shard_map/reduce_scatter | solution.py:131
  437.7 30.4 %all-to-all-start.2 = ((bf16[4,64,2048]{2,1,0:T(8,128)(2,1)}), bf16[4,64,2048]{2,1,0:T(8,128)(2,1)}, u32[]{:S(2)}, u32[]{:S(2)}) async-start(bf16[4,64,2048]{2,1,0:T(8,128)(2,1)} %bitcast.138), calls=%async_computation.4 | async-start | bytes 2097152 | tf_op jit(solution)/shard_map/all_to_all | solution.py:83
  442.3 114.6 %all-gather.15.cloned.1.call-start = ((), (), s32[]{:S(2)}) async-start(), calls=%async_computation.18 | async-start | bytes 9437184 | tf_op jit(solution)/shard_map/all_gather | solution.py:127
  456.4 18.4 %copy-start.40 = (f32[128]{0:T(128)S(1)}, f32[128]{0:T(128)}, u32[]{:S(2)}) copy-start(f32[128]{0:T(128)} %get-tuple-element.70) | copy-start | bytes 1540
  459.3 14.3 %copy-start.57 = (f32[128]{0:T(128)}, f32[128]{0:T(128)S(1)}, u32[]{:S(2)}) copy-start(f32[128]{0:T(128)S(1)} %get-tuple-element.72) | copy-start | bytes 1540
  468.2 5.4 copy-start.59
  468.2 6.6 copy-start.6
  474.7 29.5 %copy-start.42 = (f32[128,2]{0,1:T(2,128)}, f32[128,2]{0,1:T(2,128)S(1)}, u32[]{:S(2)}) copy-start(f32[128,2]{0,1:T(2,128)S(1)} %get-tuple-element.69) | copy-start | bytes 3076
  474.7 29.5 %copy-start.49 = (f32[128]{0:T(128)}, f32[128]{0:T(128)S(1)}, u32[]{:S(2)}) copy-start(f32[128]{0:T(128)S(1)} %get-tuple-element.100) | copy-start | bytes 1540
  474.7 29.5 %copy-start.51 = (f32[128]{0:T(128)}, f32[128]{0:T(128)S(1)}, u32[]{:S(2)}) copy-start(f32[128]{0:T(128)S(1)} %get-tuple-element.101) | copy-start | bytes 1540
  504.2 157.4 %reduce-scatter.11.cloned.1.call-start = ((), (), s32[]{:S(2)}) async-start(), calls=%async_computation.19 | async-start | bytes 9437184 | tf_op jit(solution)/shard_map/reduce_scatter | solution.py:132
  570.0 2.5 copy-start.63
  590.2 76.5 %copy-start.43 = (f32[128,2]{0,1:T(2,128)S(1)}, f32[128,2]{0,1:T(2,128)}, u32[]{:S(2)}) copy-start(f32[128,2]{0,1:T(2,128)} %copy-done.42) | copy-start | bytes 3076
  590.2 76.5 %copy-start.54 = (f32[128]{0:T(128)S(1)}, f32[128]{0:T(128)}, u32[]{:S(2)}) copy-start(f32[128]{0:T(128)} %copy-done.53) | copy-start | bytes 1540
  590.2 76.5 %copy-start.56 = (f32[128]{0:T(128)S(1)}, f32[128]{0:T(128)}, u32[]{:S(2)}) copy-start(f32[128]{0:T(128)} %copy-done.55) | copy-start | bytes 1540
  590.2 76.5 %copy-start.58 = (f32[128]{0:T(128)S(1)}, f32[128]{0:T(128)}, u32[]{:S(2)}) copy-start(f32[128]{0:T(128)} %get-tuple-element.68) | copy-start | bytes 1540
  590.2 102.1 %copy-start.8 = (bf16[128,2048]{1,0:T(8,128)(2,1)S(1)}, bf16[128,2048]{1,0:T(8,128)(2,1)}, u32[]{:S(2)}) copy-start(bf16[128,2048]{1,0:T(8,128)(2,1)} %reduce-scatter.7.cloned.1.call-done) | copy-start | bytes 1572868
  590.2 102.1 %copy-start.30 = (bf16[2048,6]{0,1:T(8,128)(2,1)S(1)}, bf16[2048,6]{0,1:T(8,128)(2,1)}, u32[]{:S(2)}) copy-start(bf16[2048,6]{0,1:T(8,128)(2,1)} %copy-done.29) | copy-start | bytes 73732
  590.2 102.1 %copy-start.32 = (f32[2048,1]{0,1:T(1,128)S(1)}, f32[2048,1]{0,1:T(1,128)}, u32[]{:S(2)}) copy-start(f32[2048,1]{0,1:T(1,128)} %copy-done.31) | copy-start | bytes 24580
  590.2 102.1 %copy-start.47 = (f32[128]{0:T(128)S(1)}, f32[128]{0:T(128)}, u32[]{:S(2)}) copy-start(f32[128]{0:T(128)} %copy-done.46) | copy-start | bytes 1540
  590.2 103.1 %copy-start.7 = (bf16[128,2048]{1,0:T(8,128)(2,1)S(1)}, bf16[128,2048]{1,0:T(8,128)(2,1)}, u32[]{:S(2)}) copy-start(bf16[128,2048]{1,0:T(8,128)(2,1)} %param.23) | copy-start | bytes 1572868
  590.2 103.1 %copy-start.41 = (f32[128]{0:T(128)S(1)}, f32[128]{0:T(128)}, u32[]{:S(2)}) copy-start(f32[128]{0:T(128)} %get-tuple-element.70) | copy-start | bytes 1540
  661.6 30.3 %all-to-all-start.4 = ((bf16[4,64,2048]{2,1,0:T(8,128)(2,1)}), bf16[4,64,2048]{2,1,0:T(8,128)(2,1)S(1)}, u32[]{:S(2)}, u32[]{:S(2)}) async-start(bf16[4,64,2048]{2,1,0:T(8,128)(2,1)} %bitcast.139), calls=%async_computation.7 | async-start | bytes 2097152 | tf_op jit(solution)/shard_map/all_to_all | solution.py:83
  666.2 72.6 %all-gather.17.cloned.1.call-start = ((), (), s32[]{:S(2)}) async-start(), calls=%async_computation.20 | async-start | bytes 2621440 | tf_op jit(solution)/shard_map/all_gather | solution.py:292
  691.9 2.8 copy-start.34
  691.9 2.8 copy-start.38
  691.9 46.9 %copy-start.61 = (bf16[4,128,512]{2,1,0:T(8,128)(2,1)S(1)}, bf16[4,128,512]{2,1,0:T(8,128)(2,1)}, u32[]{:S(2)}) copy-start(bf16[4,128,512]{2,1,0:T(8,128)(2,1)} %fusion.21) | copy-start | bytes 1572868
  693.3 49.7 %copy-start.10 = (f32[128,2048]{1,0:T(8,128)}, f32[128,2048]{1,0:T(8,128)S(1)}, u32[]{:S(2)}) copy-start(f32[128,2048]{1,0:T(8,128)S(1)} %get-tuple-element.107) | copy-start | bytes 3145732
  694.6 268.2 %reduce-scatter.17.cloned.1.call-start = ((), (), s32[]{:S(2)}) async-start(), calls=%async_computation.23 | async-start | bytes 2359296 | tf_op jit(solution)/shard_map/reduce_scatter | solution.py:295
  743.1 221.5 %reduce-scatter.13.cloned.1.call-start = ((), (), s32[]{:S(2)}) async-start(), calls=%async_computation.21 | async-start | bytes 2621440 | tf_op jit(solution)/shard_map/reduce_scatter | solution.py:320
  743.1 3.7 copy-start.3
  748.7 3.9 copy-start.4
  753.9 2.2 copy-start.23
  753.9 2.3 copy-start.24
  759.9 9.9 %copy-start.11 = (bf16[512,2048]{1,0:T(8,128)(2,1)S(1)}, bf16[512,2048]{1,0:T(8,128)(2,1)}, u32[]{:S(2)}) copy-start(bf16[512,2048]{1,0:T(8,128)(2,1)} %all-gather.7.cloned.1.call-done) | copy-start | bytes 6291460
  759.9 9.9 %copy-start.28 = (bf16[1,512,512]{2,1,0:T(8,128)(2,1)S(1)}, bf16[1,512,512]{2,1,0:T(8,128)(2,1)}, u32[]{:S(2)}) copy-start(bf16[1,512,512]{2,1,0:T(8,128)(2,1)} %copy.240) | copy-start | bytes 1572868
  759.9 9.9 %copy-start.36 = (f32[2048,1]{0,1:T(1,128)S(1)}, f32[2048,1]{0,1:T(1,128)}, u32[]{:S(2)}) copy-start(f32[2048,1]{0,1:T(1,128)} %copy-done.35) | copy-start | bytes 24580
  759.9 10.0 %copy-start.45 = (f32[512]{0:T(512)S(1)}, f32[512]{0:T(512)}, u32[]{:S(2)}) copy-start(f32[512]{0:T(512)} %copy-done.44) | copy-start | bytes 6148
  769.6 200.8 %reduce-scatter.15.cloned.1.call-start = ((), (), s32[]{:S(2)}) async-start(), calls=%async_computation.22 | async-start | bytes 7077888 | tf_op jit(solution)/shard_map/reduce_scatter | solution.py:324
  804.1 5.1 copy-start.13
  804.1 87.3 %all-to-all-start.5 = ((bf16[8,256,1408]{1,2,0:T(8,128)(2,1)}), bf16[8,256,1408]{1,2,0:T(8,128)(2,1)}, u32[]{:S(2)}, u32[]{:S(2)}) async-start(bf16[8,256,1408]{1,2,0:T(8,128)(2,1)} %copy.243), calls=%async_computation.11 | async-start | bytes 11534336 | tf_op jit(solution)/shard_map/all_to_all | solution.py:101
  921.5 44.6 %copy-start.50 = (f32[128]{0:T(128)S(1)}, f32[128]{0:T(128)}, u32[]{:S(2)}) copy-start(f32[128]{0:T(128)} %copy-done.49) | copy-start | bytes 1540
  921.5 44.6 %copy-start.52 = (f32[128]{0:T(128)S(1)}, f32[128]{0:T(128)}, u32[]{:S(2)}) copy-start(f32[128]{0:T(128)} %copy-done.51) | copy-start | bytes 1540
  966.0 7.0 copy-start.1
  (15 other events, 22.6 us)
Sparse Core Ops, SparseCore 0:
  9.6 48.6 all-gather.6
  60.7 45.3 all-gather.8
  108.0 28.1 all-gather.10
  140.8 43.8 reduce-scatter.6
  217.7 106.8 all-gather.12
  367.0 70.7 reduce-scatter.8
  504.4 52.5 all-gather.14
  590.3 71.2 reduce-scatter.10
  694.8 44.0 all-gather.16
  743.2 39.9 reduce-scatter.16
  785.5 43.8 reduce-scatter.12
  833.0 74.6 reduce-scatter.14

commit v2 on v1

--- a/solution.py
+++ b/solution.py
@@ -1,6 +1,10 @@
+import functools
+
 import jax
 import jax.numpy as jnp
 from jax import lax
+from jax.experimental import pallas as pl
+from jax.experimental.pallas import tpu as pltpu
 from jax.sharding import PartitionSpec as P
 
 HEAD_DIM = 128
@@ -11,6 +15,531 @@
 NEGATIVE = -1e30
 THETA = 10000.0
 HIGH = lax.Precision.HIGHEST
+MESH_ID = pl.DeviceIdType.MESH
+LANES = 128
+
+
+def remote(src, dst, send_sem, recv_sem, peer):
+    return pltpu.make_async_remote_copy(
+        src_ref=src,
+        dst_ref=dst,
+        send_sem=send_sem,
+        recv_sem=recv_sem,
+        device_id=peer,
+        device_id_type=MESH_ID,
+    )
+
+
+def greet(peers):
+    barrier = pltpu.get_barrier_semaphore()
+    for peer in peers:
+        pl.semaphore_signal(barrier, inc=1, device_id=peer, device_id_type=MESH_ID)
+    pl.semaphore_wait(barrier, len(peers))
+
+
+def dot_nn(left, right):
+    return jnp.dot(left, right, preferred_element_type=jnp.float32)
+
+
+def dot_nt(left, right):
+    return lax.dot_general(
+        left, right, (((1,), (1,)), ((), ())), preferred_element_type=jnp.float32
+    )
+
+
+def experts_kernel(
+    group,
+    sent,
+    d_back,
+    w_own,
+    w_x,
+    w_y,
+    w_diag,
+    down_own,
+    ret,
+    d_ret,
+    grad_gate_up,
+    grad_down,
+    w_buf,
+    down_buf,
+    rows_buf,
+    gate_buf,
+    act_buf,
+    part_buf,
+    half_x,
+    half_y,
+    full_x,
+    full_y,
+    other_gate,
+    other_down,
+    stage,
+    ag_sems,
+    rs_sems,
+    weight_sems,
+    local_sems,
+    grad_sems,
+):
+    cap, width = sent.shape[1], sent.shape[2]
+    half = cap // 2
+    piece = w_own.shape[0]
+    hidden2 = w_own.shape[1]
+    hidden = hidden2 // 2
+    down_rows = down_own.shape[0]
+    chunk = 4 * cap
+    total = group * chunk
+
+    index = lax.axis_index("dp")
+    place = lax.axis_index("expert")
+    core = index % 2
+    at_x = (index // 2) % 2
+    at_y = index // 4
+    partner = {"dp": at_y * 4 + at_x * 2 + (1 - core)}
+    along_x = {"dp": at_y * 4 + (1 - at_x) * 2 + core}
+    along_y = {"dp": (1 - at_y) * 4 + at_x * 2 + core}
+    chips = [
+        at_y * 2 + at_x,
+        at_y * 2 + (1 - at_x),
+        (1 - at_y) * 2 + at_x,
+        (1 - at_y) * 2 + (1 - at_x),
+    ]
+
+    def ahead(k):
+        return {"expert": (place + k) % group}
+
+    def behind(k):
+        return {"expert": (place + group - k) % group}
+
+    greet([partner, along_x, along_y] + [ahead(k) for k in range(1, group)])
+
+    def block(t, k, r, start=0, size=None):
+        size = cap if size is None else size
+        return rows_buf.at[t, pl.ds((k * 4 + r) * cap + start, size), :]
+
+    def part(t, k, r, start=0, size=None):
+        size = cap if size is None else size
+        return part_buf.at[t, pl.ds((k * 4 + r) * cap + start, size), :]
+
+    def ag(kind, t, k):
+        return ag_sems.at[0, kind, t, k], ag_sems.at[1, kind, t, k]
+
+    def rs(kind, t, k):
+        return rs_sems.at[0, kind, t, k], rs_sems.at[1, kind, t, k]
+
+    sources = (sent, d_back)
+    results = (ret, d_ret)
+
+    def z_copy(t, k):
+        return remote(sources[t].at[k], block(t, k, 0), *ag(0, t, k), ahead(k))
+
+    def own_copy(t):
+        return pltpu.make_async_copy(sources[t].at[0], block(t, 0, 0), local_sems.at[t])
+
+    def x_copy(t, k):
+        return remote(block(t, k, 0), block(t, k, 1), *ag(1, t, k), along_x)
+
+    def y_copy(t, k):
+        return remote(block(t, k, 0), block(t, k, 2), *ag(2, t, k), along_y)
+
+    def a_copy(t, k):
+        return remote(block(t, k, 2, 0, half), block(t, k, 3, 0, half), *ag(3, t, k), along_x)
+
+    def b_copy(t, k):
+        return remote(
+            block(t, k, 1, half, half), block(t, k, 3, half, half), *ag(4, t, k), along_y
+        )
+
+    def spread(t, k):
+        if k == 0:
+            own_copy(t).wait()
+        else:
+            z_copy(t, k).wait_recv()
+        x_copy(t, k).start()
+        y_copy(t, k).start()
+
+    def relay(t, k):
+        y_copy(t, k).wait_recv()
+        a_copy(t, k).start()
+        x_copy(t, k).wait_recv()
+        b_copy(t, k).start()
+
+    def arrived(t, k):
+        a_copy(t, k).wait_recv()
+        b_copy(t, k).wait_recv()
+
+    def half_x_copy(t, k):
+        return remote(part(t, k, 3, 0, half), half_x.at[t, k], *rs(0, t, k), along_x)
+
+    def half_y_copy(t, k):
+        return remote(part(t, k, 3, half, half), half_y.at[t, k], *rs(1, t, k), along_y)
+
+    def full_x_copy(t, k):
+        return remote(part(t, k, 1), full_x.at[t, k], *rs(2, t, k), along_x)
+
+    def full_y_copy(t, k):
+        return remote(part(t, k, 2), full_y.at[t, k], *rs(3, t, k), along_y)
+
+    def back_copy(t, k):
+        return remote(part(t, k, 0), results[t].at[k], *rs(4, t, k), behind(k))
+
+    def keep_copy(t):
+        return pltpu.make_async_copy(part(t, 0, 0), results[t].at[0], local_sems.at[2 + t])
+
+    def halves_out(t, k):
+        half_x_copy(t, k).start()
+        half_y_copy(t, k).start()
+
+    def add_into(target, *others):
+        value = target[...].astype(jnp.float32)
+        for other in others:
+            value = value + other[...].astype(jnp.float32)
+        target[...] = value.astype(jnp.bfloat16)
+
+    def fulls_out(t, k):
+        half_x_copy(t, k).wait_recv()
+        add_into(part(t, k, 2, 0, half), half_x.at[t, k])
+        full_y_copy(t, k).start()
+        half_y_copy(t, k).wait_recv()
+        add_into(part(t, k, 1, half, half), half_y.at[t, k])
+        full_x_copy(t, k).start()
+
+    def home(t, k):
+        full_x_copy(t, k).wait_recv()
+        full_y_copy(t, k).wait_recv()
+        add_into(part(t, k, 0), full_x.at[t, k], full_y.at[t, k])
+        if k == 0:
+            keep_copy(t).start()
+        else:
+            back_copy(t, k).start()
+
+    pieces = (w_own, w_x, w_y, w_diag)
+
+    def w_rows(r, which):
+        return w_buf.at[pl.ds(pl.multiple_of((chips[r] * 2 + which) * piece, piece), piece), :]
+
+    def w_share(r):
+        return remote(
+            pieces[r], w_rows(r, core), weight_sems.at[0, r], weight_sems.at[1, r], partner
+        )
+
+    def w_share_in(r):
+        return remote(
+            pieces[r], w_rows(r, 1 - core), weight_sems.at[0, r], weight_sems.at[1, r], partner
+        )
+
+    def w_keep(r):
+        return pltpu.make_async_copy(pieces[r], w_rows(r, core), local_sems.at[4 + r])
+
+    def down_at(which):
+        return down_buf.at[pl.ds(pl.multiple_of(which * down_rows, down_rows), down_rows), :]
+
+    def down_share():
+        return remote(
+            down_own, down_at(core), weight_sems.at[0, 4], weight_sems.at[1, 4], partner
+        )
+
+    down_keep = pltpu.make_async_copy(down_own, down_at(core), local_sems.at[8])
+
+    def forward(k):
+        base = k * chunk
+
+        def tile(j, carry):
+            cols = pl.ds(pl.multiple_of(j * 2 * LANES, 2 * LANES), 2 * LANES)
+            both = dot_nn(rows_buf[0, base : base + chunk, :], w_buf[:, cols])
+            gate = both[:, :LANES]
+            sigmoid = 1.0 / (1.0 + jnp.exp(-gate))
+            act = gate * sigmoid * both[:, LANES:]
+            gate_buf[base : base + chunk, cols] = both.astype(jnp.bfloat16)
+            narrow = pl.ds(pl.multiple_of(j * LANES, LANES), LANES)
+            act_buf[base : base + chunk, narrow] = act.astype(jnp.bfloat16)
+            return carry
+
+        lax.fori_loop(0, hidden // LANES, tile, 0)
+
+        def out_tile(j, carry):
+            cols = pl.ds(pl.multiple_of(j * 2 * LANES, 2 * LANES), 2 * LANES)
+            out = dot_nn(act_buf[base : base + chunk, :], down_buf[:, cols])
+            part_buf[0, base : base + chunk, cols] = out.astype(jnp.bfloat16)
+            return carry
+
+        lax.fori_loop(0, width // (2 * LANES), out_tile, 0)
+
+    def backward(k):
+        base = k * chunk
+
+        def tile(first, count):
+            rows = pl.ds(pl.multiple_of(first * LANES, LANES), count * LANES)
+            d_act = dot_nt(rows_buf[1, base : base + chunk, :], down_buf[rows, :])
+            for i in range(count):
+                cols = pl.ds(pl.multiple_of((first + i) * 2 * LANES, 2 * LANES), 2 * LANES)
+                both = gate_buf[base : base + chunk, cols].astype(jnp.float32)
+                gate = both[:, :LANES]
+                up = both[:, LANES:]
+                sigmoid = 1.0 / (1.0 + jnp.exp(-gate))
+                scaled = d_act[:, i * LANES : (i + 1) * LANES] * sigmoid
+                d_gate = scaled * up * (1.0 + gate * (1.0 - sigmoid))
+                d_up = scaled * gate
+                gate_buf[base : base + chunk, cols] = jnp.concatenate(
+                    [d_gate, d_up], axis=1
+                ).astype(jnp.bfloat16)
+
+        def pair(j, carry):
+            tile(2 * j, 2)
+            return carry
+
+        blocks = hidden // LANES
+        lax.fori_loop(0, blocks // 2, pair, 0)
+        if blocks % 2:
+            tile(blocks - 1, 1)
+
+        def out_tile(j, carry):
+            cols = pl.ds(pl.multiple_of(j * 2 * LANES, 2 * LANES), 2 * LANES)
+            out = dot_nt(gate_buf[base : base + chunk, :], w_buf[cols, :])
+            part_buf[1, base : base + chunk, cols] = out.astype(jnp.bfloat16)
+            return carry
+
+        lax.fori_loop(0, width // (2 * LANES), out_tile, 0)
+
+    w_share(0).start()
+    w_keep(0).start()
+    own_copy(0).start()
+    for k in range(1, group):
+        z_copy(0, k).start()
+    for r in range(1, 4):
+        w_share(r).start()
+        w_keep(r).start()
+    down_share().start()
+    down_keep.start()
+    own_copy(1).start()
+
+    spread(0, 0)
+    spread(0, 1)
+    relay(0, 0)
+    for k in range(1, group):
+        z_copy(1, k).start()
+    spread(0, 2)
+    relay(0, 1)
+    arrived(0, 0)
+    for r in range(4):
+        w_keep(r).wait()
+        w_share_in(r).wait_recv()
+    down_keep.wait()
+    down_share().wait_recv()
+    forward(0)
+    spread(0, 3)
+    relay(0, 2)
+    arrived(0, 1)
+    forward(1)
+    spread(1, 0)
+    relay(0, 3)
+    arrived(0, 2)
+    forward(2)
+    spread(1, 1)
+    relay(1, 0)
+    arrived(0, 3)
+    forward(3)
+    spread(1, 2)
+    relay(1, 1)
+    arrived(1, 0)
+    backward(0)
+    spread(1, 3)
+    relay(1, 2)
+    arrived(1, 1)
+    halves_out(0, 0)
+    halves_out(0, 1)
+    backward(1)
+    relay(1, 3)
+    arrived(1, 2)
+    halves_out(0, 2)
+    halves_out(0, 3)
+    fulls_out(0, 0)
+    fulls_out(0, 1)
+    halves_out(1, 0)
+    backward(2)
+    arrived(1, 3)
+    fulls_out(0, 2)
+    fulls_out(0, 3)
+    halves_out(1, 1)
+    home(0, 0)
+    home(0, 1)
+    backward(3)
+    halves_out(1, 2)
+    halves_out(1, 3)
+    fulls_out(1, 0)
+    fulls_out(1, 1)
+
+    act_t = down_buf.at[:, pl.ds(0, total)]
+    rows_t = down_buf.at[pl.ds(0, piece), pl.ds(total, total)]
+    send_down = w_buf.at[pl.ds(4 * piece, down_rows), pl.ds(0, width)]
+
+    def send_gate(r):
+        return w_buf.at[pl.ds(r * piece, piece), :]
+
+    def turn(j, carry):
+        cols = pl.ds(pl.multiple_of(j * LANES, LANES), LANES)
+        act_t[cols, :] = act_buf[:, cols].T
+        return carry
+
+    lax.fori_loop(0, hidden // LANES, turn, 0)
+
+    def down_grad(which, j):
+        cols = pl.ds(pl.multiple_of(j * 2 * LANES, 2 * LANES), 2 * LANES)
+        rows = pl.ds(pl.multiple_of(which * down_rows, down_rows), down_rows)
+        return cols, dot_nn(act_t[rows, :], rows_buf[1, :, cols])
+
+    def down_for_partner(j, carry):
+        cols, value = down_grad(1 - core, j)
+        send_down[:, cols] = value.astype(jnp.bfloat16)
+        return carry
+
+    tiles = width // (2 * LANES)
+    lax.fori_loop(0, tiles, down_for_partner, 0)
+    down_send = remote(
+        send_down, other_down, grad_sems.at[0, 4], grad_sems.at[1, 4], partner
+    )
+    down_send.start()
+    home(0, 2)
+    home(0, 3)
+    fulls_out(1, 2)
+    fulls_out(1, 3)
+
+    def gate_grad(r, which, store):
+        start = pl.multiple_of((chips[r] * 2 + which) * piece, piece)
+        rows_t[...] = rows_buf[0, :, pl.ds(start, piece)].T
+
+        def tile(j, carry):
+            cols = pl.ds(pl.multiple_of(j * 2 * LANES, 2 * LANES), 2 * LANES)
+            store(cols, dot_nn(rows_t[...], gate_buf[:, cols]))
+            return carry
+
+        lax.fori_loop(0, hidden2 // (2 * LANES), tile, 0)
+
+    def gate_send(r):
+        return remote(
+            send_gate(r), other_gate.at[r], grad_sems.at[0, r], grad_sems.at[1, r], partner
+        )
+
+    for r in range(4):
+        target = send_gate(r)
+
+        def store(cols, value, target=target):
+            target[:, cols] = value.astype(jnp.bfloat16)
+
+        gate_grad(r, 1 - core, store)
+        gate_send(r).start()
+        if r == 0:
+            home(1, 0)
+            home(1, 1)
+        if r == 1:
+            home(1, 2)
+        if r == 2:
+            home(1, 3)
+
+    down_send.wait_recv()
+
+    def stage_copy(j):
+        cols = pl.ds(pl.multiple_of(j * 2 * LANES, 2 * LANES), 2 * LANES)
+        return pltpu.make_async_copy(
+            stage.at[j % 2], grad_down.at[:, cols], grad_sems.at[2, j % 2]
+        )
+
+    def down_for_self(j, carry):
+        cols, value = down_grad(core, j)
+
+        @pl.when(j >= 2)
+        def _():
+            stage_copy(j - 2).wait()
+
+        stage[j % 2] = value + other_down[:, cols].astype(jnp.float32)
+        stage_copy(j).start()
+        return carry
+
+    lax.fori_loop(0, tiles, down_for_self, 0)
+
+    def gate_out(r):
+        return pltpu.make_async_copy(other_gate.at[r], grad_gate_up.at[r], grad_sems.at[2, 2 + r])
+
+    for r in range(4):
+        gate_send(r).wait_recv()
+        target = other_gate.at[r]
+
+        def store(cols, value, target=target):
+            target[:, cols] = (value + target[:, cols].astype(jnp.float32)).astype(jnp.bfloat16)
+
+        gate_grad(r, core, store)
+        gate_out(r).start()
+
+    stage_copy(tiles - 2).wait()
+    stage_copy(tiles - 1).wait()
+    for r in range(4):
+        gate_out(r).wait()
+        gate_send(r).wait_send()
+        w_share(r).wait_send()
+    down_share().wait_send()
+    down_send.wait_send()
+    for t in range(2):
+        keep_copy(t).wait()
+        for k in range(group):
+            x_copy(t, k).wait_send()
+            y_copy(t, k).wait_send()
+            a_copy(t, k).wait_send()
+            b_copy(t, k).wait_send()
+            half_x_copy(t, k).wait_send()
+            half_y_copy(t, k).wait_send()
+            full_x_copy(t, k).wait_send()
+            full_y_copy(t, k).wait_send()
+            if k > 0:
+                z_copy(t, k).wait_send()
+                back_copy(t, k).wait_send()
+                back_copy(t, k).wait_recv()
+
+
+def experts_call(sent, d_back, pieces, down_own):
+    group, cap, width = sent.shape
+    piece, hidden2 = pieces[0].shape
+    hidden = hidden2 // 2
+    down_rows = down_own.shape[0]
+    chunk = 4 * cap
+    total = group * chunk
+    low = jnp.bfloat16
+    anywhere = pl.BlockSpec(memory_space=pl.ANY)
+    flops = 2 * total * width * hidden * 9
+    moved = 2 * (4 * piece * hidden2 * 2 + down_rows * width * 3)
+    return pl.pallas_call(
+        functools.partial(experts_kernel, group),
+        out_shape=(
+            jax.ShapeDtypeStruct((group, cap, width), low),
+            jax.ShapeDtypeStruct((group, cap, width), low),
+            jax.ShapeDtypeStruct((4, piece, hidden2), low),
+            jax.ShapeDtypeStruct((down_rows, width), jnp.float32),
+        ),
+        in_specs=[anywhere] * 7,
+        out_specs=(anywhere,) * 4,
+        scratch_shapes=[
+            pltpu.VMEM((width, hidden2), low),
+            pltpu.VMEM((hidden, width), low),
+            pltpu.VMEM((2, total, width), low),
+            pltpu.VMEM((total, hidden2), low),
+            pltpu.VMEM((total, hidden), low),
+            pltpu.VMEM((2, total, width), low),
+            pltpu.VMEM((2, group, cap // 2, width), low),
+            pltpu.VMEM((2, group, cap // 2, width), low),
+            pltpu.VMEM((2, group, cap, width), low),
+            pltpu.VMEM((2, group, cap, width), low),
+            pltpu.VMEM((4, piece, hidden2), low),
+            pltpu.VMEM((down_rows, width), low),
+            pltpu.VMEM((2, down_rows, 2 * LANES), jnp.float32),
+            pltpu.SemaphoreType.DMA((2, 5, 2, group)),
+            pltpu.SemaphoreType.DMA((2, 5, 2, group)),
+            pltpu.SemaphoreType.DMA((2, 5)),
+            pltpu.SemaphoreType.DMA((9,)),
+            pltpu.SemaphoreType.DMA((3, 6)),
+        ],
+        compiler_params=pltpu.CompilerParams(
+            collective_id=1, has_side_effects=True, vmem_limit_bytes=67043328
+        ),
+        cost_estimate=pl.CostEstimate(flops=flops, bytes_accessed=moved, transcendentals=0),
+        name="experts",
+    )(sent, d_back, *pieces, down_own)
 
 
 def rotary_tables(length_total, head_size):
@@ -38,7 +567,7 @@
     )
 
 
-def slot_table(routes, order, valid, capacity):
+def slot_table(routes, order, valid, capacity, first_expert, experts):
     row_count = routes.shape[0]
     top_count = routes.shape[1]
     pair_rank = order[:, None] + row_count * jnp.arange(top_count, dtype=jnp.int32)[None, :]
@@ -52,7 +581,8 @@
     )
     slot_index = jnp.sum(earlier.astype(jnp.int32), axis=1).reshape(row_count, top_count)
     kept_pair = valid[:, None] & (slot_index < capacity)
-    target = routes * capacity + jnp.minimum(slot_index, capacity - 1)
+    place = (routes + experts - first_expert) % experts
+    target = place * capacity + jnp.minimum(slot_index, capacity - 1)
     return (target, kept_pair)
 
 
@@ -83,24 +613,41 @@
     return lax.all_to_all(blocks, "expert", split_axis=0, concat_axis=0, tiled=True)
 
 
-def by_hidden(w_gate_up):
+def across(index, step):
+    return ((index // 2) ^ step) * 2 + index % 2
+
+
+def swap_chips(pieces):
     parts = lax.axis_size("dp")
-    rows = w_gate_up.shape[1]
-    ff_part = w_gate_up.shape[2] // 2 // parts
-    pieces = w_gate_up[0].reshape(rows, 2, parts, ff_part).transpose(2, 0, 1, 3)
-    pieces = pieces.reshape(parts, rows, 2 * ff_part)
-    got = lax.all_to_all(pieces, "dp", split_axis=0, concat_axis=0, tiled=True)
-    return got.reshape(parts * rows, 2 * ff_part)
-
-
-def by_rows(grad):
-    parts = lax.axis_size("dp")
-    rows = grad.shape[0] // parts
-    ff_part = grad.shape[1] // 2
-    pieces = grad.astype(jnp.bfloat16).reshape(parts, rows, 2 * ff_part)
-    got = lax.all_to_all(pieces, "dp", split_axis=0, concat_axis=0, tiled=True)
-    got = got.reshape(parts, rows, 2, ff_part).transpose(1, 2, 0, 3)
-    return got.reshape(1, rows, 2 * parts * ff_part).astype(jnp.float32)
+    got = [pieces[0]]
+    for step in (1, 2, 3):
+        pairs = [(index, across(index, step)) for index in range(parts)]
+        got.append(lax.ppermute(pieces[step], "dp", pairs))
+    return got
+
+
+def chip_slices(w_gate_up):
+    rows, ff2 = w_gate_up.shape[1:]
+    chips = lax.axis_size("dp") // 2
+    blocks = ff2 // 2 // chips // LANES
+    own = lax.axis_index("dp") // 2
+    slices = w_gate_up[0].reshape(rows, 2, chips, blocks, LANES).transpose(2, 0, 3, 1, 4)
+    slices = slices.reshape(chips, rows, ff2 // chips)
+    return swap_chips(
+        [lax.dynamic_index_in_dim(slices, own ^ step, 0, keepdims=False) for step in range(chips)]
+    )
+
+
+def chip_slices_back(grads):
+    chips, rows, hidden2 = grads.shape
+    own = lax.axis_index("dp") // 2
+    got = swap_chips([grads[step] for step in range(chips)])
+    whole = jnp.zeros((chips, rows, hidden2), jnp.bfloat16)
+    for step in range(chips):
+        whole = lax.dynamic_update_index_in_dim(whole, got[step], own ^ step, 0)
+    blocks = hidden2 // 2 // LANES
+    whole = whole.reshape(chips, rows, blocks, 2, LANES).transpose(1, 3, 0, 2, 4)
+    return whole.reshape(1, rows, chips * hidden2).astype(jnp.float32)
 
 
 def expert_step(gate_up_w, down_w, rows, d_rows_out):
@@ -122,21 +669,22 @@
 
 
 def experts_split_hidden(w_gate_up, w_down, rows, d_rows_out):
-    gate_up_w = by_hidden(w_gate_up)
-    all_rows = lax.all_gather(rows, "dp", axis=0, tiled=True)
-    all_d_out = lax.all_gather(d_rows_out, "dp", axis=0, tiled=True)
-    out, d_rows, grad_gate_up, grad_down = expert_step(
-        gate_up_w, w_down[0], all_rows, all_d_out
-    )
-    out = lax.psum_scatter(out, "dp", scatter_dimension=0, tiled=True)
-    d_rows = lax.psum_scatter(d_rows, "dp", scatter_dimension=0, tiled=True)
-    return out, d_rows, by_rows(grad_gate_up), grad_down[None]
+    out, d_rows, grad_gate_up, grad_down = experts_call(
+        rows, d_rows_out, chip_slices(w_gate_up), w_down[0]
+    )
+    return out, d_rows, chip_slices_back(grad_gate_up), grad_down[None]
 
 
 def experts_gather_weights(w_gate_up, w_down, rows, d_rows_out):
     gate_up_w = lax.all_gather(w_gate_up, "dp", axis=1, tiled=True)[0]
     down_w = lax.all_gather(w_down, "dp", axis=1, tiled=True)[0]
+    shape = rows.shape
+    flat = (-1, shape[2])
+    rows = exchange_experts(rows).reshape(flat)
+    d_rows_out = exchange_experts(d_rows_out).reshape(flat)
     out, d_rows, grad_gate_up, grad_down = expert_step(gate_up_w, down_w, rows, d_rows_out)
+    out = exchange_experts(out.reshape(shape))
+    d_rows = exchange_experts(d_rows.reshape(shape))
     grad_gate_up = lax.psum_scatter(
         grad_gate_up.astype(jnp.bfloat16), "dp", scatter_dimension=0, tiled=True
     )
@@ -191,7 +739,9 @@
     own_position = own_start + jnp.arange(tok_dev, dtype=jnp.int32)
     live_own = own_position < lengths[0]
     live_rows = live_own.astype(jnp.float32)[:, None]
-    target, kept_pair = slot_table(routes, order, live_own, capacity)
+    split = dp_size == 8 and group_size == 4
+    first_expert = lax.axis_index("expert") if split else 0
+    target, kept_pair = slot_table(routes, order, live_own, capacity, first_expert, group_size)
     slot_ids = jnp.arange(slots, dtype=jnp.int32)
     pair_hits = (slot_ids[:, None, None] == target[None]) & kept_pair[None]
     select = jnp.sum(pair_hits.astype(jnp.float32), axis=2).astype(jnp.bfloat16)
@@ -229,7 +779,6 @@
     hhat, inverse_two = normalize(resid)
     hidden_in = (hhat * gain_two).astype(jnp.bfloat16)
     sent = jnp.dot(select, hidden_in, preferred_element_type=jnp.float32).astype(jnp.bfloat16)
-    dispatched = exchange_experts(sent.reshape(group_size, capacity, width)).reshape(slots, width)
 
     logits = jnp.dot(hidden_in, router_full, preferred_element_type=jnp.float32)
     chosen = jnp.take_along_axis(logits, routes, axis=1)
@@ -244,20 +793,13 @@
             preferred_element_type=jnp.float32,
         )
     d_back = d_back.astype(jnp.bfloat16)
-    d_out_rows = exchange_experts(d_back.reshape(group_size, capacity, width)).reshape(
-        slots, width
-    )
-
-    split_cost = 4 * dp_size * slots * width + 2 * 2 * FF * width // dp_size
-    gather_cost = 2 * 3 * FF * width
-    experts = experts_split_hidden if split_cost < gather_cost else experts_gather_weights
-    expert_out, d_rows, grad_gate_up, grad_down = experts(
-        w_gate_up, w_down, dispatched, d_out_rows
-    )
-    d_sent = exchange_experts(d_rows.reshape(group_size, capacity, width)).reshape(slots, width)
-    returned = exchange_experts(expert_out.reshape(group_size, capacity, width)).reshape(
-        slots, width
-    )
+    experts = experts_split_hidden if split else experts_gather_weights
+    blocked = (group_size, capacity, width)
+    returned, d_sent, grad_gate_up, grad_down = experts(
+        w_gate_up, w_down, sent.reshape(blocked), d_back.reshape(blocked)
+    )
+    returned = returned.reshape(slots, width)
+    d_sent = d_sent.reshape(slots, width)
 
     moe = jnp.zeros_like(resid)
     d_gates_list = []

time: 991 us -> 699 us (0.71)
  waiting for transfers between devices: 466 us -> 244 us
  Pallas kernels: 0 us -> 176 us
  blocking collectives: 199 us -> 49.2 us
  matrix products: 142 us -> 56.2 us
  local copies, waits for them, and re-layouts: 88.3 us -> 108 us
  starting transfers between devices: 24.9 us -> 8.21 us
  other arithmetic: 43.5 us -> 33.1 us
    pallas_call x0 -> x1, Pallas kernels: none -> 176 us  [experts_call(): pl.pallas_call(functools.partial(experts_kernel, group), out_shape=(jax.S...]
    all_to_all x3 -> x0, blocking collectives: 152 us -> none  [the longest x1 94.4 us: by_hidden(): got = lax.all_to_all(pieces, 'dp', split_axis=0, concat_axis=0, tiled=True)]
    reduce_scatter x2 -> x0, waiting for transfers between devices: 142 us -> none  [the longest x1 71.3 us: experts_split_hidden(): d_rows = lax.psum_scatter(d_rows, 'dp', scatter_dimension=0, tiled=True)]
    all_to_all x3 -> x0, waiting for transfers between devices: 105 us -> none  [the longest x1 70.9 us: by_rows(): got = lax.all_to_all(pieces, 'dp', split_axis=0, concat_axis=0, tiled=True)]
    ppermute x0 -> x6, waiting for transfers between devices: none -> 90.1 us  [swap_chips(): got.append(lax.ppermute(pieces[step], 'dp', pairs))]
    all_gather x2 -> x0, waiting for transfers between devices: 52.6 us -> none  [the longest x1 52.6 us: experts_split_hidden(): all_d_out = lax.all_gather(d_rows_out, 'dp', axis=0, tiled=True)]
    reduce_scatter x1, waiting for transfers between devices: 41.9 us -> 10.6 us  [on_device(): lax.psum_scatter(attn_part.astype(jnp.bfloat16), 'expert', scatter_dimens...]
    dot_general x3 -> x1, matrix products: 34.4 us -> 3.65 us  [contract_last(): lax.dot_general(left, right, (((1,), (1,)), ((), ())), preferred_element_...]
  transfers between devices with their start and end apart: 15 -> 14, of which waited for: 11 -> 9; matrix products, arithmetic and copies ran while one was open for 18% -> 25% of each run, Pallas kernels for 0% -> 0%
where the time goes in v2:
time: 699 us; the launch traced here: 691 us
  waiting for transfers between devices  244 us (35%)
  Pallas kernels  176 us (25%)
  local copies, waits for them, and re-layouts  108 us (15%)
  matrix products  56.2 us (8%)
  blocking collectives  49.2 us (7%)
  other arithmetic  33.1 us (5%)
  between operations  16.3 us (2%)
  starting transfers between devices  8.21 us (1%)
    pallas_call x1, Pallas kernels, experts_call(): pl.pallas_call(functools.partial(experts_kernel, group), out_shape=(jax.S...  176 us
    ppermute x6, waiting for transfers between devices, swap_chips(): got.append(lax.ppermute(pieces[step], 'dp', pairs))  90.1 us
    all_gather x1, waiting for transfers between devices, on_device(): whole_grad = lax.all_gather(d_attn, 'expert', axis=0, tiled=True)  53.7 us
    all_gather x1, waiting for transfers between devices, on_device(): qkv_full = lax.all_gather(w_qkv, 'dp', axis=1, tiled=True)  45.8 us
    unnamed x134, local copies, waits for them, and re-layouts  38.9 us
    psum x1, blocking collectives, on_device(): small_sum = lax.psum(small_part, ('dp', 'expert'))  38.7 us
    all_gather x1, waiting for transfers between devices, on_device(): tokens_all = lax.all_gather(tokens, 'expert', axis=0, tiled=True)  33.4 us
  transfers between devices with their start and end apart: 14, of which 9 were waited for; matrix products, arithmetic and copies ran while one was open for 25% of the time, Pallas kernels for 0%

profile of v2, /device:TPU:0, one launch (start us, length us, event | category | flops | bytes accessed | tf_op | source)
XLA Modules:
  0.0 690.6 jit_solution(9599435043548869980)
XLA Ops:
  8.0 2.3 copy.249
  11.8 10.5 %all_gather.16 = bf16[2048,6]{0,1:T(8,128)(2,1)S(1)} all-gather(bf16[256,6]{0,1:T(8,128)(2,1)S(1)} %pad_maximum_fusion.12), channel_id=1, replica_groups=mesh['dp'=8,'expert'=4] {'dp'}, dimensions={0}, use_global_device_ids=true | all-gather | bytes 27648 | tf_op jit(solution)/shard_map/all_gather | solution.py:731
  22.4 1.7 fusion.38
  24.9 33.4 %all-gather.5.cloned.1.call-done = bf16[512,2048]{1,0:T(8,128)(2,1)} async-done(((bf16[128,2048]{1,0:T(8,128)(2,1)}), bf16[512,2048]{1,0:T(8,128)(2,1)}) %all-gather.5.cloned.1.call-update) | async-done | bytes 2097168 | tf_op jit(solution)/shard_map/all_gather | solution.py:727
  58.3 2.1 fusion.4
  60.4 45.8 %all-gather.7.cloned.1.call-done = bf16[3,2048,512]{1,2,0:T(8,128)(2,1)} async-done(((bf16[3,256,512]{1,2,0:T(8,128)(2,1)}), bf16[3,2048,512]{1,2,0:T(8,128)(2,1)}) %all-gather.7.cloned.1.call-update) | async-done | bytes 6291472 | tf_op jit(solution)/shard_map/all_gather | solution.py:732
  106.1 6.4 convolution_bitcast_fusion
  114.8 1.4 copy.301
  117.3 1.4 copy.303
  118.7 2.4 copy.304
  121.0 1.9 subtract_convert_fusion.3
  123.0 1.4 fusion.65
  125.0 1.4 copy-done
  127.4 8.8 %all-gather.9.cloned.1.call-done = bf16[512,2048]{1,0:T(8,128)(2,1)} async-done(((bf16[512,256]{1,0:T(8,128)(2,1)}), bf16[512,2048]{1,0:T(8,128)(2,1)}) %all-gather.9.cloned.1.call-update) | async-done | bytes 2097168 | tf_op jit(solution)/shard_map/all_gather | solution.py:733
  136.3 4.2 convolution_convert_fusion.1
  141.0 8.3 %copy.260 = bf16[1,256,11264]{1,2,0:T(8,128)(2,1)} copy(bf16[1,256,11264]{2,1,0:T(8,128)(2,1)} %param.18) | data formatting | bytes 11534336 | tf_op args[6]
  149.4 5.9 copy.261
  155.2 4.7 constant_dynamic-slice_fusion.1
  159.9 2.5 copy.263
  162.4 1.5 collective-permute-start
  163.9 2.5 copy.264
  167.1 1.7 copy.265
  168.8 1.3 collective-permute-start.2
  172.0 1.7 copy.262
  173.9 10.6 %reduce-scatter.5.cloned.1.call-done = bf16[128,2048]{1,0:T(8,128)(2,1)} async-done(((bf16[512,2048]{1,0:T(8,128)(2,1)}), bf16[128,2048]{1,0:T(8,128)(2,1)}) %reduce-scatter.5.cloned.1.call-update) | async-done | bytes 524304 | tf_op jit(solution)/shard_map/reduce_scatter | solution.py:775
  184.5 1.3 multiply_reduce_fusion.5
  187.3 2.4 gather_fusion
  190.1 1.4 convolution_convert_fusion.2
  192.1 1.5 fusion.7
  193.6 3.6 collective-permute-done.w_x
  197.2 33.9 %collective-permute-done.1.w_y = bf16[256,2816]{1,0:T(8,128)(2,1)} collective-permute-done((bf16[256,2816]{1,0:T(8,128)(2,1)}, bf16[256,2816]{1,0:T(8,128)(2,1)}, u32[]{:S(2)}, u32[]{:S(2)}) %collective-permute-start.1) | collective-permute-done | bytes 1441824 | tf_op jit(solution)/shard_map/ppermute | solution.py:625
  231.1 176.0 %experts.1 = (bf16[4,64,2048]{2,1,0:T(8,128)(2,1)}, bf16[4,64,2048]{2,1,0:T(8,128)(2,1)}, bf16[4,256,2816]{2,1,0:T(8,128)(2,1)}, f32[704,2048]{1,0:T(8,128)}) custom-call(bf16[4,64,2048]{2,1,0:T(8,128)(2,1)} %bitcast.128, bf16[4,64,2048]{2,1,0:T(8,128)(2,1)} %bitcast.131, bf16[256,2816]{1,0:T(8,128)(2,1)} %bitcast.126, ...), custom_call_target="tpu_custom_call" | custom-call | flops 53150220288 | bytes 20185088 | tf_op jit(solution)/shard_map/experts/pallas_call | solution.py:507
  407.1 1.7 fusion.41
  408.9 3.4 multiply_reduce_fusion.4
  415.2 53.7 %all-gather.11.cloned.1.call-done = bf16[512,2048]{1,0:T(8,128)(2,1)} async-done(((bf16[128,2048]{1,0:T(8,128)(2,1)}), bf16[512,2048]{1,0:T(8,128)(2,1)}) %all-gather.11.cloned.1.call-update) | async-done | bytes 2097168 | tf_op jit(solution)/shard_map/all_gather | solution.py:834
  468.9 4.4 convolution_convert_fusion
  473.6 3.7 convolution_convert_fusion.3
  477.3 1.6 fusion.15
  478.9 2.1 copy.279
  481.0 3.7 multiply_reduce_fusion
  489.3 1.5 pad_maximum_fusion.5
  495.4 9.4 %bitcast_convert_fusion = (bf16[512,2048]{1,0:T(8,128)(2,1)}, f32[512,2048,1]{1,0,2:T(8,128)}) fusion(bf16[3,2048,512]{1,2,0:T(8,128)(2,1)} %all-gather.7.cloned.1.call-done, bf16[1,512,512]{2,1,0:T(8,128)(2,1)} %copy.279, bf16[1,512,512]{2,1,0:T(8,128)(2,1)} %copy.278, bf16[1,512,512]{2,1,0:T(8,128)(2,1)} %copy.277), kind=kOutput, calls=%fused_computation.10 | convolution fusion | flops 3223846912 | bytes 14155776 | tf_op jit(solution)/shard_map/cte,cde->td/dot_general | solution.py:859
  505.2 8.2 %convert_bitcast_fusion.1 = bf16[3,2048,512]{1,2,0:T(8,128)(2,1)} fusion(bf16[512,2048]{1,0:T(8,128)(2,1)} %all-gather.5.cloned.1.call-done, f32[2048]{0:T(1024)S(1)} %bitcast.137, f32[512]{0:T(512)S(1)} %copy-done.52, bf16[1,512,512]{2,1,0:T(8,128)(2,1)S(1)} %copy-done.29, bf16[1,512,512]{2,1,0:T(8,128)(2,1)} %copy.278, bf16[1,512,512]{2,1,0:T(8,128)(2,1)} %copy.277), kind=kOutput, calls=%fused_computation.2 | convolution fusion | flops 3230138368 | bytes 9971712 | tf_op jit(solution)/shard_map/td,cte->cde/dot_general | solution.py:865
  513.4 5.3 slice_bitcast_fusion
  518.7 1.6 collective-permute-start.3
  520.3 1.5 collective-permute-start.4
  522.2 2.6 copy.282
  525.1 2.9 broadcast_in_dim.53
  529.2 24.3 %collective-permute-done.3 = bf16[256,2816]{1,0:T(8,128)(2,1)} collective-permute-done((bf16[256,2816]{1,0:T(8,128)(2,1)}, bf16[256,2816]{1,0:T(8,128)(2,1)}, u32[]{:S(2)}, u32[]{:S(2)}) %collective-permute-start.3) | collective-permute-done | bytes 1441824 | tf_op jit(solution)/shard_map/ppermute | solution.py:625
  553.5 2.6 copy.283
  556.1 28.4 %collective-permute-done.4 = bf16[256,2816]{1,0:T(8,128)(2,1)} collective-permute-done((bf16[256,2816]{1,0:T(8,128)(2,1)}, bf16[256,2816]{1,0:T(8,128)(2,1)}, u32[]{:S(2)}, u32[]{:S(2)}) %collective-permute-start.4) | collective-permute-done | bytes 1441824 | tf_op jit(solution)/shard_map/ppermute | solution.py:625
  584.5 2.5 copy.284
  587.0 2.7 copy.285
  589.7 2.7 constant_dynamic-update-slice_fusion.2
  594.8 8.7 %convert_bitcast_fusion = f32[256,2,4,11,128]{0,4,1,3,2:T(8,128)} fusion(bf16[4,256,11,2,128]{1,4,3,2,0:T(8,128)(2,1)} %bitcast.56), kind=kLoop, calls=%fused_computation.1 | loop fusion | flops 2883584 | bytes 17301504 | tf_op jit(solution)/shard_map/convert_element_type | solution.py:650
  603.6 10.2 %copy.286 = f32[256,2,4,11,128]{0,4,3,2,1:T(8,128)} copy(f32[256,2,4,11,128]{0,4,1,3,2:T(8,128)} %convert_bitcast_fusion) | data formatting | bytes 23068672 | tf_op jit(solution)/shard_map/convert_element_type | solution.py:650
  613.8 11.9 %copy.288 = f32[1,256,11264]{2,1,0:T(8,128)} copy(f32[1,256,11264]{1,2,0:T(8,128)} %bitcast.110) | data formatting | bytes 23068672
  625.7 3.4 fusion.3
  629.2 38.7 %psum.7 = f32[6,2048]{1,0:T(8,128)S(1)} all-reduce(f32[6,2048]{1,0:T(8,128)S(1)} %pad_maximum_fusion.11), channel_id=1, replica_groups=mesh['dp'=8,'expert'=4] {'dp','expert'}, use_global_device_ids=true, to_apply=%region_22.23 | all-reduce | flops 12288 | bytes 98304 | tf_op jit(solution)/shard_map/psum | solution.py:879
  669.2 1.8 convert_element_type.222
  670.9 1.4 fusion.23
  672.3 2.6 fusion.27
  674.9 2.6 copy.287
  677.5 5.9 copy.312
  (218 shorter events, 30.8 us)
Async XLA Ops:
  7.2 4.6 copy-start.59
  7.2 4.6 copy-start.60
  7.2 4.6 copy-start.57
  7.2 51.1 %all-gather.5.cloned.1.call-start = ((), (), s32[]{:S(2)}) async-start(), calls=%async_computation.4 | async-start | bytes 2621440 | tf_op jit(solution)/shard_map/all_gather | solution.py:727
  7.9 98.2 %all-gather.7.cloned.1.call-start = ((), (), s32[]{:S(2)}) async-start(), calls=%async_computation.5 | async-start | bytes 7077888 | tf_op jit(solution)/shard_map/all_gather | solution.py:732
  10.3 126.0 %all-gather.9.cloned.1.call-start = ((), (), s32[]{:S(2)}) async-start(), calls=%async_computation.6 | async-start | bytes 2359296 | tf_op jit(solution)/shard_map/all_gather | solution.py:733
  11.0 173.5 %reduce-scatter.5.cloned.1.call-start = ((), (), s32[]{:S(2)}) async-start(), calls=%async_computation.7 | async-start | bytes 2621440 | tf_op jit(solution)/shard_map/reduce_scatter | solution.py:775
  22.4 164.7 %copy-start.31 = (bf16[2048,6]{0,1:T(8,128)(2,1)}, bf16[2048,6]{0,1:T(8,128)(2,1)S(1)}, u32[]{:S(2)}) copy-start(bf16[2048,6]{0,1:T(8,128)(2,1)S(1)} %all_gather.16) | copy-start | bytes 73732
  22.4 90.2 %copy-start.37 = (f32[2048,1]{0,1:T(1,128)}, f32[2048,1]{0,1:T(1,128)S(1)}, u32[]{:S(2)}) copy-start(f32[2048,1]{0,1:T(1,128)S(1)} %get-tuple-element.110) | copy-start | bytes 24580
  22.4 163.4 %copy-start.33 = (f32[2048,1]{0,1:T(1,128)}, f32[2048,1]{0,1:T(1,128)S(1)}, u32[]{:S(2)}) copy-start(f32[2048,1]{0,1:T(1,128)S(1)} %get-tuple-element.109) | copy-start | bytes 24580
  24.1 97.0 %copy-start.21 = (f32[512,64]{1,0:T(8,128)}, f32[512,64]{1,0:T(8,128)S(1)}, u32[]{:S(2)}) copy-start(f32[512,64]{1,0:T(8,128)S(1)} %get-tuple-element.113) | copy-start | bytes 393220
  60.4 52.2 %copy-start.51 = (f32[512]{0:T(512)}, f32[512]{0:T(512)S(1)}, u32[]{:S(2)}) copy-start(f32[512]{0:T(512)S(1)} %add_rsqrt_fusion) | copy-start | bytes 6148
  121.0 1.9 copy-start.26
  124.4 2.1 copy-start
  124.4 2.1 copy-start.35
  124.4 2.1 copy-start.24
  127.4 13.1 %copy-start.61 = (bf16[4,128,512]{2,1,0:T(8,128)(2,1)}, bf16[4,128,512]{2,1,0:T(8,128)(2,1)S(1)}, u32[]{:S(2)}) copy-start(bf16[4,128,512]{2,1,0:T(8,128)(2,1)S(1)} %fusion.18) | copy-start | bytes 1572868
  140.5 328.4 %all-gather.11.cloned.1.call-start = ((), (), s32[]{:S(2)}) async-start(), calls=%async_computation.8 | async-start | bytes 2621440 | tf_op jit(solution)/shard_map/all_gather | solution.py:834
  162.4 7.7 %copy-start.41 = (s32[128,2]{0,1:T(2,128)S(1)}, s32[128,2]{0,1:T(2,128)}, u32[]{:S(2)}) copy-start(s32[128,2]{0,1:T(2,128)} %param.21) | copy-start | bytes 3076
  162.4 8.0 %copy-start.58 = (s32[128]{0:T(128)S(1)}, s32[128]{0:T(128)}, u32[]{:S(2)}) copy-start(s32[128]{0:T(128)} %param.22) | copy-start | bytes 1540
  162.4 34.7 %collective-permute-start = (bf16[256,2816]{1,0:T(8,128)(2,1)}, bf16[256,2816]{1,0:T(8,128)(2,1)}, u32[]{:S(2)}, u32[]{:S(2)}) collective-permute-start(bf16[256,2816]{1,0:T(8,128)(2,1)} %bitcast.123), channel_id=1, source_target_pairs={{0,8},{4,12},{8,0},{12,4},{16,24},{20,28},{24,16},{28,20},{1,9},{5... | collective-permute-start | bytes 4325384 | tf_op jit(solution)/shard_map/ppermute | solution.py:625
  166.5 64.6 %collective-permute-start.1 = (bf16[256,2816]{1,0:T(8,128)(2,1)}, bf16[256,2816]{1,0:T(8,128)(2,1)}, u32[]{:S(2)}, u32[]{:S(2)}) collective-permute-start(bf16[256,2816]{1,0:T(8,128)(2,1)} %bitcast.124), channel_id=1, source_target_pairs={{0,16},{4,20},{8,24},{12,28},{16,0},{20,4},{24,8},{28,12},{1,17},{... | collective-permute-start | bytes 4325384 | tf_op jit(solution)/shard_map/ppermute | solution.py:625
  167.1 17.4 %copy-start.3 = (bf16[128,2048]{1,0:T(8,128)(2,1)S(1)}, bf16[128,2048]{1,0:T(8,128)(2,1)}, u32[]{:S(2)}) copy-start(bf16[128,2048]{1,0:T(8,128)(2,1)} %param.12) | copy-start | bytes 1572868
  168.8 62.3 %collective-permute-start.2 = (bf16[256,2816]{1,0:T(8,128)(2,1)}, bf16[256,2816]{1,0:T(8,128)(2,1)}, u32[]{:S(2)}, u32[]{:S(2)}) collective-permute-start(bf16[256,2816]{1,0:T(8,128)(2,1)} %bitcast.125), channel_id=1, source_target_pairs={{0,24},{4,28},{8,16},{12,20},{16,8},{20,12},{24,0},{28,4},{1,25},{... | collective-permute-start | bytes 4325384 | tf_op jit(solution)/shard_map/ppermute | solution.py:625
  170.7 21.4 %copy-start.45 = (f32[128]{0:T(128)}, f32[128]{0:T(128)S(1)}, u32[]{:S(2)}) copy-start(f32[128]{0:T(128)S(1)} %get-tuple-element.76) | copy-start | bytes 1540
  173.8 16.3 %copy-start.27 = (bf16[256,128]{1,0:T(8,128)(2,1)}, bf16[256,128]{1,0:T(8,128)(2,1)S(1)}, u32[]{:S(2)}) copy-start(bf16[256,128]{1,0:T(8,128)(2,1)S(1)} %convert_reduce_fusion) | copy-start | bytes 196612
  173.8 18.2 %copy-start.30 = (pred[256,128,2]{1,0,2:T(32,128)(4,1)}, pred[256,128,2]{1,0,2:T(32,128)(4,1)S(1)}, u32[]{:S(2)}) copy-start(pred[256,128,2]{1,0,2:T(32,128)(4,1)S(1)} %fusion.39) | copy-start | bytes 196612
  185.8 3.9 copy-start.49
  187.1 3.0 copy-start.8
  187.3 4.2 copy-start.6
  190.0 3.6 copy-start.43
  190.0 3.6 copy-start.47
  190.0 3.6 copy-start.53
  190.1 3.5 copy-start.55
  190.1 3.5 copy-start.56
  407.1 5.2 copy-start.44
  407.1 5.2 copy-start.48
  407.1 5.2 copy-start.54
  407.1 5.3 copy-start.42
  407.1 5.3 copy-start.32
  408.8 4.3 copy-start.4
  408.8 4.3 copy-start.5
  408.8 4.3 copy-start.25
  408.8 4.3 copy-start.28
  408.8 4.3 copy-start.34
  408.9 4.3 copy-start.50
  412.3 1.5 copy-start.46
  413.1 2.0 copy-start.36
  413.1 2.0 copy-start.40
  415.1 254.1 %reduce-scatter.11.cloned.1.call-start = ((), (), s32[]{:S(2)}) async-start(), calls=%async_computation.11 | async-start | bytes 2359296 | tf_op jit(solution)/shard_map/reduce_scatter | solution.py:837
  473.3 197.6 %reduce-scatter.7.cloned.1.call-start = ((), (), s32[]{:S(2)}) async-start(), calls=%async_computation.9 | async-start | bytes 2621440 | tf_op jit(solution)/shard_map/reduce_scatter | solution.py:862
  473.6 3.7 copy-start.1
  481.0 4.0 copy-start.2
  495.4 9.8 %copy-start.29 = (bf16[1,512,512]{2,1,0:T(8,128)(2,1)S(1)}, bf16[1,512,512]{2,1,0:T(8,128)(2,1)}, u32[]{:S(2)}) copy-start(bf16[1,512,512]{2,1,0:T(8,128)(2,1)} %copy.279) | copy-start | bytes 1572868
  495.4 9.8 %copy-start.38 = (f32[2048,1]{0,1:T(1,128)S(1)}, f32[2048,1]{0,1:T(1,128)}, u32[]{:S(2)}) copy-start(f32[2048,1]{0,1:T(1,128)} %copy-done.37) | copy-start | bytes 24580
  495.4 9.8 %copy-start.52 = (f32[512]{0:T(512)S(1)}, f32[512]{0:T(512)}, u32[]{:S(2)}) copy-start(f32[512]{0:T(512)} %copy-done.51) | copy-start | bytes 6148
  504.8 170.1 %reduce-scatter.9.cloned.1.call-start = ((), (), s32[]{:S(2)}) async-start(), calls=%async_computation.10 | async-start | bytes 7077888 | tf_op jit(solution)/shard_map/reduce_scatter | solution.py:866
  513.4 11.4 %copy-start.9 = (bf16[128,2048]{1,0:T(8,128)(2,1)S(1)}, bf16[128,2048]{1,0:T(8,128)(2,1)}, u32[]{:S(2)}) copy-start(bf16[128,2048]{1,0:T(8,128)(2,1)} %copy-done.8) | copy-start | bytes 1572868
  518.7 34.8 %collective-permute-start.3 = (bf16[256,2816]{1,0:T(8,128)(2,1)}, bf16[256,2816]{1,0:T(8,128)(2,1)}, u32[]{:S(2)}, u32[]{:S(2)}) collective-permute-start(bf16[256,2816]{1,0:T(8,128)(2,1)} %get-tuple-element.82), channel_id=1, source_target_pairs={{0,8},{4,12},{8,0},{12,4},{16,24},{20,28},{24,16},{28,20},{1,9},{5... | collective-permute-start | bytes 4325384 | tf_op jit(solution)/shard_map/ppermute | solution.py:625
  520.3 64.1 %collective-permute-start.4 = (bf16[256,2816]{1,0:T(8,128)(2,1)}, bf16[256,2816]{1,0:T(8,128)(2,1)}, u32[]{:S(2)}, u32[]{:S(2)}) collective-permute-start(bf16[256,2816]{1,0:T(8,128)(2,1)} %get-tuple-element.81), channel_id=1, source_target_pairs={{0,16},{4,20},{8,24},{12,28},{16,0},{20,4},{24,8},{28,12},{1,17},{... | collective-permute-start | bytes 4325384 | tf_op jit(solution)/shard_map/ppermute | solution.py:625
  521.8 65.2 %collective-permute-start.5 = (bf16[256,2816]{1,0:T(8,128)(2,1)}, bf16[256,2816]{1,0:T(8,128)(2,1)}, u32[]{:S(2)}, u32[]{:S(2)}) collective-permute-start(bf16[256,2816]{1,0:T(8,128)(2,1)} %get-tuple-element.80), channel_id=1, source_target_pairs={{0,24},{4,28},{8,16},{12,20},{16,8},{20,12},{24,0},{28,4},{1,25},{... | collective-permute-start | bytes 4325384 | tf_op jit(solution)/shard_map/ppermute | solution.py:625
  524.8 3.2 copy-start.11
  589.7 2.7 copy-start.10
  589.7 3.9 copy-start.12
  (12 other events, 15.4 us)
Sparse Core Ops, SparseCore 0:
  9.6 48.6 all-gather.4
  60.7 45.3 all-gather.6
  108.0 28.1 all-gather.8
  140.6 43.8 reduce-scatter.4
  415.2 53.6 all-gather.10
  473.4 39.9 reduce-scatter.10
  515.7 43.8 reduce-scatter.6
  563.4 61.0 reduce-scatter.8

commit v3 on v2

--- a/solution.py
+++ b/solution.py
@@ -242,18 +242,31 @@
     def forward(k):
         base = k * chunk
 
-        def tile(j, carry):
-            cols = pl.ds(pl.multiple_of(j * 2 * LANES, 2 * LANES), 2 * LANES)
-            both = dot_nn(rows_buf[0, base : base + chunk, :], w_buf[:, cols])
-            gate = both[:, :LANES]
+        def tile(first, count):
+            gate_cols = pl.ds(pl.multiple_of(first * LANES, LANES), count * LANES)
+            up_cols = pl.ds(pl.multiple_of(hidden + first * LANES, LANES), count * LANES)
+            rows = rows_buf[0, base : base + chunk, :]
+            if count == 1:
+                weights = jnp.concatenate([w_buf[:, gate_cols], w_buf[:, up_cols]], axis=1)
+                both = dot_nn(rows, weights)
+                gate = both[:, :LANES]
+                up = both[:, LANES:]
+            else:
+                gate = dot_nn(rows, w_buf[:, gate_cols])
+                up = dot_nn(rows, w_buf[:, up_cols])
             sigmoid = 1.0 / (1.0 + jnp.exp(-gate))
-            act = gate * sigmoid * both[:, LANES:]
-            gate_buf[base : base + chunk, cols] = both.astype(jnp.bfloat16)
-            narrow = pl.ds(pl.multiple_of(j * LANES, LANES), LANES)
-            act_buf[base : base + chunk, narrow] = act.astype(jnp.bfloat16)
+            gate_buf[base : base + chunk, gate_cols] = gate.astype(jnp.bfloat16)
+            gate_buf[base : base + chunk, up_cols] = up.astype(jnp.bfloat16)
+            act_buf[base : base + chunk, gate_cols] = (gate * sigmoid * up).astype(jnp.bfloat16)
+
+        def pair(j, carry):
+            tile(2 * j, 2)
             return carry
 
-        lax.fori_loop(0, hidden // LANES, tile, 0)
+        blocks = hidden // LANES
+        lax.fori_loop(0, blocks // 2, pair, 0)
+        if blocks % 2:
+            tile(blocks - 1, 1)
 
         def out_tile(j, carry):
             cols = pl.ds(pl.multiple_of(j * 2 * LANES, 2 * LANES), 2 * LANES)
@@ -269,18 +282,14 @@
         def tile(first, count):
             rows = pl.ds(pl.multiple_of(first * LANES, LANES), count * LANES)
             d_act = dot_nt(rows_buf[1, base : base + chunk, :], down_buf[rows, :])
-            for i in range(count):
-                cols = pl.ds(pl.multiple_of((first + i) * 2 * LANES, 2 * LANES), 2 * LANES)
-                both = gate_buf[base : base + chunk, cols].astype(jnp.float32)
-                gate = both[:, :LANES]
-                up = both[:, LANES:]
-                sigmoid = 1.0 / (1.0 + jnp.exp(-gate))
-                scaled = d_act[:, i * LANES : (i + 1) * LANES] * sigmoid
-                d_gate = scaled * up * (1.0 + gate * (1.0 - sigmoid))
-                d_up = scaled * gate
-                gate_buf[base : base + chunk, cols] = jnp.concatenate(
-                    [d_gate, d_up], axis=1
-                ).astype(jnp.bfloat16)
+            up_rows = pl.ds(pl.multiple_of(hidden + first * LANES, LANES), count * LANES)
+            gate = gate_buf[base : base + chunk, rows].astype(jnp.float32)
+            up = gate_buf[base : base + chunk, up_rows].astype(jnp.float32)
+            sigmoid = 1.0 / (1.0 + jnp.exp(-gate))
+            scaled = d_act * sigmoid
+            d_gate = scaled * up * (1.0 + gate * (1.0 - sigmoid))
+            gate_buf[base : base + chunk, rows] = d_gate.astype(jnp.bfloat16)
+            gate_buf[base : base + chunk, up_rows] = (scaled * gate).astype(jnp.bfloat16)
 
         def pair(j, carry):
             tile(2 * j, 2)
@@ -613,6 +622,608 @@
     return lax.all_to_all(blocks, "expert", split_axis=0, concat_axis=0, tiled=True)
 
 
+def line_order(place, step):
+    upper = place // 2
+    low = place * (1 - upper) + (3 - place) * upper
+    first = 1 - (step + 1) // 2
+    block = step + first * (1 - low) + (1 - first)
+    return block * (1 - upper) + (3 - block) * upper
+
+
+def rotated(grad, cosine, sine):
+    return grad * cosine + pltpu.roll(grad, grad.shape[1] // 2, 1) * sine
+
+
+def attention_back_kernel(
+    heads,
+    length,
+    d_attn,
+    tokens_all,
+    inverse_all,
+    whole,
+    w_out,
+    w_qkv,
+    query,
+    key_rows,
+    value,
+    attended,
+    log_total,
+    cosine,
+    sine,
+    small_part,
+    gate_grads,
+    grad_normed,
+    grad_weights,
+    small_out,
+    gate_got,
+    da_buf,
+    tokens_buf,
+    inverse_buf,
+    whole_buf,
+    w_out_buf,
+    w_qkv_buf,
+    query_buf,
+    key_buf,
+    value_buf,
+    attended_buf,
+    log_buf,
+    cosine_buf,
+    sine_buf,
+    d_key_acc,
+    d_value_acc,
+    d_proj,
+    normed_part,
+    from_left,
+    from_right,
+    send_pair,
+    recv_pair,
+    own_part,
+    half_x,
+    half_y,
+    full_x,
+    full_y,
+    small_buf,
+    small_recv,
+    small_z,
+    keep_buf,
+    load_sems,
+    line_sems,
+    sum_sems,
+    pair_sems,
+    ring_sems,
+    small_sems,
+    gate_sems,
+):
+    tok, width = d_attn.shape
+    seq_len = tokens_all.shape[0]
+    group = seq_len // tok
+    local_width = w_out.shape[0]
+    head_size = local_width // heads
+    piece = own_part.shape[1]
+    half = piece // 2
+    scale = head_size**-0.5
+
+    index = lax.axis_index("dp")
+    place = lax.axis_index("expert")
+    core = index % 2
+    at_x = (index // 2) % 2
+    at_y = index // 4
+    partner = {"dp": at_y * 4 + at_x * 2 + (1 - core)}
+    along_x = {"dp": at_y * 4 + (1 - at_x) * 2 + core}
+    along_y = {"dp": (1 - at_y) * 4 + at_x * 2 + core}
+    over = {"dp": (1 - at_y) * 4 + (1 - at_x) * 2 + core}
+    parts = width // piece
+
+    def chip(r):
+        step_y = r // 2
+        step_x = r % 2
+        return (at_y + step_y - 2 * at_y * step_y) * 2 + (at_x + step_x - 2 * at_x * step_x)
+
+    def ring_peer(k):
+        return {"dp": (index + k) % parts}
+
+    def line_peer(k):
+        return {"expert": (place + k) % group}
+
+    right = {"expert": (place + 1) % group}
+    left = {"expert": (place + group - 1) % group}
+
+    loads = [
+        pltpu.make_async_copy(source, target, load_sems.at[number])
+        for number, (source, target) in enumerate(
+            [
+                (w_out, w_out_buf),
+                (query, query_buf),
+                (key_rows, key_buf),
+                (value, value_buf),
+                (log_total, log_buf),
+                (cosine, cosine_buf),
+                (sine, sine_buf),
+                (w_qkv, w_qkv_buf),
+                (tokens_all, tokens_buf),
+                (inverse_all, inverse_buf),
+                (whole, whole_buf),
+                (attended, attended_buf),
+                (small_part, small_buf),
+                (gate_grads.at[0], keep_buf),
+            ]
+        )
+    ]
+    early = 7
+    for load in loads[:early]:
+        load.start()
+
+    greet([ring_peer(k) for k in range(1, parts)] + [line_peer(k) for k in range(1, group)])
+
+    def rows_of(block):
+        return pl.ds(pl.multiple_of(block * tok, tok), tok)
+
+    own_load = pltpu.make_async_copy(d_attn, da_buf.at[rows_of(place)], load_sems.at[14])
+    own_load.start()
+
+    def own_right():
+        return remote(
+            d_attn, da_buf.at[rows_of(place)], line_sems.at[0, place], line_sems.at[2, place], right
+        )
+
+    def own_left():
+        return remote(
+            d_attn, da_buf.at[rows_of(place)], line_sems.at[1, place], line_sems.at[2, place], left
+        )
+
+    def pass_right(block):
+        spot = da_buf.at[rows_of(block)]
+        return remote(spot, spot, line_sems.at[0, block], line_sems.at[2, block], right)
+
+    def pass_left(block):
+        spot = da_buf.at[rows_of(block)]
+        return remote(spot, spot, line_sems.at[1, block], line_sems.at[2, block], left)
+
+    @pl.when(place < group - 1)
+    def _():
+        own_right().start()
+
+    @pl.when(place > 0)
+    def _():
+        own_left().start()
+
+    def gate_copy(r, peer):
+        return remote(
+            gate_grads.at[r], gate_got.at[r], gate_sems.at[0, r], gate_sems.at[1, r], peer
+        )
+
+    peers = (None, along_x, along_y, over)
+    for r in (3, 1, 2):
+        gate_copy(r, peers[r]).start()
+    for load in loads[early:]:
+        load.start()
+    d_key_acc[...] = jnp.zeros_like(d_key_acc)
+    d_value_acc[...] = jnp.zeros_like(d_value_acc)
+
+    def attend_back(block):
+        rows = rows_of(block)
+        d_heads = dot_nt(da_buf[rows, :], w_out_buf[...]).astype(jnp.bfloat16)
+        shape = (tok, seq_len)
+        at_query = block * tok + lax.broadcasted_iota(jnp.int32, shape, 0)
+        at_key = lax.broadcasted_iota(jnp.int32, shape, 1)
+        allowed = (at_key <= at_query) & (at_key < length[0])
+        for head in range(heads):
+            cols = slice(head * head_size, (head + 1) * head_size)
+            one_query = query_buf[rows, cols]
+            one_key = key_buf[:, cols]
+            d_head = d_heads[:, cols]
+            scores = jnp.where(allowed, dot_nt(one_query, one_key) * scale, NEGATIVE)
+            probs = jnp.exp(scores - log_buf[rows, head : head + 1])
+            d_probs = dot_nt(d_head, value_buf[:, cols])
+            delta = jnp.sum(probs * d_probs, axis=-1, keepdims=True)
+            d_scores = (probs * (d_probs - delta)).astype(jnp.bfloat16)
+            d_query = dot_nn(d_scores, one_key) * scale
+            d_key_acc[:, cols] += dot_nn(d_scores.T, one_query) * scale
+            d_value_acc[:, cols] += dot_nn(probs.astype(jnp.bfloat16).T, d_head)
+            d_proj[rows, cols] = rotated(d_query, cosine_buf[rows, :], sine_buf[rows, :]).astype(
+                jnp.bfloat16
+            )
+
+    for load in loads[:early]:
+        load.wait()
+    own_load.wait()
+    attend_back(place)
+
+    def arrive(step, carry):
+        block = line_order(place, step)
+        pass_right(block).wait_recv()
+
+        @pl.when((block < place) & (place < group - 1))
+        def _():
+            pass_right(block).start()
+
+        @pl.when((block > place) & (place > 0))
+        def _():
+            pass_left(block).start()
+
+        attend_back(block)
+        return carry
+
+    lax.fori_loop(0, group - 1, arrive, 0)
+    for load in loads[early:]:
+        load.wait()
+    keep = pltpu.make_async_copy(keep_buf, gate_got.at[0], load_sems.at[15])
+    keep.start()
+
+    for head in range(heads):
+        cols = slice(head * head_size, (head + 1) * head_size)
+        key_cols = slice(local_width + head * head_size, local_width + (head + 1) * head_size)
+        d_proj[:, key_cols] = rotated(d_key_acc[:, cols], cosine_buf[...], sine_buf[...]).astype(
+            jnp.bfloat16
+        )
+    d_proj[:, 2 * local_width :] = d_value_acc[...].astype(jnp.bfloat16)
+
+    def normed_tile(j, carry):
+        cols = pl.ds(pl.multiple_of(j * piece, piece), piece)
+        d_normed = jnp.zeros((seq_len, piece), jnp.float32)
+        for c in range(3):
+            d_normed += dot_nt(
+                d_proj[:, c * local_width : (c + 1) * local_width], w_qkv_buf[c, cols, :]
+            )
+        hat = tokens_buf[:, cols].astype(jnp.float32) * inverse_buf[...]
+        small_buf[0:1, cols] = jnp.sum(d_normed * hat, axis=0, keepdims=True)
+        normed_part[:, cols] = d_normed.astype(jnp.bfloat16)
+        return carry
+
+    lax.fori_loop(0, parts, normed_tile, 0)
+
+    def go_right(block):
+        return remote(
+            normed_part.at[pl.ds(block * tok, tok)],
+            from_left.at[block],
+            sum_sems.at[0, block],
+            sum_sems.at[1, block],
+            right,
+        )
+
+    def go_left(block):
+        return remote(
+            normed_part.at[pl.ds(block * tok, tok)],
+            from_right.at[block],
+            sum_sems.at[0, block],
+            sum_sems.at[2, block],
+            left,
+        )
+
+    def add_into(target, other):
+        value = target[...].astype(jnp.float32) + other[...].astype(jnp.float32)
+        target[...] = value.astype(jnp.bfloat16)
+
+    def on_right(block):
+        go_right(block).wait_recv()
+        add_into(normed_part.at[pl.ds(block * tok, tok)], from_left.at[block])
+        go_right(block).start()
+
+    def on_left(block):
+        go_left(block).wait_recv()
+        add_into(normed_part.at[pl.ds(block * tok, tok)], from_right.at[block])
+        go_left(block).start()
+
+    @pl.when(place == 0)
+    def _():
+        for block in (3, 2, 1):
+            go_right(block).start()
+
+    @pl.when(place == 3)
+    def _():
+        for block in (0, 1, 2):
+            go_left(block).start()
+
+    def small_copy(k):
+        to = (index + k) % parts
+        cols = pl.ds(pl.multiple_of(to * piece, piece), piece)
+        return remote(
+            small_buf.at[:, cols],
+            small_recv.at[k],
+            small_sems.at[0, k],
+            small_sems.at[1, k],
+            ring_peer(k),
+        )
+
+    for k in range(1, parts):
+        small_copy(k).start()
+
+    def weight_grad(which, r):
+        cols = pl.ds(pl.multiple_of((chip(r) * 2 + which) * piece, piece), piece)
+        left_side = whole_buf[:, cols].T
+        first = dot_nn(left_side, d_proj[...])
+        second = dot_nn(da_buf[:, cols].T, attended_buf[...])
+        return jnp.concatenate([first, second], axis=1)
+
+    def pair_copy(r):
+        return remote(
+            send_pair.at[r], recv_pair.at[r], pair_sems.at[0, r], pair_sems.at[1, r], partner
+        )
+
+    def for_partner(i, carry):
+        r = 3 - i
+        send_pair[r] = weight_grad(1 - core, r).astype(jnp.bfloat16)
+        pair_copy(r).start()
+        return carry
+
+    lax.fori_loop(0, 4, for_partner, 0)
+
+    @pl.when(place == 1)
+    def _():
+        on_right(3)
+
+    @pl.when(place == 2)
+    def _():
+        on_left(0)
+
+    def half_x_copy():
+        return remote(
+            own_part.at[3, pl.ds(0, half)], half_x, ring_sems.at[0, 0], ring_sems.at[1, 0], along_x
+        )
+
+    def half_y_copy():
+        return remote(
+            own_part.at[3, pl.ds(half, half)],
+            half_y,
+            ring_sems.at[0, 1],
+            ring_sems.at[1, 1],
+            along_y,
+        )
+
+    def full_x_copy():
+        return remote(own_part.at[1], full_x, ring_sems.at[0, 2], ring_sems.at[1, 2], along_x)
+
+    def full_y_copy():
+        return remote(own_part.at[2], full_y, ring_sems.at[0, 3], ring_sems.at[1, 3], along_y)
+
+    def for_self(i, carry):
+        r = 3 - i
+        pair_copy(r).wait_recv()
+        own_part[r] = (weight_grad(core, r) + recv_pair[r].astype(jnp.float32)).astype(
+            jnp.bfloat16
+        )
+
+        @pl.when(i == 0)
+        def _():
+            half_x_copy().start()
+            half_y_copy().start()
+
+        return carry
+
+    lax.fori_loop(0, 4, for_self, 0)
+
+    total = small_buf[:, pl.ds(pl.multiple_of(index * piece, piece), piece)]
+    for k in range(1, parts):
+        small_copy(k).wait_recv()
+        total = total + small_recv[k]
+    small_z[0] = total
+
+    @pl.when(place == 1)
+    def _():
+        on_right(2)
+
+    @pl.when(place == 2)
+    def _():
+        on_left(1)
+
+    def small_line_copy(k):
+        return remote(
+            small_z.at[0],
+            small_z.at[k],
+            small_sems.at[0, parts + k],
+            small_sems.at[1, parts + k],
+            line_peer(k),
+        )
+
+    for k in range(1, group):
+        small_line_copy(k).start()
+
+    half_x_copy().wait_recv()
+    add_into(own_part.at[2, pl.ds(0, half)], half_x)
+    full_y_copy().start()
+    half_y_copy().wait_recv()
+    add_into(own_part.at[1, pl.ds(half, half)], half_y)
+    full_x_copy().start()
+
+    @pl.when(place == 1)
+    def _():
+        on_left(0)
+
+    @pl.when(place == 2)
+    def _():
+        on_right(3)
+
+    total = small_z[0]
+    for k in range(1, group):
+        small_line_copy(k).wait_recv()
+        total = total + small_z[k]
+    small_out[...] = total
+
+    grad_normed[...] = normed_part[rows_of(place), :].astype(jnp.float32)
+
+    @pl.when(place > 0)
+    def _():
+        go_right(place).wait_recv()
+        grad_normed[...] += from_left[place].astype(jnp.float32)
+
+    @pl.when(place < group - 1)
+    def _():
+        go_left(place).wait_recv()
+        grad_normed[...] += from_right[place].astype(jnp.float32)
+
+    full_x_copy().wait_recv()
+    full_y_copy().wait_recv()
+    grad_weights[...] = (
+        own_part[0].astype(jnp.float32)
+        + full_x[...].astype(jnp.float32)
+        + full_y[...].astype(jnp.float32)
+    )
+
+    for r in (1, 2, 3):
+        gate_copy(r, peers[r]).wait()
+    keep.wait()
+    half_x_copy().wait_send()
+    half_y_copy().wait_send()
+    full_x_copy().wait_send()
+    full_y_copy().wait_send()
+    for r in range(4):
+        pair_copy(r).wait_send()
+    for k in range(1, parts):
+        small_copy(k).wait_send()
+    for k in range(1, group):
+        small_line_copy(k).wait_send()
+    for block in range(group):
+
+        @pl.when(block > place)
+        def _():
+            go_right(block).wait_send()
+
+        @pl.when(block < place)
+        def _():
+            go_left(block).wait_send()
+
+        @pl.when((block <= place) & (place < group - 1))
+        def _():
+            pass_right(block).wait_send()
+
+        @pl.when((block >= place) & (place > 0))
+        def _():
+            pass_left(block).wait_send()
+
+
+def attention_back_call(
+    lengths,
+    d_attn,
+    tokens_all,
+    inverse_all,
+    whole,
+    w_out,
+    w_qkv,
+    query,
+    key_rows,
+    value,
+    attended,
+    log_total,
+    cosine,
+    sine,
+    small_part,
+    gate_grads,
+):
+    tok, width = d_attn.shape
+    seq_len = tokens_all.shape[0]
+    group = seq_len // tok
+    local_width = w_out.shape[0]
+    heads = log_total.shape[1]
+    piece = gate_grads.shape[1]
+    half = piece // 2
+    parts = width // piece
+    small_rows = small_part.shape[0]
+    low, full = jnp.bfloat16, jnp.float32
+    anywhere = pl.BlockSpec(memory_space=pl.ANY)
+    inside = pl.BlockSpec(memory_space=pltpu.VMEM)
+
+    def like(array):
+        return pltpu.VMEM(array.shape, array.dtype)
+
+    flops = 2 * seq_len * width * local_width * 8 + 10 * seq_len * seq_len * local_width
+    return pl.pallas_call(
+        functools.partial(attention_back_kernel, heads),
+        out_shape=(
+            jax.ShapeDtypeStruct((tok, width), full),
+            jax.ShapeDtypeStruct((piece, 4 * local_width), full),
+            jax.ShapeDtypeStruct((small_rows, piece), full),
+            jax.ShapeDtypeStruct(gate_grads.shape, low),
+        ),
+        in_specs=[pl.BlockSpec(memory_space=pltpu.SMEM)] + [anywhere] * 15,
+        out_specs=(inside, inside, inside, anywhere),
+        scratch_shapes=[
+            pltpu.VMEM((seq_len, width), low),
+            like(tokens_all),
+            like(inverse_all),
+            like(whole),
+            like(w_out),
+            like(w_qkv),
+            like(query),
+            like(key_rows),
+            like(value),
+            like(attended),
+            like(log_total),
+            like(cosine),
+            like(sine),
+            pltpu.VMEM((seq_len, local_width), full),
+            pltpu.VMEM((seq_len, local_width), full),
+            pltpu.VMEM((seq_len, 3 * local_width), low),
+            pltpu.VMEM((seq_len, width), low),
+            pltpu.VMEM((group, tok, width), low),
+            pltpu.VMEM((group, tok, width), low),
+            pltpu.VMEM((4, piece, 4 * local_width), low),
+            pltpu.VMEM((4, piece, 4 * local_width), low),
+            pltpu.VMEM((4, piece, 4 * local_width), low),
+            pltpu.VMEM((half, 4 * local_width), low),
+            pltpu.VMEM((half, 4 * local_width), low),
+            pltpu.VMEM((piece, 4 * local_width), low),
+            pltpu.VMEM((piece, 4 * local_width), low),
+            like(small_part),
+            pltpu.VMEM((parts, small_rows, piece), full),
+            pltpu.VMEM((group, small_rows, piece), full),
+            pltpu.VMEM(gate_grads.shape[1:], low),
+            pltpu.SemaphoreType.DMA((16,)),
+            pltpu.SemaphoreType.DMA((3, group)),
+            pltpu.SemaphoreType.DMA((3, group)),
+            pltpu.SemaphoreType.DMA((2, 4)),
+            pltpu.SemaphoreType.DMA((2, 4)),
+            pltpu.SemaphoreType.DMA((2, parts + group)),
+            pltpu.SemaphoreType.DMA((2, 4)),
+        ],
+        compiler_params=pltpu.CompilerParams(
+            collective_id=2, has_side_effects=True, vmem_limit_bytes=67043328
+        ),
+        cost_estimate=pl.CostEstimate(flops=flops, bytes_accessed=40000000, transcendentals=0),
+        name="attention_back",
+    )(
+        lengths,
+        d_attn,
+        tokens_all,
+        inverse_all,
+        whole,
+        w_out,
+        w_qkv,
+        query,
+        key_rows,
+        value,
+        attended,
+        log_total,
+        cosine,
+        sine,
+        small_part,
+        gate_grads,
+    )
+
+
+def widen_slices(grads):
+    chips, rows, hidden2 = grads.shape
+    own = (lax.axis_index("dp") // 2).astype(jnp.int32).reshape(1)
+    size = hidden2 // 2
+
+    def body(own_ref, source, target):
+        target[...] = source[0].astype(jnp.float32)
+
+    wide = pl.pallas_call(
+        body,
+        out_shape=jax.ShapeDtypeStruct((rows, chips * hidden2), jnp.float32),
+        grid_spec=pltpu.PrefetchScalarGridSpec(
+            num_scalar_prefetch=1,
+            grid=(2, chips),
+            in_specs=[
+                pl.BlockSpec((1, rows, size), lambda part, at, own_ref: (at ^ own_ref[0], 0, part))
+            ],
+            out_specs=pl.BlockSpec((rows, size), lambda part, at, own_ref: (0, part * chips + at)),
+        ),
+        name="widen",
+    )(own, grads)
+    return wide[None]
+
+
 def across(index, step):
     return ((index // 2) ^ step) * 2 + index % 2
 
@@ -629,25 +1240,15 @@
 def chip_slices(w_gate_up):
     rows, ff2 = w_gate_up.shape[1:]
     chips = lax.axis_size("dp") // 2
-    blocks = ff2 // 2 // chips // LANES
+    size = ff2 // 2 // chips
     own = lax.axis_index("dp") // 2
-    slices = w_gate_up[0].reshape(rows, 2, chips, blocks, LANES).transpose(2, 0, 3, 1, 4)
-    slices = slices.reshape(chips, rows, ff2 // chips)
-    return swap_chips(
-        [lax.dynamic_index_in_dim(slices, own ^ step, 0, keepdims=False) for step in range(chips)]
-    )
-
-
-def chip_slices_back(grads):
-    chips, rows, hidden2 = grads.shape
-    own = lax.axis_index("dp") // 2
-    got = swap_chips([grads[step] for step in range(chips)])
-    whole = jnp.zeros((chips, rows, hidden2), jnp.bfloat16)
-    for step in range(chips):
-        whole = lax.dynamic_update_index_in_dim(whole, got[step], own ^ step, 0)
-    blocks = hidden2 // 2 // LANES
-    whole = whole.reshape(chips, rows, blocks, 2, LANES).transpose(1, 3, 0, 2, 4)
-    return whole.reshape(1, rows, chips * hidden2).astype(jnp.float32)
+
+    def of_chip(chip):
+        gate = lax.dynamic_slice(w_gate_up[0], (0, chip * size), (rows, size))
+        up = lax.dynamic_slice(w_gate_up[0], (0, ff2 // 2 + chip * size), (rows, size))
+        return jnp.concatenate([gate, up], axis=1)
+
+    return swap_chips([of_chip(own ^ step) for step in range(chips)])
 
 
 def expert_step(gate_up_w, down_w, rows, d_rows_out):
@@ -672,7 +1273,7 @@
     out, d_rows, grad_gate_up, grad_down = experts_call(
         rows, d_rows_out, chip_slices(w_gate_up), w_down[0]
     )
-    return out, d_rows, chip_slices_back(grad_gate_up), grad_down[None]
+    return out, d_rows, grad_gate_up, grad_down[None]
 
 
 def experts_gather_weights(w_gate_up, w_down, rows, d_rows_out):
@@ -697,6 +1298,64 @@
         grad_gate_up.astype(jnp.float32)[None],
         grad_down.astype(jnp.float32)[None],
     )
+
+
+def attention_back_plain(
+    lengths,
+    d_attn,
+    hat_all,
+    whole,
+    out_full,
+    qkv_full,
+    query,
+    key_rows,
+    value,
+    attended,
+    log_total,
+    cosine,
+    sine,
+):
+    seq_len, heads_local, head_size = query.shape
+    local_width = heads_local * head_size
+    position = jnp.arange(seq_len, dtype=jnp.int32)
+    allowed = (position[None, :] <= position[:, None]) & (position < lengths[0])[None, :]
+    whole_grad = lax.all_gather(d_attn, "expert", axis=0, tiled=True)
+    d_attended = contract_last(whole_grad, out_full).astype(jnp.bfloat16)
+    out_part = contract_first(attended, whole_grad)
+    grad_out = lax.psum_scatter(
+        out_part.astype(jnp.bfloat16), "dp", scatter_dimension=1, tiled=True
+    ).astype(jnp.float32)
+    d_heads = d_attended.reshape(seq_len, heads_local, head_size)
+    probs = jnp.exp(masked_scores(query, key_rows, allowed) - log_total)
+    probs_low = probs.astype(jnp.bfloat16)
+    d_value = jnp.einsum(
+        "hqk,qhd->khd", probs_low, d_heads, preferred_element_type=jnp.float32
+    ).astype(jnp.bfloat16)
+    d_probs = jnp.einsum("qhd,khd->hqk", d_heads, value, preferred_element_type=jnp.float32)
+    row_delta = jnp.sum(probs * d_probs, axis=-1, keepdims=True)
+    d_scores = (probs * (d_probs - row_delta)).astype(jnp.bfloat16)
+    scale = head_size ** (-0.5)
+    d_query = (
+        jnp.einsum("hqk,khd->qhd", d_scores, key_rows, preferred_element_type=jnp.float32) * scale
+    )
+    d_key = jnp.einsum("hqk,qhd->khd", d_scores, query, preferred_element_type=jnp.float32) * scale
+    d_query_pre = (
+        rotate_back(d_query, cosine, sine).reshape(seq_len, local_width).astype(jnp.bfloat16)
+    )
+    d_key_pre = rotate_back(d_key, cosine, sine).reshape(seq_len, local_width).astype(jnp.bfloat16)
+    d_projected = jnp.stack([d_query_pre, d_key_pre, d_value.reshape(seq_len, local_width)])
+    d_normed_part = jnp.einsum(
+        "cte,cde->td", d_projected, qkv_full, preferred_element_type=jnp.float32
+    )
+    grad_normalized = lax.psum_scatter(
+        d_normed_part.astype(jnp.bfloat16), "expert", scatter_dimension=0, tiled=True
+    ).astype(jnp.float32)
+    qkv_part = jnp.einsum("td,cte->cde", whole, d_projected, preferred_element_type=jnp.float32)
+    grad_qkv = lax.psum_scatter(
+        qkv_part.astype(jnp.bfloat16), "dp", scatter_dimension=1, tiled=True
+    ).astype(jnp.float32)
+    first_gain_part = jnp.sum(d_normed_part * hat_all, axis=0)
+    return grad_normalized, grad_qkv, grad_out, first_gain_part
 
 
 def on_device(
@@ -748,7 +1407,7 @@
 
     inputs_float = tokens.astype(jnp.float32)
     input_normalized_hat, first_inverse_rms = normalize(inputs_float)
-    hat_all, _ = normalize(tokens_all.astype(jnp.float32))
+    hat_all, inverse_all = normalize(tokens_all.astype(jnp.float32))
     whole = (hat_all * first_norm_gain).astype(jnp.bfloat16)
     cosine, sine = rotary_tables(seq_len, head_size)
     projected = jnp.einsum("td,cde->cte", whole, qkv_full, preferred_element_type=jnp.float32)
@@ -831,55 +1490,63 @@
         scaled_two - hhat * jnp.mean(scaled_two * hhat, axis=-1, keepdims=True)
     )
     d_attn = d_resid.astype(jnp.bfloat16)
-    whole_grad = lax.all_gather(d_attn, "expert", axis=0, tiled=True)
-    d_attended = contract_last(whole_grad, out_full).astype(jnp.bfloat16)
-    out_part = contract_first(attended, whole_grad)
-    grad_out = lax.psum_scatter(
-        out_part.astype(jnp.bfloat16), "dp", scatter_dimension=1, tiled=True
-    ).astype(jnp.float32)
-    d_heads = d_attended.reshape(seq_len, heads_local, head_size)
-    probs = jnp.exp(masked_scores(query, key_rows, allowed) - log_total)
-    probs_low = probs.astype(jnp.bfloat16)
-    d_value = jnp.einsum(
-        "hqk,qhd->khd", probs_low, d_heads, preferred_element_type=jnp.float32
-    ).astype(jnp.bfloat16)
-    d_probs = jnp.einsum("qhd,khd->hqk", d_heads, value, preferred_element_type=jnp.float32)
-    row_delta = jnp.sum(probs * d_probs, axis=-1, keepdims=True)
-    d_scores = (probs * (d_probs - row_delta)).astype(jnp.bfloat16)
-    scale = head_size ** (-0.5)
-    d_query = (
-        jnp.einsum("hqk,khd->qhd", d_scores, key_rows, preferred_element_type=jnp.float32) * scale
-    )
-    d_key = jnp.einsum("hqk,qhd->khd", d_scores, query, preferred_element_type=jnp.float32) * scale
-    d_query_pre = (
-        rotate_back(d_query, cosine, sine).reshape(seq_len, local_width).astype(jnp.bfloat16)
-    )
-    d_key_pre = rotate_back(d_key, cosine, sine).reshape(seq_len, local_width).astype(jnp.bfloat16)
-    d_projected = jnp.stack([d_query_pre, d_key_pre, d_value.reshape(seq_len, local_width)])
-    d_normed_part = jnp.einsum(
-        "cte,cde->td", d_projected, qkv_full, preferred_element_type=jnp.float32
-    )
-    grad_normalized = lax.psum_scatter(
-        d_normed_part.astype(jnp.bfloat16), "expert", scatter_dimension=0, tiled=True
-    ).astype(jnp.float32)
-    qkv_part = jnp.einsum("td,cte->cde", whole, d_projected, preferred_element_type=jnp.float32)
-    grad_qkv = lax.psum_scatter(
-        qkv_part.astype(jnp.bfloat16), "dp", scatter_dimension=1, tiled=True
-    ).astype(jnp.float32)
-    first_gain_part = jnp.sum(d_normed_part * hat_all, axis=0)
+    if split:
+        small_part = jnp.concatenate(
+            [jnp.zeros((1, width)), gain_two_part[None], router_part.T, jnp.zeros((2, width))],
+            axis=0,
+        )
+        grad_normalized, grad_weights, small_own, gate_got = attention_back_call(
+            lengths,
+            d_attn,
+            tokens_all,
+            inverse_all,
+            whole,
+            out_full,
+            qkv_full,
+            query.reshape(seq_len, local_width),
+            key_rows.reshape(seq_len, local_width),
+            value.reshape(seq_len, local_width),
+            attended,
+            log_total[:, :, 0].T,
+            jnp.concatenate([cosine[:, 0], cosine[:, 0]], axis=1),
+            jnp.concatenate([sine[:, 0], -sine[:, 0]], axis=1),
+            small_part,
+            grad_gate_up,
+        )
+        grad_gate_up = widen_slices(gate_got)
+        grad_qkv = jnp.stack(
+            [grad_weights[:, c * local_width : (c + 1) * local_width] for c in range(3)]
+        )
+        grad_out = grad_weights[:, 3 * local_width :].T
+    else:
+        grad_normalized, grad_qkv, grad_out, first_gain_part = attention_back_plain(
+            lengths,
+            d_attn,
+            hat_all,
+            whole,
+            out_full,
+            qkv_full,
+            query,
+            key_rows,
+            value,
+            attended,
+            log_total,
+            cosine,
+            sine,
+        )
+        small_part = jnp.concatenate(
+            [first_gain_part[None], gain_two_part[None], router_part.T], axis=0
+        )
+        small_sum = lax.psum(small_part, ("dp", "expert"))
+        own_rows = width // dp_size
+        small_own = lax.dynamic_slice_in_dim(
+            small_sum, lax.axis_index("dp") * own_rows, own_rows, axis=1
+        )
     first_scaled_input = grad_normalized * first_norm_gain
     grad_tokens = d_resid + first_inverse_rms * (
         first_scaled_input
         - input_normalized_hat
         * jnp.mean(first_scaled_input * input_normalized_hat, axis=-1, keepdims=True)
-    )
-    small_part = jnp.concatenate(
-        [first_gain_part[None], gain_two_part[None], router_part.T], axis=0
-    )
-    small_sum = lax.psum(small_part, ("dp", "expert"))
-    own_rows = width // dp_size
-    small_own = lax.dynamic_slice_in_dim(
-        small_sum, lax.axis_index("dp") * own_rows, own_rows, axis=1
     )
     return (
         output,
@@ -888,7 +1555,7 @@
         grad_out,
         small_own[0],
         small_own[1],
-        small_own[2:].T,
+        small_own[2 : 2 + group_size].T,
         grad_gate_up,
         grad_down,
     )

time: 699 us -> 538 us (0.77)
  waiting for transfers between devices: 244 us -> 97.6 us
  Pallas kernels: 176 us -> 290 us
  local copies, waits for them, and re-layouts: 108 us -> 37.1 us
  matrix products: 56.2 us -> 23.4 us
  blocking collectives: 49.2 us -> 35.4 us
  other arithmetic: 33.1 us -> 23.2 us
    pallas_call x0 -> x2, Pallas kernels: none -> 112 us  [the longest x1 104 us: attention_back_call(): pl.pallas_call(functools.partial(attention_back_kernel, heads), out_shape...]
    ppermute x6 -> x3, waiting for transfers between devices: 90.1 us -> 12.9 us  [swap_chips(): got.append(lax.ppermute(pieces[step], 'dp', pairs))]
    all_gather x1 -> x0, waiting for transfers between devices: 53.7 us -> none  [on_device(): whole_grad = lax.all_gather(d_attn, 'expert', axis=0, tiled=True)]
    psum x1 -> x0, blocking collectives: 38.7 us -> none  [on_device(): small_sum = lax.psum(small_part, ('dp', 'expert'))]
    all_gather x1, waiting for transfers between devices: 33.4 us -> 2.35 us  [on_device(): tokens_all = lax.all_gather(tokens, 'expert', axis=0, tiled=True)]
    unnamed x134 -> x129, local copies, waits for them, and re-layouts: 38.9 us -> 9.27 us
    dot_general x7 -> x0, matrix products: 28.5 us -> none  [the longest x1 9.42 us: on_device(): jnp.einsum('cte,cde->td', d_projected, qkv_full, preferred_element_type=j...]
    all_gather x1, blocking collectives: 10.5 us -> 35.4 us  [on_device(): small_full = lax.all_gather(small, 'dp', axis=0, tiled=True)]
  transfers between devices with their start and end apart: 14 -> 7, of which waited for: 9 -> 5; matrix products, arithmetic and copies ran while one was open for 25% -> 11% of each run, Pallas kernels for 0% -> 0%
where the time goes in v3:
time: 538 us; the launch traced here: 528 us
  Pallas kernels  290 us (54%)
  waiting for transfers between devices  97.6 us (18%)
  local copies, waits for them, and re-layouts  37.1 us (7%)
  blocking collectives  35.4 us (7%)
  matrix products  23.4 us (4%)
  other arithmetic  23.2 us (4%)
  between operations  15.6 us (3%)
  starting transfers between devices  6.02 us (1%)
    pallas_call x1, Pallas kernels, experts_call(): pl.pallas_call(functools.partial(experts_kernel, group), out_shape=(jax.S...  177 us
    pallas_call x1, Pallas kernels, attention_back_call(): pl.pallas_call(functools.partial(attention_back_kernel, heads), out_shape...  104 us
    all_gather x1, waiting for transfers between devices, on_device(): qkv_full = lax.all_gather(w_qkv, 'dp', axis=1, tiled=True)  43.4 us
    all_gather x1, blocking collectives, on_device(): small_full = lax.all_gather(small, 'dp', axis=0, tiled=True)  35.4 us
    reduce_scatter x1, waiting for transfers between devices, on_device(): lax.psum_scatter(attn_part.astype(jnp.bfloat16), 'expert', scatter_dimens...  24.1 us
    all_gather x1, waiting for transfers between devices, on_device(): out_full = lax.all_gather(w_out, 'dp', axis=1, tiled=True)  13.5 us
    ppermute x3, waiting for transfers between devices, swap_chips(): got.append(lax.ppermute(pieces[step], 'dp', pairs))  12.9 us
  transfers between devices with their start and end apart: 7, of which 5 were waited for; matrix products, arithmetic and copies ran while one was open for 11% of the time, Pallas kernels for 0%

profile of v3, /device:TPU:0, one launch (start us, length us, event | category | flops | bytes accessed | tf_op | source)
XLA Modules:
  0.0 528.0 jit_solution(10563138046303870307)
XLA Ops:
  7.2 0.7 all-gather.4.cloned.1.call-update
  8.0 0.7 all-gather.6.cloned.1.call-update
  8.8 4.8 dynamic-slice_bitcast_fusion.1
  13.6 1.2 pad_maximum_fusion.2
  14.8 2.9 collective-permute-start
  18.5 35.4 %all_gather.13 = bf16[2048,6]{0,1:T(8,128)(2,1)S(1)} all-gather(bf16[256,6]{0,1:T(8,128)(2,1)S(1)} %pad_maximum_fusion.7), channel_id=1, replica_groups=mesh['dp'=8,'expert'=4] {'dp'}, dimensions={0}, use_global_device_ids=true | all-gather | bytes 27648 | tf_op jit(solution)/shard_map/all_gather | solution.py:1390
  54.1 1.8 fusion.33
  55.9 2.4 all-gather.4.cloned.1.call-done.tokens_all
  58.3 2.2 fusion
  60.5 0.5 fusion.2.whole
  61.1 43.4 %all-gather.6.cloned.1.call-done.w_qkv = bf16[3,2048,512]{2,1,0:T(8,128)(2,1)} async-done(((bf16[3,256,512]{2,1,0:T(8,128)(2,1)}), bf16[3,2048,512]{2,1,0:T(8,128)(2,1)}) %all-gather.6.cloned.1.call-update) | async-done | bytes 6291472 | tf_op jit(solution)/shard_map/all_gather | solution.py:1391
  104.4 5.7 %fusion.9 = f32[3,512,512]{2,1,0:T(8,128)S(1)} fusion(bf16[3,2048,512]{2,1,0:T(8,128)(2,1)} %all-gather.6.cloned.1.call-done.w_qkv, bf16[512,2048]{1,0:T(8,128)(2,1)S(1)} %fusion.2.whole), kind=kOutput, calls=%fused_computation.19 | convolution fusion | flops 3221225472 | bytes 11534336 | tf_op jit(solution)/shard_map/td,cde->cte/dot_general | solution.py:1413
  110.2 0.9 slice.122
  111.3 0.7 copy-done.14
  112.4 2.1 copy.188
  114.8 0.6 fusion.52
  115.4 0.6 fusion.51
  116.5 0.5 multiply_subtract_fusion
  117.0 0.6 maximum_convert_fusion
  117.6 0.9 fusion.3
  118.5 0.9 fusion.4
  119.5 1.5 fusion.12
  121.0 13.5 %all-gather.8.cloned.1.call-done.w_out = bf16[512,2048]{1,0:T(8,128)(2,1)} async-done(((bf16[512,256]{1,0:T(8,128)(2,1)}), bf16[512,2048]{1,0:T(8,128)(2,1)}) %all-gather.8.cloned.1.call-update) | async-done | bytes 2097168 | tf_op jit(solution)/shard_map/all_gather | solution.py:1392
  134.5 4.3 convolution_convert_fusion
  138.9 1.2 pad_maximum_fusion.3
  140.2 1.2 collective-permute-start.1
  141.4 2.6 pad_maximum_fusion.4
  144.0 1.8 collective-permute-start.2
  145.7 0.5 pad.3.clone
  146.3 0.6 pad.6.clone
  148.9 1.0 pad_maximum_fusion.5
  150.0 1.2 pad_maximum_fusion.1.w_own
  151.2 0.9 copy.183.inverse_all
  152.0 2.0 copy.189.attended
  154.1 0.9 copy.182
  154.9 0.8 copy_bitcast_fusion.1.query
  155.8 0.9 copy_bitcast_fusion.key_rows
  156.7 2.1 slice_bitcast_fusion.13.value
  158.8 24.1 %reduce-scatter.2.cloned.1.call-done = bf16[128,2048]{1,0:T(8,128)(2,1)} async-done(((bf16[512,2048]{1,0:T(8,128)(2,1)}), bf16[128,2048]{1,0:T(8,128)(2,1)}) %reduce-scatter.2.cloned.1.call-update) | async-done | bytes 524304 | tf_op jit(solution)/shard_map/reduce_scatter | solution.py:1434
  182.9 1.3 multiply_reduce_fusion.4
  184.2 1.3 multiply_convert_fusion.3
  185.8 2.6 gather_fusion
  188.7 1.4 convolution_convert_fusion.1
  190.1 0.5 fusion.23
  190.7 1.5 fusion.5
  192.2 12.9 %collective-permute-done.1.w_y = bf16[256,2816]{1,0:T(8,128)(2,1)} collective-permute-done((bf16[256,2816]{1,0:T(8,128)(2,1)}, bf16[256,2816]{1,0:T(8,128)(2,1)}, u32[]{:S(2)}, u32[]{:S(2)}) %collective-permute-start.1) | collective-permute-done | bytes 1441824 | tf_op jit(solution)/shard_map/ppermute | solution.py:1236
  205.1 177.2 %experts.1 = (bf16[4,64,2048]{2,1,0:T(8,128)(2,1)}, bf16[4,64,2048]{2,1,0:T(8,128)(2,1)}, bf16[4,256,2816]{2,1,0:T(8,128)(2,1)}, f32[704,2048]{1,0:T(8,128)}) custom-call(bf16[4,64,2048]{2,1,0:T(8,128)(2,1)} %bitcast.107, bf16[4,64,2048]{2,1,0:T(8,128)(2,1)} %bitcast.110, bf16[256,2816]{1,0:T(8,128)(2,1)} %pad_maximum_fusion.1.w_own, ...), custom_call_target="tpu_custom_call" | custom-call | flops 53150220288 | bytes 20185088 | tf_op jit(solution)/shard_map/experts/pallas_call | solution.py:516
  382.4 1.7 fusion.32
  384.2 3.4 multiply_reduce_fusion.3
  388.1 0.6 fusion.36
  388.8 1.2 multiply_reduce_fusion
  390.0 0.8 maximum_maximum_fusion.small_part
  390.9 1.2 fusion.47.d_attn
  392.1 103.9 %attention_back.1 = (f32[128,2048]{1,0:T(8,128)}, f32[256,2048]{1,0:T(8,128)}, f32[8,256]{1,0:T(8,128)}, bf16[4,256,2816]{2,1,0:T(8,128)(2,1)}) custom-call(s32[1]{0:T(128)} %copy.208.length, bf16[128,2048]{1,0:T(8,128)(2,1)} %fusion.47.d_attn, bf16[512,2048]{1,0:T(8,128)(2,1)} %all-gather.4.cloned.1.call-done.tokens_all, f32[512,1]{1,0:T(8,128)} %copy.183.inverse_all, ...), custom_call_target="tpu_custom_call" | custom-call | flops 9932111872 | bytes 40000000 | tf_op jit(solution)/shard_map/attention_back/pallas_call | solution.py:1129
  496.0 1.4 fusion.53
  497.4 1.3 slice_bitcast_fusion.10
  498.7 0.7 add_rsqrt_fusion.1
  499.4 2.5 slice_bitcast_fusion
  501.9 1.0 copy.184
  503.2 8.5 %widen.1 = f32[256,11264]{1,0:T(8,128)} custom-call(s32[1]{0:T(128)} %bitcast.40.own_ref, bf16[4,256,2816]{2,1,0:T(8,128)(2,1)} %get-tuple-element.23.source), custom_call_target="tpu_custom_call" | custom-call | tf_op jit(solution)/shard_map/widen/pallas_call | solution.py:1211
  511.8 1.3 pad_maximum_fusion
  513.0 0.6 copy-done.6
  513.8 1.6 fusion.19
  515.4 5.9 %copy.209 = f32[1,704,2048]{2,1,0:T(8,128)} copy(f32[1,704,2048]{2,1,0:T(8,128)} %bitcast.105) | data formatting | bytes 11534336
  (182 shorter events, 5.3 us)
Async XLA Ops:
  7.2 51.1 %all-gather.4.cloned.1.call-start = ((), (), s32[]{:S(2)}) async-start(), calls=%async_computation.1 | async-start | bytes 2621440 | tf_op jit(solution)/shard_map/all_gather | solution.py:1386
  7.9 96.5 %all-gather.6.cloned.1.call-start = ((), (), s32[]{:S(2)}) async-start(), calls=%async_computation.2 | async-start | bytes 7077888 | tf_op jit(solution)/shard_map/all_gather | solution.py:1391
  8.7 125.9 %all-gather.8.cloned.1.call-start = ((), (), s32[]{:S(2)}) async-start(), calls=%async_computation.3 | async-start | bytes 2359296 | tf_op jit(solution)/shard_map/all_gather | solution.py:1392
  13.5 4.9 copy-start.61
  13.5 4.9 copy-start.62
  13.5 5.0 copy-start.57
  14.8 177.5 %collective-permute-start = (bf16[256,2816]{1,0:T(8,128)(2,1)}, bf16[256,2816]{1,0:T(8,128)(2,1)}, u32[]{:S(2)}, u32[]{:S(2)}) collective-permute-start(bf16[256,2816]{1,0:T(8,128)(2,1)} %pad_maximum_fusion.2), channel_id=1, source_target_pairs={{0,8},{4,12},{8,0},{12,4},{16,24},{20,28},{24,16},{28,20},{1,9},{5... | collective-permute-start | bytes 4325384 | tf_op jit(solution)/shard_map/ppermute | solution.py:1236
  17.7 165.2 %reduce-scatter.2.cloned.1.call-start = ((), (), s32[]{:S(2)}) async-start(), calls=%async_computation.4 | async-start | bytes 2621440 | tf_op jit(solution)/shard_map/reduce_scatter | solution.py:1434
  53.9 131.6 %copy-start.32 = (bf16[2048,6]{0,1:T(8,128)(2,1)}, bf16[2048,6]{0,1:T(8,128)(2,1)S(1)}, u32[]{:S(2)}) copy-start(bf16[2048,6]{0,1:T(8,128)(2,1)S(1)} %all_gather.13) | copy-start | bytes 73732
  54.0 7.1 %copy-start.37 = (f32[2048,1]{0,1:T(1,128)}, f32[2048,1]{0,1:T(1,128)S(1)}, u32[]{:S(2)}) copy-start(f32[2048,1]{0,1:T(1,128)S(1)} %get-tuple-element.114) | copy-start | bytes 24580
  54.0 130.2 %copy-start.34 = (f32[2048,1]{0,1:T(1,128)}, f32[2048,1]{0,1:T(1,128)S(1)}, u32[]{:S(2)}) copy-start(f32[2048,1]{0,1:T(1,128)S(1)} %get-tuple-element.113) | copy-start | bytes 24580
  58.3 2.2 copy-start.9
  61.1 49.1 %copy-start.23 = (bf16[512,2048]{1,0:T(8,128)(2,1)}, bf16[512,2048]{1,0:T(8,128)(2,1)S(1)}, u32[]{:S(2)}) copy-start(bf16[512,2048]{1,0:T(8,128)(2,1)S(1)} %fusion.2.whole) | copy-start | bytes 6291460
  121.0 17.8 %copy-start.29 = (bf16[4,128,512]{2,1,0:T(8,128)(2,1)}, bf16[4,128,512]{2,1,0:T(8,128)(2,1)S(1)}, u32[]{:S(2)}) copy-start(bf16[4,128,512]{2,1,0:T(8,128)(2,1)S(1)} %fusion.12) | copy-start | bytes 1572868
  134.5 4.3 copy-start.17
  134.5 4.3 copy-start.18
  138.9 8.3 %copy-start.39 = (s32[128,2]{0,1:T(2,128)S(1)}, s32[128,2]{0,1:T(2,128)}, u32[]{:S(2)}) copy-start(s32[128,2]{0,1:T(2,128)} %param.21) | copy-start | bytes 3076
  138.9 8.6 %copy-start.58 = (s32[128]{0:T(128)S(1)}, s32[128]{0:T(128)}, u32[]{:S(2)}) copy-start(s32[128]{0:T(128)} %param.22) | copy-start | bytes 1540
  138.9 9.9 %copy-start.20 = (f32[512,64]{1,0:T(8,128)S(1)}, f32[512,64]{1,0:T(8,128)}, u32[]{:S(2)}) copy-start(f32[512,64]{1,0:T(8,128)} %get-tuple-element.120) | copy-start | bytes 393220
  138.9 9.9 %copy-start.22 = (f32[512,64]{1,0:T(8,128)S(1)}, f32[512,64]{1,0:T(8,128)}, u32[]{:S(2)}) copy-start(f32[512,64]{1,0:T(8,128)} %get-tuple-element.121) | copy-start | bytes 393220
  138.9 9.9 %copy-start.26 = (f32[512,64]{1,0:T(8,128)S(1)}, f32[512,64]{1,0:T(8,128)}, u32[]{:S(2)}) copy-start(f32[512,64]{1,0:T(8,128)} %get-tuple-element.119) | copy-start | bytes 393220
  140.2 9.8 %copy-start.15 = (bf16[256,1408]{1,0:T(8,128)(2,1)S(1)}, bf16[256,1408]{1,0:T(8,128)(2,1)}, u32[]{:S(2)}) copy-start(bf16[256,1408]{1,0:T(8,128)(2,1)} %get-tuple-element.93) | copy-start | bytes 2162692
  140.2 9.8 %copy-start.16 = (bf16[256,1408]{1,0:T(8,128)(2,1)S(1)}, bf16[256,1408]{1,0:T(8,128)(2,1)}, u32[]{:S(2)}) copy-start(bf16[256,1408]{1,0:T(8,128)(2,1)} %get-tuple-element.94) | copy-start | bytes 2162692
  140.2 65.0 %collective-permute-start.1 = (bf16[256,2816]{1,0:T(8,128)(2,1)}, bf16[256,2816]{1,0:T(8,128)(2,1)}, u32[]{:S(2)}, u32[]{:S(2)}) collective-permute-start(bf16[256,2816]{1,0:T(8,128)(2,1)} %pad_maximum_fusion.3), channel_id=1, source_target_pairs={{0,16},{4,20},{8,24},{12,28},{16,0},{20,4},{24,8},{28,12},{1,17},{... | collective-permute-start | bytes 4325384 | tf_op jit(solution)/shard_map/ppermute | solution.py:1236
  144.0 61.2 %collective-permute-start.2 = (bf16[256,2816]{1,0:T(8,128)(2,1)}, bf16[256,2816]{1,0:T(8,128)(2,1)}, u32[]{:S(2)}, u32[]{:S(2)}) collective-permute-start(bf16[256,2816]{1,0:T(8,128)(2,1)} %pad_maximum_fusion.4), channel_id=1, source_target_pairs={{0,24},{4,28},{8,16},{12,20},{16,8},{20,12},{24,0},{28,4},{1,25},{... | collective-permute-start | bytes 4325384 | tf_op jit(solution)/shard_map/ppermute | solution.py:1236
  146.9 43.8 %copy-start.43 = (f32[128]{0:T(128)}, f32[128]{0:T(128)S(1)}, u32[]{:S(2)}) copy-start(f32[128]{0:T(128)S(1)} %get-tuple-element.84) | copy-start | bytes 1540
  148.8 39.9 %copy-start.27 = (bf16[256,128]{1,0:T(8,128)(2,1)}, bf16[256,128]{1,0:T(8,128)(2,1)S(1)}, u32[]{:S(2)}) copy-start(bf16[256,128]{1,0:T(8,128)(2,1)S(1)} %convert_reduce_fusion) | copy-start | bytes 196612
  149.9 40.7 %copy-start.31 = (pred[256,128,2]{1,0,2:T(32,128)(4,1)}, pred[256,128,2]{1,0,2:T(32,128)(4,1)S(1)}, u32[]{:S(2)}) copy-start(pred[256,128,2]{1,0,2:T(32,128)(4,1)S(1)} %fusion.30) | copy-start | bytes 196612
  151.2 31.7 %copy-start = (bf16[128,2048]{1,0:T(8,128)(2,1)S(1)}, bf16[128,2048]{1,0:T(8,128)(2,1)}, u32[]{:S(2)}) copy-start(bf16[128,2048]{1,0:T(8,128)(2,1)} %param.12) | copy-start | bytes 1572868
  184.2 4.2 copy-start.48
  185.5 3.2 copy-start.7
  185.7 4.4 copy-start.10
  188.6 3.6 copy-start.41
  188.6 3.6 copy-start.46
  188.7 3.5 copy-start.51
  188.7 3.5 copy-start.55
  188.7 3.5 copy-start.56
  382.3 5.3 %copy-start.42 = (f32[128,2]{0,1:T(2,128)S(1)}, f32[128,2]{0,1:T(2,128)}, u32[]{:S(2)}) copy-start(f32[128,2]{0,1:T(2,128)} %copy-done.41) | copy-start | bytes 3076
  382.3 5.3 copy-start.47
  382.4 5.3 copy-start.52
  382.4 5.3 %copy-start.40 = (s32[128,2]{0,1:T(2,128)S(1)}, s32[128,2]{0,1:T(2,128)}, u32[]{:S(2)}) copy-start(s32[128,2]{0,1:T(2,128)} %param.21) | copy-start | bytes 3076
  382.4 5.3 %copy-start.8 = (bf16[128,2048]{1,0:T(8,128)(2,1)S(1)}, bf16[128,2048]{1,0:T(8,128)(2,1)}, u32[]{:S(2)}) copy-start(bf16[128,2048]{1,0:T(8,128)(2,1)} %copy-done.7) | copy-start | bytes 1572868
  384.1 4.0 copy-start.33
  384.1 4.6 copy-start.1
  384.1 4.6 copy-start.3
  384.1 4.6 copy-start.25
  384.1 4.6 copy-start.28
  384.1 4.6 copy-start.35
  384.2 4.6 copy-start.49
  387.7 2.3 copy-start.59
  387.7 2.3 copy-start.60
  387.7 3.1 copy-start.11
  387.7 3.1 copy-start.44
  390.0 2.1 copy-start.5
  390.0 2.1 copy-start.53
  496.0 6.9 %copy-start.2 = (bf16[128,2048]{1,0:T(8,128)(2,1)S(1)}, bf16[128,2048]{1,0:T(8,128)(2,1)}, u32[]{:S(2)}) copy-start(bf16[128,2048]{1,0:T(8,128)(2,1)} %param.12) | copy-start | bytes 1572868
  496.0 6.9 %copy-start.13 = (f32[128,2048]{1,0:T(8,128)S(1)}, f32[128,2048]{1,0:T(8,128)}, u32[]{:S(2)}) copy-start(f32[128,2048]{1,0:T(8,128)} %get-tuple-element.20) | copy-start | bytes 3145732
  496.0 6.8 %copy-start.38 = (f32[2048,1]{0,1:T(1,128)S(1)}, f32[2048,1]{0,1:T(1,128)}, u32[]{:S(2)}) copy-start(f32[2048,1]{0,1:T(1,128)} %copy-done.37) | copy-start | bytes 24580
  503.2 8.6 %copy-start.24 = (f32[1,256,512]{2,1,0:T(8,128)S(1)}, f32[1,256,512]{2,1,0:T(8,128)}, u32[]{:S(2)}) copy-start(f32[1,256,512]{2,1,0:T(8,128)} %get-tuple-element.106) | copy-start | bytes 1572868
  511.7 2.1 copy-start.12
  511.7 2.1 copy-start.36
  511.7 2.1 copy-start.45
  511.7 2.1 copy-start.50
  511.8 2.1 copy-start.54
  (6 other events, 8.1 us)
Sparse Core Ops, SparseCore 0:
  9.6 48.6 all-gather.3
  60.2 44.2 all-gather.5
  106.3 28.1 all-gather.7
  139.0 43.8 reduce-scatter.1

commit v4 on v3

--- a/solution.py
+++ b/solution.py
@@ -2,6 +2,7 @@
 
 import jax
 import jax.numpy as jnp
+import numpy as np
 from jax import lax
 from jax.experimental import pallas as pl
 from jax.experimental.pallas import tpu as pltpu
@@ -51,11 +52,9 @@
     group,
     sent,
     d_back,
-    w_own,
-    w_x,
-    w_y,
-    w_diag,
-    down_own,
+    w_gate_up,
+    w_got,
+    w_down,
     ret,
     d_ret,
     grad_gate_up,
@@ -81,9 +80,9 @@
 ):
     cap, width = sent.shape[1], sent.shape[2]
     half = cap // 2
-    piece = w_own.shape[0]
-    hidden2 = w_own.shape[1]
+    piece, hidden2 = w_got.shape[1:]
     hidden = hidden2 // 2
+    down_own = w_down.at[0]
     down_rows = down_own.shape[0]
     chunk = 4 * cap
     total = group * chunk
@@ -211,33 +210,45 @@
         else:
             back_copy(t, k).start()
 
-    pieces = (w_own, w_x, w_y, w_diag)
-
     def w_rows(r, which):
-        return w_buf.at[pl.ds(pl.multiple_of((chips[r] * 2 + which) * piece, piece), piece), :]
-
-    def w_share(r):
-        return remote(
-            pieces[r], w_rows(r, core), weight_sems.at[0, r], weight_sems.at[1, r], partner
-        )
-
-    def w_share_in(r):
-        return remote(
-            pieces[r], w_rows(r, 1 - core), weight_sems.at[0, r], weight_sems.at[1, r], partner
-        )
+        return pl.ds(pl.multiple_of((chips[r] * 2 + which) * piece, piece), piece)
+
+    def w_parts(r, which):
+        rows = w_rows(r, which)
+        if r > 0:
+            return [(w_got.at[r - 1], w_buf.at[rows, :], r)]
+        return [
+            (
+                w_gate_up.at[
+                    0, :, pl.ds(pl.multiple_of((4 * part + chips[0]) * hidden, LANES), hidden)
+                ],
+                w_buf.at[rows, pl.ds(part * hidden, hidden)],
+                4 * part,
+            )
+            for part in range(2)
+        ]
+
+    def w_share(r, which):
+        return [
+            remote(source, target, weight_sems.at[0, n], weight_sems.at[1, n], partner)
+            for source, target, n in w_parts(r, which)
+        ]
 
     def w_keep(r):
-        return pltpu.make_async_copy(pieces[r], w_rows(r, core), local_sems.at[4 + r])
+        return [
+            pltpu.make_async_copy(source, target, local_sems.at[4 + n])
+            for source, target, n in w_parts(r, core)
+        ]
 
     def down_at(which):
         return down_buf.at[pl.ds(pl.multiple_of(which * down_rows, down_rows), down_rows), :]
 
     def down_share():
         return remote(
-            down_own, down_at(core), weight_sems.at[0, 4], weight_sems.at[1, 4], partner
-        )
-
-    down_keep = pltpu.make_async_copy(down_own, down_at(core), local_sems.at[8])
+            down_own, down_at(core), weight_sems.at[0, 5], weight_sems.at[1, 5], partner
+        )
+
+    down_keep = pltpu.make_async_copy(down_own, down_at(core), local_sems.at[9])
 
     def forward(k):
         base = k * chunk
@@ -308,14 +319,12 @@
 
         lax.fori_loop(0, width // (2 * LANES), out_tile, 0)
 
-    w_share(0).start()
-    w_keep(0).start()
     own_copy(0).start()
     for k in range(1, group):
         z_copy(0, k).start()
-    for r in range(1, 4):
-        w_share(r).start()
-        w_keep(r).start()
+    for r in range(4):
+        for copy in w_share(r, core) + w_keep(r):
+            copy.start()
     down_share().start()
     down_keep.start()
     own_copy(1).start()
@@ -329,8 +338,10 @@
     relay(0, 1)
     arrived(0, 0)
     for r in range(4):
-        w_keep(r).wait()
-        w_share_in(r).wait_recv()
+        for copy in w_keep(r):
+            copy.wait()
+        for copy in w_share(r, 1 - core):
+            copy.wait_recv()
     down_keep.wait()
     down_share().wait_recv()
     forward(0)
@@ -482,7 +493,8 @@
     for r in range(4):
         gate_out(r).wait()
         gate_send(r).wait_send()
-        w_share(r).wait_send()
+        for copy in w_share(r, core):
+            copy.wait_send()
     down_share().wait_send()
     down_send.wait_send()
     for t in range(2):
@@ -502,11 +514,11 @@
                 back_copy(t, k).wait_recv()
 
 
-def experts_call(sent, d_back, pieces, down_own):
+def experts_call(sent, d_back, w_gate_up, w_got, w_down):
     group, cap, width = sent.shape
-    piece, hidden2 = pieces[0].shape
+    piece, hidden2 = w_got.shape[1:]
     hidden = hidden2 // 2
-    down_rows = down_own.shape[0]
+    down_rows = w_down.shape[1]
     chunk = 4 * cap
     total = group * chunk
     low = jnp.bfloat16
@@ -521,7 +533,7 @@
             jax.ShapeDtypeStruct((4, piece, hidden2), low),
             jax.ShapeDtypeStruct((down_rows, width), jnp.float32),
         ),
-        in_specs=[anywhere] * 7,
+        in_specs=[anywhere] * 5,
         out_specs=(anywhere,) * 4,
         scratch_shapes=[
             pltpu.VMEM((width, hidden2), low),
@@ -539,8 +551,8 @@
             pltpu.VMEM((2, down_rows, 2 * LANES), jnp.float32),
             pltpu.SemaphoreType.DMA((2, 5, 2, group)),
             pltpu.SemaphoreType.DMA((2, 5, 2, group)),
-            pltpu.SemaphoreType.DMA((2, 5)),
-            pltpu.SemaphoreType.DMA((9,)),
+            pltpu.SemaphoreType.DMA((2, 6)),
+            pltpu.SemaphoreType.DMA((10,)),
             pltpu.SemaphoreType.DMA((3, 6)),
         ],
         compiler_params=pltpu.CompilerParams(
@@ -548,7 +560,7 @@
         ),
         cost_estimate=pl.CostEstimate(flops=flops, bytes_accessed=moved, transcendentals=0),
         name="experts",
-    )(sent, d_back, *pieces, down_own)
+    )(sent, d_back, w_gate_up, w_got, w_down)
 
 
 def rotary_tables(length_total, head_size):
@@ -576,7 +588,7 @@
     )
 
 
-def slot_table(routes, order, valid, capacity, first_expert, experts):
+def slot_table(routes, order, valid, capacity):
     row_count = routes.shape[0]
     top_count = routes.shape[1]
     pair_rank = order[:, None] + row_count * jnp.arange(top_count, dtype=jnp.int32)[None, :]
@@ -590,8 +602,7 @@
     )
     slot_index = jnp.sum(earlier.astype(jnp.int32), axis=1).reshape(row_count, top_count)
     kept_pair = valid[:, None] & (slot_index < capacity)
-    place = (routes + experts - first_expert) % experts
-    target = place * capacity + jnp.minimum(slot_index, capacity - 1)
+    target = routes * capacity + jnp.minimum(slot_index, capacity - 1)
     return (target, kept_pair)
 
 
@@ -820,7 +831,7 @@
             d_query = dot_nn(d_scores, one_key) * scale
             d_key_acc[:, cols] += dot_nn(d_scores.T, one_query) * scale
             d_value_acc[:, cols] += dot_nn(probs.astype(jnp.bfloat16).T, d_head)
-            d_proj[rows, cols] = rotated(d_query, cosine_buf[rows, :], sine_buf[rows, :]).astype(
+            d_proj[rows, cols] = rotated(d_query, cosine_buf[rows, :], -sine_buf[rows, :]).astype(
                 jnp.bfloat16
             )
 
@@ -853,7 +864,7 @@
     for head in range(heads):
         cols = slice(head * head_size, (head + 1) * head_size)
         key_cols = slice(local_width + head * head_size, local_width + (head + 1) * head_size)
-        d_proj[:, key_cols] = rotated(d_key_acc[:, cols], cosine_buf[...], sine_buf[...]).astype(
+        d_proj[:, key_cols] = rotated(d_key_acc[:, cols], cosine_buf[...], -sine_buf[...]).astype(
             jnp.bfloat16
         )
     d_proj[:, 2 * local_width :] = d_value_acc[...].astype(jnp.bfloat16)
@@ -1224,31 +1235,578 @@
     return wide[None]
 
 
-def across(index, step):
-    return ((index // 2) ^ step) * 2 + index % 2
-
-
-def swap_chips(pieces):
-    parts = lax.axis_size("dp")
-    got = [pieces[0]]
-    for step in (1, 2, 3):
-        pairs = [(index, across(index, step)) for index in range(parts)]
-        got.append(lax.ppermute(pieces[step], "dp", pairs))
-    return got
-
-
-def chip_slices(w_gate_up):
-    rows, ff2 = w_gate_up.shape[1:]
-    chips = lax.axis_size("dp") // 2
-    size = ff2 // 2 // chips
-    own = lax.axis_index("dp") // 2
-
-    def of_chip(chip):
-        gate = lax.dynamic_slice(w_gate_up[0], (0, chip * size), (rows, size))
-        up = lax.dynamic_slice(w_gate_up[0], (0, ff2 // 2 + chip * size), (rows, size))
-        return jnp.concatenate([gate, up], axis=1)
-
-    return swap_chips([of_chip(own ^ step) for step in range(chips)])
+def rotary_constants(length_total, head_size):
+    position = np.arange(length_total, dtype=np.float32)
+    steps = np.arange(head_size // 2, dtype=np.float32) * np.float32(2.0) / np.float32(head_size)
+    frequency = np.power(np.float32(THETA), -steps).astype(np.float32)
+    angles = (position[:, None] * frequency[None, :]).astype(np.float32)
+    cosine, sine = np.cos(angles), np.sin(angles)
+    return (
+        np.concatenate([cosine, cosine], axis=1).astype(np.float32),
+        np.concatenate([-sine, sine], axis=1).astype(np.float32),
+    )
+
+
+def attention_kernel(
+    heads,
+    length,
+    tokens,
+    w_qkv,
+    w_out,
+    small,
+    w_gate_up,
+    pair_cols,
+    pair_rows,
+    cosine,
+    sine,
+    cotangent,
+    tokens_all,
+    whole,
+    qkv_full,
+    out_full,
+    w_got,
+    inverse_all,
+    query,
+    key_rows,
+    value,
+    attended,
+    log_total,
+    small_full,
+    resid,
+    inverse_two,
+    gates,
+    hits,
+    sent,
+    d_back,
+    tokens_buf,
+    whole_buf,
+    w_qkv_buf,
+    w_out_buf,
+    part_buf,
+    from_left,
+    from_right,
+    cols_buf,
+    rows_buf,
+    cosine_buf,
+    sine_buf,
+    cotangent_buf,
+    load_sems,
+    line_sems,
+    sum_sems,
+    gather_sems,
+    small_sems,
+    slice_sems,
+):
+    tok, width = tokens.shape
+    seq_len = tokens_buf.shape[0]
+    group = seq_len // tok
+    local_width = w_out.shape[0]
+    head_size = local_width // heads
+    piece = w_qkv.shape[1]
+    parts = width // piece
+    ff = w_gate_up.shape[2] // 2
+    hidden = ff // 4
+    slots = hits.shape[1]
+    cap = slots // group
+    scale = head_size**-0.5
+
+    index = lax.axis_index("dp")
+    place = lax.axis_index("expert")
+    core = index % 2
+    at_x = (index // 2) % 2
+    at_y = index // 4
+    other = at_y * 4 + at_x * 2 + (1 - core)
+    by_x = at_y * 4 + (1 - at_x) * 2 + core
+    by_y = (1 - at_y) * 4 + at_x * 2 + core
+    by_both = (1 - at_y) * 4 + (1 - at_x) * 2 + core
+    partner = {"dp": other}
+    along_x = {"dp": by_x}
+    along_y = {"dp": by_y}
+    over = {"dp": by_both}
+    right = {"expert": (place + 1) % group}
+    left = {"expert": (place + group - 1) % group}
+
+    def ring_peer(k):
+        return {"dp": (index + k) % parts}
+
+    def rows_of(block):
+        return pl.ds(pl.multiple_of(block * tok, tok), tok)
+
+    def piece_of(number):
+        return pl.ds(pl.multiple_of(number * piece, piece), piece)
+
+    def qkv_spot(number):
+        return w_qkv_buf.at[:, piece_of(number), :]
+
+    def qkv_half(number, which):
+        start = pl.multiple_of(number * piece + which * (piece // 2), piece // 2)
+        return w_qkv_buf.at[:, pl.ds(start, piece // 2), :]
+
+    def out_spot(number):
+        return w_out_buf.at[:, piece_of(number)]
+
+    def out_half(number, which):
+        rows = pl.ds(which * (local_width // 2), local_width // 2)
+        return w_out_buf.at[rows, piece_of(number)]
+
+    class Gather:
+        def __init__(self, number, source, spot, half_spot):
+            self.number, self.source, self.spot, self.half_spot = number, source, spot, half_spot
+
+        def copy(self, slot, source, target, peer):
+            sems = gather_sems.at[self.number]
+            return remote(source, target, sems.at[0, slot], sems.at[1, slot], peer)
+
+        def own(self, slot, peer):
+            return self.copy(slot, self.source, self.spot(index), peer)
+
+        def keep(self):
+            return pltpu.make_async_copy(
+                self.source, self.spot(index), load_sems.at[8 + self.number]
+            )
+
+        def relay_x(self):
+            spot = self.half_spot(by_y, 0)
+            return self.copy(3, spot, spot, along_x)
+
+        def relay_y(self):
+            spot = self.half_spot(by_x, 1)
+            return self.copy(4, spot, spot, along_y)
+
+        def hand(self, slot):
+            spot = (
+                self.spot(by_x),
+                self.spot(by_y),
+                self.half_spot(by_both, 0),
+                self.half_spot(by_both, 1),
+            )[slot - 5]
+            return self.copy(slot, spot, spot, partner)
+
+        def begin(self):
+            self.own(0, along_x).start()
+            self.own(1, along_y).start()
+            self.own(2, partner).start()
+            self.keep().start()
+
+        def relay(self):
+            self.own(1, along_y).wait_recv()
+            self.relay_x().start()
+            self.own(0, along_x).wait_recv()
+            self.relay_y().start()
+            self.hand(5).start()
+            self.hand(6).start()
+
+        def finish(self):
+            self.relay_x().wait_recv()
+            self.hand(7).start()
+            self.relay_y().wait_recv()
+            self.hand(8).start()
+            self.keep().wait()
+            self.own(2, partner).wait_recv()
+            for slot in (5, 6, 7, 8):
+                self.hand(slot).wait_recv()
+
+        def drain(self):
+            for slot, peer in ((0, along_x), (1, along_y), (2, partner)):
+                self.own(slot, peer).wait_send()
+            self.relay_x().wait_send()
+            self.relay_y().wait_send()
+            for slot in (5, 6, 7, 8):
+                self.hand(slot).wait_send()
+
+    gather_qkv = Gather(0, w_qkv, qkv_spot, qkv_half)
+    gather_out = Gather(1, w_out, out_spot, out_half)
+
+    loads = [
+        pltpu.make_async_copy(source, target, load_sems.at[number])
+        for number, (source, target) in enumerate(
+            [
+                (tokens, tokens_buf.at[rows_of(place)]),
+                (small, small_full.at[:, piece_of(index)]),
+                (pair_cols, cols_buf),
+                (pair_rows, rows_buf),
+                (cosine, cosine_buf),
+                (sine, sine_buf),
+                (cotangent, cotangent_buf),
+            ]
+        )
+    ]
+    for load in loads:
+        load.start()
+
+    greet([ring_peer(k) for k in range(1, parts)] + [right, left])
+
+    def own_pass(side, peer):
+        return remote(
+            tokens,
+            tokens_buf.at[rows_of(place)],
+            line_sems.at[side, place],
+            line_sems.at[2, place],
+            peer,
+        )
+
+    def pass_on(block, side, peer):
+        spot = tokens_buf.at[rows_of(block)]
+        return remote(spot, spot, line_sems.at[side, block], line_sems.at[2, block], peer)
+
+    @pl.when(place < group - 1)
+    def _():
+        own_pass(0, right).start()
+
+    @pl.when(place > 0)
+    def _():
+        own_pass(1, left).start()
+
+    def small_copy(k):
+        return remote(
+            small,
+            small_full.at[:, piece_of(index)],
+            small_sems.at[0, k],
+            small_sems.at[1, k],
+            ring_peer(k),
+        )
+
+    for k in range(1, parts):
+        small_copy(k).start()
+    gather_qkv.begin()
+
+    for load in loads:
+        load.wait()
+
+    cols = cols_buf[...]
+    rows = rows_buf[...]
+    first_col, second_col, order_col = cols[:, 0:1], cols[:, 1:2], cols[:, 2:3]
+    first_row, second_row, order_row = rows[0:1], rows[1:2], rows[2:3]
+    start = place * tok
+    live_col = (start + lax.broadcasted_iota(jnp.int32, (tok, 1), 0)) < length[0]
+    live_row = (start + lax.broadcasted_iota(jnp.int32, (1, tok), 1)) < length[0]
+    before = order_col < order_row
+
+    def count(mask):
+        return jnp.sum(jnp.where(mask & live_col, 1.0, 0.0), axis=0, keepdims=True)
+
+    slot_first = count((first_col == first_row) & before)
+    slot_second = count(first_col == second_row) + count((second_col == second_row) & before)
+    slot_ids = lax.broadcasted_iota(jnp.int32, (slots, tok), 0)
+    for number, (named, slot) in enumerate(((first_row, slot_first), (second_row, slot_second))):
+        slot = slot.astype(jnp.int32)
+        step = named - place
+        step = jnp.where(step < 0, step + group, step)
+        target = jnp.where(live_row & (slot < cap), step * cap + slot, -1)
+        hits[number] = jnp.where(slot_ids == target, 1.0, 0.0).astype(jnp.bfloat16)
+
+    for k in range(1, parts):
+        small_copy(k).wait_recv()
+
+    def normalize_block(block):
+        at = rows_of(block)
+        value = tokens_buf[at, :].astype(jnp.float32)
+        inverse = lax.rsqrt(jnp.mean(value * value, axis=-1, keepdims=True) + NORM_EPSILON)
+        inverse_all[at, :] = inverse
+        whole_buf[at, :] = (value * inverse * small_full[0:1, :]).astype(jnp.bfloat16)
+
+    def arrive(step):
+        block = line_order(place, step)
+        pass_on(block, 0, right).wait_recv()
+
+        @pl.when((block < place) & (place < group - 1))
+        def _():
+            pass_on(block, 0, right).start()
+
+        @pl.when((block > place) & (place > 0))
+        def _():
+            pass_on(block, 1, left).start()
+
+        normalize_block(block)
+
+    normalize_block(place)
+    arrive(0)
+    gather_qkv.relay()
+    gather_out.begin()
+    arrive(1)
+    gather_qkv.finish()
+
+    def project(first, size):
+        at = pl.ds(pl.multiple_of(first, tok), size)
+        source = whole_buf[at, :]
+
+        def two_heads(number, carry):
+            lanes = pl.ds(pl.multiple_of(number * 2 * head_size, 2 * head_size), 2 * head_size)
+            for c, target in ((0, query), (1, key_rows)):
+                plain = dot_nn(source, w_qkv_buf[c, :, lanes])
+                turned = [
+                    rotated(
+                        plain[:, side * head_size : (side + 1) * head_size],
+                        cosine_buf[at, :],
+                        sine_buf[at, :],
+                    )
+                    for side in range(2)
+                ]
+                target[at, lanes] = jnp.concatenate(turned, axis=1).astype(jnp.bfloat16)
+            value[at, lanes] = dot_nn(source, w_qkv_buf[2, :, lanes]).astype(jnp.bfloat16)
+            return carry
+
+        lax.fori_loop(0, heads // 2, two_heads, 0)
+
+    upper = place // 2
+    project(upper * tok, seq_len - tok)
+    gather_out.relay()
+
+    def slice_copy(r, part):
+        number = (by_x // 2, by_y // 2, by_both // 2)[r - 1]
+        lanes = pl.ds(pl.multiple_of(part * ff + number * hidden, LANES), hidden)
+        return remote(
+            w_gate_up.at[0, :, lanes],
+            w_got.at[r - 1, :, pl.ds(part * hidden, hidden)],
+            slice_sems.at[0, r - 1, part],
+            slice_sems.at[1, r - 1, part],
+            (along_x, along_y, over)[r - 1],
+        )
+
+    for part in range(2):
+        for r in (3, 1, 2):
+            slice_copy(r, part).start()
+    gather_out.finish()
+    arrive(2)
+    project((1 - upper) * (seq_len - tok), tok)
+
+    stores = [
+        pltpu.make_async_copy(source, target, load_sems.at[10 + number])
+        for number, (source, target) in enumerate(
+            [
+                (w_qkv_buf, qkv_full),
+                (w_out_buf, out_full),
+                (tokens_buf, tokens_all),
+                (whole_buf, whole),
+            ]
+        )
+    ]
+    for store in stores:
+        store.start()
+
+    for number in range(group):
+        at = slice(number * tok, (number + 1) * tok)
+        extent = (number + 1) * tok
+        shape = (tok, extent)
+        at_query = number * tok + lax.broadcasted_iota(jnp.int32, shape, 0)
+        at_key = lax.broadcasted_iota(jnp.int32, shape, 1)
+        allowed = (at_key <= at_query) & (at_key < length[0])
+        for head in range(heads):
+            lanes = slice(head * head_size, (head + 1) * head_size)
+            scores = dot_nt(query[at, lanes], key_rows[0:extent, lanes]) * scale
+            scores = jnp.where(allowed, scores, NEGATIVE)
+            top = jnp.max(scores, axis=-1, keepdims=True)
+            exponent = jnp.exp(scores - top)
+            row_total = jnp.sum(exponent, axis=-1, keepdims=True)
+            probs = (exponent / row_total).astype(jnp.bfloat16)
+            attended[at, lanes] = dot_nn(probs, value[0:extent, lanes]).astype(jnp.bfloat16)
+            log_total[at, head : head + 1] = top + jnp.log(row_total)
+
+    def out_tile(j, carry):
+        lanes = piece_of(j)
+        part_buf[:, lanes] = dot_nn(attended[...], w_out_buf[:, lanes]).astype(jnp.bfloat16)
+        return carry
+
+    lax.fori_loop(0, parts, out_tile, 0)
+
+    def go_right(block):
+        return remote(
+            part_buf.at[rows_of(block)],
+            from_left.at[block],
+            sum_sems.at[0, block],
+            sum_sems.at[1, block],
+            right,
+        )
+
+    def go_left(block):
+        return remote(
+            part_buf.at[rows_of(block)],
+            from_right.at[block],
+            sum_sems.at[0, block],
+            sum_sems.at[2, block],
+            left,
+        )
+
+    def add_into(target, added):
+        total = target[...].astype(jnp.float32) + added[...].astype(jnp.float32)
+        target[...] = total.astype(jnp.bfloat16)
+
+    def on_right(block):
+        go_right(block).wait_recv()
+        add_into(part_buf.at[rows_of(block)], from_left.at[block])
+        go_right(block).start()
+
+    def on_left(block):
+        go_left(block).wait_recv()
+        add_into(part_buf.at[rows_of(block)], from_right.at[block])
+        go_left(block).start()
+
+    @pl.when(place == 0)
+    def _():
+        for block in (3, 2, 1):
+            go_right(block).start()
+
+    @pl.when(place == 3)
+    def _():
+        for block in (0, 1, 2):
+            go_left(block).start()
+
+    @pl.when(place == 1)
+    def _():
+        on_right(3)
+        on_right(2)
+        on_left(0)
+
+    @pl.when(place == 2)
+    def _():
+        on_left(0)
+        on_left(1)
+        on_right(3)
+
+    resid[...] = tokens_buf[rows_of(place), :].astype(jnp.float32) + part_buf[
+        rows_of(place), :
+    ].astype(jnp.float32)
+
+    @pl.when(place > 0)
+    def _():
+        go_right(place).wait_recv()
+        resid[...] += from_left[place].astype(jnp.float32)
+
+    @pl.when(place < group - 1)
+    def _():
+        go_left(place).wait_recv()
+        resid[...] += from_right[place].astype(jnp.float32)
+
+    total = resid[...]
+    inverse = lax.rsqrt(jnp.mean(total * total, axis=-1, keepdims=True) + NORM_EPSILON)
+    inverse_two[...] = inverse
+    hidden_in = (total * inverse * small_full[1:2, :]).astype(jnp.bfloat16)
+    logits = dot_nt(hidden_in, small_full[...].astype(jnp.bfloat16))
+    lane = lax.broadcasted_iota(jnp.int32, logits.shape, 1)
+    chosen = [
+        jnp.sum(jnp.where(lane == named + 2, logits, 0.0), axis=1, keepdims=True)
+        for named in (first_col, second_col)
+    ]
+    top = jnp.maximum(chosen[0], chosen[1])
+    raised = [jnp.exp(entry - top) for entry in chosen]
+    both = raised[0] + raised[1]
+    gate = [entry / both for entry in raised]
+    for number in range(2):
+        gates[:, number : number + 1] = gate[number]
+    sent[...] = dot_nn(hits[0] + hits[1], hidden_in).astype(jnp.bfloat16)
+    d_out = jnp.where(live_col, 1.0, 0.0) * cotangent_buf[...].astype(jnp.float32)
+    d_back[...] = (
+        dot_nn(hits[0], (gate[0] * d_out).astype(jnp.bfloat16))
+        + dot_nn(hits[1], (gate[1] * d_out).astype(jnp.bfloat16))
+    ).astype(jnp.bfloat16)
+
+    for store in stores:
+        store.wait()
+    gather_qkv.drain()
+    gather_out.drain()
+    for k in range(1, parts):
+        small_copy(k).wait_send()
+    for block in range(group):
+
+        @pl.when(block > place)
+        def _():
+            go_right(block).wait_send()
+
+        @pl.when(block < place)
+        def _():
+            go_left(block).wait_send()
+
+        @pl.when((block <= place) & (place < group - 1))
+        def _():
+            pass_on(block, 0, right).wait_send()
+
+        @pl.when((block >= place) & (place > 0))
+        def _():
+            pass_on(block, 1, left).wait_send()
+
+    for part in range(2):
+        for r in (1, 2, 3):
+            slice_copy(r, part).wait()
+
+
+def attention_call(
+    lengths, tokens, w_qkv, w_out, small, w_gate_up, routes, order, cosine, sine, cotangent, group
+):
+    tok, width = tokens.shape
+    seq_len = tok * group
+    local_width = w_qkv.shape[2]
+    heads = local_width // HEAD_DIM
+    slots = tok * routes.shape[1]
+    piece = w_qkv.shape[1]
+    low, full = jnp.bfloat16, jnp.float32
+    pair_cols = jnp.concatenate([routes, order[:, None], jnp.zeros((tok, 5), jnp.int32)], axis=1)
+    pair_rows = pair_cols.T
+    anywhere = pl.BlockSpec(memory_space=pl.ANY)
+    inside = pl.BlockSpec(memory_space=pltpu.VMEM)
+    narrow = jax.ShapeDtypeStruct((seq_len, local_width), low)
+    flops = 2 * seq_len * width * local_width * 4 + 4 * seq_len * seq_len * local_width
+    return pl.pallas_call(
+        functools.partial(attention_kernel, heads),
+        out_shape=(
+            jax.ShapeDtypeStruct((seq_len, width), low),
+            jax.ShapeDtypeStruct((seq_len, width), low),
+            jax.ShapeDtypeStruct((3, width, local_width), low),
+            jax.ShapeDtypeStruct((local_width, width), low),
+            jax.ShapeDtypeStruct((3, piece, w_gate_up.shape[2] // 4), low),
+            jax.ShapeDtypeStruct((seq_len, 1), full),
+            narrow,
+            narrow,
+            narrow,
+            narrow,
+            jax.ShapeDtypeStruct((seq_len, heads), full),
+            jax.ShapeDtypeStruct((small.shape[0], width), full),
+            jax.ShapeDtypeStruct((tok, width), full),
+            jax.ShapeDtypeStruct((tok, 1), full),
+            jax.ShapeDtypeStruct((tok, 2), full),
+            jax.ShapeDtypeStruct((2, slots, tok), low),
+            jax.ShapeDtypeStruct((slots, width), low),
+            jax.ShapeDtypeStruct((slots, width), low),
+        ),
+        in_specs=[pl.BlockSpec(memory_space=pltpu.SMEM)] + [anywhere] * 10,
+        out_specs=(anywhere,) * 5 + (inside,) * 13,
+        scratch_shapes=[
+            pltpu.VMEM((seq_len, width), low),
+            pltpu.VMEM((seq_len, width), low),
+            pltpu.VMEM((3, width, local_width), low),
+            pltpu.VMEM((local_width, width), low),
+            pltpu.VMEM((seq_len, width), low),
+            pltpu.VMEM((group, tok, width), low),
+            pltpu.VMEM((group, tok, width), low),
+            pltpu.VMEM((tok, 8), jnp.int32),
+            pltpu.VMEM((8, tok), jnp.int32),
+            pltpu.VMEM(cosine.shape, full),
+            pltpu.VMEM(sine.shape, full),
+            pltpu.VMEM((tok, width), low),
+            pltpu.SemaphoreType.DMA((14,)),
+            pltpu.SemaphoreType.DMA((3, group)),
+            pltpu.SemaphoreType.DMA((3, group)),
+            pltpu.SemaphoreType.DMA((2, 2, 9)),
+            pltpu.SemaphoreType.DMA((2, width // piece)),
+            pltpu.SemaphoreType.DMA((2, 3, 2)),
+        ],
+        compiler_params=pltpu.CompilerParams(
+            collective_id=3, has_side_effects=True, vmem_limit_bytes=67043328
+        ),
+        cost_estimate=pl.CostEstimate(flops=flops, bytes_accessed=40000000, transcendentals=0),
+        name="attention",
+    )(
+        lengths,
+        tokens,
+        w_qkv,
+        w_out,
+        small,
+        w_gate_up,
+        pair_cols,
+        pair_rows,
+        cosine,
+        sine,
+        cotangent,
+    )
 
 
 def expert_step(gate_up_w, down_w, rows, d_rows_out):
@@ -1267,13 +1825,6 @@
     d_rows = contract_last(d_gate_up, gate_up_w).astype(jnp.bfloat16)
     grad_gate_up = contract_first(rows, d_gate_up)
     return out, d_rows, grad_gate_up, grad_down
-
-
-def experts_split_hidden(w_gate_up, w_down, rows, d_rows_out):
-    out, d_rows, grad_gate_up, grad_down = experts_call(
-        rows, d_rows_out, chip_slices(w_gate_up), w_down[0]
-    )
-    return out, d_rows, grad_gate_up, grad_down[None]
 
 
 def experts_gather_weights(w_gate_up, w_down, rows, d_rows_out):
@@ -1398,16 +1949,14 @@
     own_position = own_start + jnp.arange(tok_dev, dtype=jnp.int32)
     live_own = own_position < lengths[0]
     live_rows = live_own.astype(jnp.float32)[:, None]
-    split = dp_size == 8 and group_size == 4
-    first_expert = lax.axis_index("expert") if split else 0
-    target, kept_pair = slot_table(routes, order, live_own, capacity, first_expert, group_size)
+    target, kept_pair = slot_table(routes, order, live_own, capacity)
     slot_ids = jnp.arange(slots, dtype=jnp.int32)
     pair_hits = (slot_ids[:, None, None] == target[None]) & kept_pair[None]
     select = jnp.sum(pair_hits.astype(jnp.float32), axis=2).astype(jnp.bfloat16)
 
     inputs_float = tokens.astype(jnp.float32)
     input_normalized_hat, first_inverse_rms = normalize(inputs_float)
-    hat_all, inverse_all = normalize(tokens_all.astype(jnp.float32))
+    hat_all, _ = normalize(tokens_all.astype(jnp.float32))
     whole = (hat_all * first_norm_gain).astype(jnp.bfloat16)
     cosine, sine = rotary_tables(seq_len, head_size)
     projected = jnp.einsum("td,cde->cte", whole, qkv_full, preferred_element_type=jnp.float32)
@@ -1452,9 +2001,8 @@
             preferred_element_type=jnp.float32,
         )
     d_back = d_back.astype(jnp.bfloat16)
-    experts = experts_split_hidden if split else experts_gather_weights
     blocked = (group_size, capacity, width)
-    returned, d_sent, grad_gate_up, grad_down = experts(
+    returned, d_sent, grad_gate_up, grad_down = experts_gather_weights(
         w_gate_up, w_down, sent.reshape(blocked), d_back.reshape(blocked)
     )
     returned = returned.reshape(slots, width)
@@ -1490,58 +2038,29 @@
         scaled_two - hhat * jnp.mean(scaled_two * hhat, axis=-1, keepdims=True)
     )
     d_attn = d_resid.astype(jnp.bfloat16)
-    if split:
-        small_part = jnp.concatenate(
-            [jnp.zeros((1, width)), gain_two_part[None], router_part.T, jnp.zeros((2, width))],
-            axis=0,
-        )
-        grad_normalized, grad_weights, small_own, gate_got = attention_back_call(
-            lengths,
-            d_attn,
-            tokens_all,
-            inverse_all,
-            whole,
-            out_full,
-            qkv_full,
-            query.reshape(seq_len, local_width),
-            key_rows.reshape(seq_len, local_width),
-            value.reshape(seq_len, local_width),
-            attended,
-            log_total[:, :, 0].T,
-            jnp.concatenate([cosine[:, 0], cosine[:, 0]], axis=1),
-            jnp.concatenate([sine[:, 0], -sine[:, 0]], axis=1),
-            small_part,
-            grad_gate_up,
-        )
-        grad_gate_up = widen_slices(gate_got)
-        grad_qkv = jnp.stack(
-            [grad_weights[:, c * local_width : (c + 1) * local_width] for c in range(3)]
-        )
-        grad_out = grad_weights[:, 3 * local_width :].T
-    else:
-        grad_normalized, grad_qkv, grad_out, first_gain_part = attention_back_plain(
-            lengths,
-            d_attn,
-            hat_all,
-            whole,
-            out_full,
-            qkv_full,
-            query,
-            key_rows,
-            value,
-            attended,
-            log_total,
-            cosine,
-            sine,
-        )
-        small_part = jnp.concatenate(
-            [first_gain_part[None], gain_two_part[None], router_part.T], axis=0
-        )
-        small_sum = lax.psum(small_part, ("dp", "expert"))
-        own_rows = width // dp_size
-        small_own = lax.dynamic_slice_in_dim(
-            small_sum, lax.axis_index("dp") * own_rows, own_rows, axis=1
-        )
+    grad_normalized, grad_qkv, grad_out, first_gain_part = attention_back_plain(
+        lengths,
+        d_attn,
+        hat_all,
+        whole,
+        out_full,
+        qkv_full,
+        query,
+        key_rows,
+        value,
+        attended,
+        log_total,
+        cosine,
+        sine,
+    )
+    small_part = jnp.concatenate(
+        [first_gain_part[None], gain_two_part[None], router_part.T], axis=0
+    )
+    small_sum = lax.psum(small_part, ("dp", "expert"))
+    own_rows = width // dp_size
+    small_own = lax.dynamic_slice_in_dim(
+        small_sum, lax.axis_index("dp") * own_rows, own_rows, axis=1
+    )
     first_scaled_input = grad_normalized * first_norm_gain
     grad_tokens = d_resid + first_inverse_rms * (
         first_scaled_input
@@ -1558,6 +2077,154 @@
         small_own[2 : 2 + group_size].T,
         grad_gate_up,
         grad_down,
+    )
+
+
+def on_device_split(
+    tokens,
+    w_qkv,
+    w_out,
+    attention_norm_gain,
+    gain_ffn,
+    w_router,
+    w_gate_up,
+    w_down,
+    lengths,
+    routes,
+    order,
+    cotangent,
+):
+    group = lax.axis_size("expert")
+    tok, width = tokens.shape
+    piece = w_router.shape[0]
+    local_width = w_qkv.shape[2]
+    slots = tok * routes.shape[1]
+    cosine, sine = rotary_constants(tok * group, HEAD_DIM)
+    small = jnp.concatenate(
+        [
+            attention_norm_gain[None],
+            gain_ffn[None],
+            w_router.T,
+            jnp.zeros((2, piece), jnp.bfloat16),
+        ],
+        axis=0,
+    ).astype(jnp.float32)
+    (
+        tokens_all,
+        whole,
+        qkv_full,
+        out_full,
+        w_got,
+        inverse_all,
+        query,
+        key_rows,
+        value,
+        attended,
+        log_total,
+        small_full,
+        resid,
+        inverse_two,
+        gates,
+        hits,
+        sent,
+        d_back,
+    ) = attention_call(
+        lengths,
+        tokens,
+        w_qkv,
+        w_out,
+        small,
+        w_gate_up,
+        routes,
+        order,
+        cosine,
+        sine,
+        cotangent,
+        group,
+    )
+    blocked = (group, slots // group, width)
+    returned, d_sent, grad_gate_up, grad_down = experts_call(
+        sent.reshape(blocked), d_back.reshape(blocked), w_gate_up, w_got, w_down
+    )
+    returned = returned.reshape(slots, width)
+    d_sent = d_sent.reshape(slots, width)
+
+    gain_one = small_full[0]
+    gain_two = small_full[1]
+    router_f = small_full[2 : 2 + group]
+    position = lax.axis_index("expert") * tok + jnp.arange(tok, dtype=jnp.int32)
+    live_rows = (position < lengths[0]).astype(jnp.float32)[:, None]
+    d_out = live_rows * cotangent.astype(jnp.float32)
+    hhat = resid * inverse_two
+    hidden_in = (hhat * gain_two).astype(jnp.bfloat16)
+    moe = jnp.zeros_like(resid)
+    d_gates_list = []
+    for index in range(2):
+        picked = contract_first(hits[index], returned)
+        d_gates_list.append(jnp.sum(d_out * picked, axis=-1))
+        moe = moe + gates[:, index : index + 1] * picked
+    output = (live_rows * (resid + moe)).astype(jnp.bfloat16)
+    d_gates = jnp.stack(d_gates_list, axis=1)
+    d_hidden = contract_first(hits[0] + hits[1], d_sent)
+    d_chosen = gates * (d_gates - jnp.sum(gates * d_gates, axis=1, keepdims=True))
+    expert_ids = jnp.arange(group, dtype=jnp.int32)
+    route_hits = (routes[:, :, None] == expert_ids[None, None, :]).astype(jnp.float32)
+    d_logits = jnp.sum(route_hits * d_chosen[:, :, None], axis=1)
+    d_hidden = d_hidden + jnp.dot(
+        d_logits, router_f, precision=HIGH, preferred_element_type=jnp.float32
+    )
+    router_part = jnp.dot(
+        d_logits.T,
+        hidden_in.astype(jnp.float32),
+        precision=HIGH,
+        preferred_element_type=jnp.float32,
+    )
+    gain_two_part = jnp.sum(d_hidden * hhat, axis=0)
+    scaled_two = d_hidden * gain_two
+    d_resid = d_out + inverse_two * (
+        scaled_two - hhat * jnp.mean(scaled_two * hhat, axis=-1, keepdims=True)
+    )
+    d_attn = d_resid.astype(jnp.bfloat16)
+    small_part = jnp.concatenate(
+        [jnp.zeros((1, width)), gain_two_part[None], router_part, jnp.zeros((2, width))], axis=0
+    )
+    grad_normalized, grad_weights, small_own, gate_got = attention_back_call(
+        lengths,
+        d_attn,
+        tokens_all,
+        inverse_all,
+        whole,
+        out_full,
+        qkv_full,
+        query,
+        key_rows,
+        value,
+        attended,
+        log_total,
+        cosine,
+        sine,
+        small_part,
+        grad_gate_up,
+    )
+    grad_qkv = jnp.stack(
+        [grad_weights[:, c * local_width : (c + 1) * local_width] for c in range(3)]
+    )
+    grad_out = grad_weights[:, 3 * local_width :].T
+    hat, inverse_one = normalize(tokens.astype(jnp.float32))
+    scaled_one = grad_normalized * gain_one
+    grad_tokens = d_resid + inverse_one * (
+        scaled_one - hat * jnp.mean(scaled_one * hat, axis=-1, keepdims=True)
+    )
+    return (
+        output,
+        grad_tokens.astype(jnp.bfloat16),
+        grad_qkv,
+        grad_out,
+        small_own[0],
+        small_own[1],
+        small_own[2 : 2 + group].T,
+        widen_slices(gate_got),
+        grad_down[None],
     )
 
 
@@ -1576,8 +2243,9 @@
         P(("dp", "expert")),
         P(("dp", "expert"), None),
     )
+    split = mesh.shape["dp"] == 8 and mesh.shape["expert"] == 4
     return jax.shard_map(
-        on_device,
+        on_device_split if split else on_device,
         mesh=mesh,
         in_specs=placed,
         out_specs=(

time: 538 us -> 463 us (0.86)
  the two profiles are of different devices: /device:TPU:0 before, /device:TPU:26 now
where the time goes in v4:
time: 463 us; the launch traced here: 456 us
  Pallas kernels  422 us (91%)
  other arithmetic  12.6 us (3%)
  local copies, waits for them, and re-layouts  11.7 us (3%)
  matrix products  7.54 us (2%)
    pallas_call x1, Pallas kernels, experts_call(): pl.pallas_call(functools.partial(experts_kernel, group), out_shape=(jax.S...  201 us
    pallas_call x1, Pallas kernels, attention_call(): pl.pallas_call(functools.partial(attention_kernel, heads), out_shape=(jax...  108 us
    pallas_call x1, Pallas kernels, attention_back_call(): pl.pallas_call(functools.partial(attention_back_kernel, heads), out_shape...  105 us

profile of v4, /device:TPU:26, one launch (start us, length us, event | category | flops | bytes accessed | tf_op | source)
XLA Modules:
  0.0 455.6 jit_solution(15526563410897779387)
XLA Ops:
  1.3 0.5 compare_convert_fusion
  1.8 0.7 broadcast_in_dim.39
  2.5 0.7 broadcast_in_dim.38
  3.1 0.1 pad.15.clone
  3.2 1.3 maximum_convert_fusion.small
  4.6 0.1 pad.11.clone
  4.6 1.4 fusion.23
  6.0 0.7 copy.45.pair_cols
  6.7 108.0 %attention.1 = (bf16[512,2048]{1,0:T(8,128)(2,1)}, bf16[512,2048]{1,0:T(8,128)(2,1)}, bf16[3,2048,512]{2,1,0:T(8,128)(2,1)}, bf16[512,2048]{1,0:T(8,128)(2,1)}, ...) custom-call(s32[1]{0:T(128)} %copy.51.length, ...), custom_call_target="tpu_custom_call" | custom-call | flops 4831838208 | bytes 40000000 | tf_op jit(solution)/shard_map/attention/pallas_call | solution.py:1748
  114.8 200.7 %experts.1 = (bf16[4,64,2048]{2,1,0:T(8,128)(2,1)}, bf16[4,64,2048]{2,1,0:T(8,128)(2,1)}, bf16[4,256,2816]{2,1,0:T(8,128)(2,1)}, f32[704,2048]{1,0:T(8,128)}) custom-call(bf16[4,64,2048]{2,1,0:T(8,128)(2,1)} %bitcast.66, bf16[4,64,2048]{2,1,0:T(8,128)(2,1)} %bitcast.67, bf16[1,256,11264]{2,1,0:T(8,128)(2,1)} %w_gate_up.3, ...), custom_call_target="tpu_custom_call" | custom-call | flops 53150220288 | bytes 20185088 | tf_op jit(solution)/shard_map/experts/pallas_call | solution.py:528
  315.5 0.0 copy-start.6
  315.5 0.0 copy-start
  315.5 0.0 copy-start.3
  315.5 0.0 copy-start.7
  315.5 0.0 copy-start.13
  315.5 1.7 fusion.13
  317.3 0.0 copy-done.6
  317.3 0.2 slice_reduce_fusion.1
  317.4 0.0 copy-done
  317.5 0.0 copy-done.3
  317.5 0.0 copy-done.7
  317.5 0.0 copy-done.13
  317.5 0.0 copy-start.10
  317.5 0.0 copy-start.8
  317.5 2.5 multiply_reduce_fusion.3
  320.0 0.0 copy-start.12
  320.0 0.0 copy-done.10
  320.0 0.1 reduce.2
  320.1 0.0 copy-done.8
  320.1 0.6 fusion.25
  320.8 1.6 fusion.11
  322.3 0.0 copy-start.5
  322.3 0.1 copy.46
  322.4 0.1 multiply_reduce_fusion.4
  322.6 0.1 copy.47
  322.7 0.1 copy.48
  322.8 0.0 copy-done.12
  322.8 1.3 multiply_reduce_fusion
  324.1 0.0 copy-done.5
  324.1 1.5 fusion.24
  325.7 0.4 fusion.8
  326.1 0.1 pad.6.clone
  326.2 0.7 maximum_maximum_fusion.small_part
  326.9 104.7 %attention_back.1 = (f32[128,2048]{1,0:T(8,128)}, f32[256,2048]{1,0:T(8,128)}, f32[8,256]{1,0:T(8,128)}, bf16[4,256,2816]{2,1,0:T(8,128)(2,1)}) custom-call(s32[1]{0:T(128)} %copy.51.length, bf16[128,2048]{1,0:T(8,128)(2,1)} %get-tuple-element.112.d_attn, bf16[512,2048]{1,0:T(8,128)(2,1)} %get-tuple-element.45.tokens_all, ...), custom_call_target="tpu_custom_call" | custom-call | flops 9932111872 | bytes 40000000 | tf_op jit(solution)/shard_map/attention_back/pallas_call | solution.py:1140
  431.6 0.0 copy-start.1
  431.6 0.0 copy-start.2
  431.6 0.0 copy-start.9
  431.6 1.3 fusion.7
  433.0 0.0 copy-start.4
  433.0 1.8 fusion.2
  434.8 0.0 copy-done.1
  434.8 0.0 copy-done.2
  434.8 0.0 copy-done.9
  434.8 2.4 fusion.6
  437.2 0.0 copy-done.4
  437.2 0.2 slice_bitcast_fusion
  437.4 0.0 copy-start.11
  437.4 1.3 pad_maximum_fusion
  438.7 1.0 copy.49
  439.7 0.0 copy-done.11
  439.7 0.6 fusion.26
  440.3 0.6 slice_bitcast_fusion.4
  440.9 8.4 %widen.1 = f32[256,11264]{1,0:T(8,128)} custom-call(s32[1]{0:T(128)} %bitcast.23.own_ref, bf16[4,256,2816]{2,1,0:T(8,128)(2,1)} %get-tuple-element.59.source), custom_call_target="tpu_custom_call" | custom-call | tf_op jit(solution)/shard_map/widen/pallas_call | solution.py:1222
  449.3 5.9 %copy.52 = f32[1,704,2048]{2,1,0:T(8,128)} copy(f32[1,704,2048]{2,1,0:T(8,128)} %bitcast.48) | data formatting | bytes 11534336
  (11 shorter events, 0.1 us)
Async XLA Ops:
  315.5 1.8 copy-start.6
  315.5 2.0 copy-start
  315.5 2.0 copy-start.3
  315.5 2.0 copy-start.7
  315.5 2.0 copy-start.13
  317.5 2.5 copy-start.10
  317.5 2.6 copy-start.8
  320.0 2.8 copy-start.12
  322.3 1.8 copy-start.5
  431.6 3.2 copy-start.1
  431.6 3.2 copy-start.2
  431.6 3.2 copy-start.9
  433.0 4.3 copy-start.4
  437.4 2.3 copy-start.11

commit v5 on v4

--- a/solution.py
+++ b/solution.py
@@ -71,7 +71,6 @@
     full_y,
     other_gate,
     other_down,
-    stage,
     ag_sems,
     rs_sems,
     weight_sems,
@@ -155,15 +154,25 @@
         x_copy(t, k).start()
         y_copy(t, k).start()
 
-    def relay(t, k):
+    def relay_a(t, k):
         y_copy(t, k).wait_recv()
         a_copy(t, k).start()
+
+    def relay_b(t, k):
         x_copy(t, k).wait_recv()
         b_copy(t, k).start()
 
     def arrived(t, k):
         a_copy(t, k).wait_recv()
         b_copy(t, k).wait_recv()
+        if t == 0 and k == 0:
+            for r in range(4):
+                for copy in w_keep(r):
+                    copy.wait()
+                for copy in w_share(r, 1 - core):
+                    copy.wait_recv()
+            down_keep.wait()
+            down_share().wait_recv()
 
     def half_x_copy(t, k):
         return remote(part(t, k, 3, 0, half), half_x.at[t, k], *rs(0, t, k), along_x)
@@ -193,10 +202,12 @@
             value = value + other[...].astype(jnp.float32)
         target[...] = value.astype(jnp.bfloat16)
 
-    def fulls_out(t, k):
+    def full_y_out(t, k):
         half_x_copy(t, k).wait_recv()
         add_into(part(t, k, 2, 0, half), half_x.at[t, k])
         full_y_copy(t, k).start()
+
+    def full_x_out(t, k):
         half_y_copy(t, k).wait_recv()
         add_into(part(t, k, 1, half, half), half_y.at[t, k])
         full_x_copy(t, k).start()
@@ -250,74 +261,108 @@
 
     down_keep = pltpu.make_async_copy(down_own, down_at(core), local_sems.at[9])
 
-    def forward(k):
-        base = k * chunk
+    def take(steps, k, number):
+        for at in range(group):
+            if (at, number) in steps:
+
+                @pl.when(k == at)
+                def _(events=steps[at, number]):
+                    for event, t, which in events:
+                        event(t, which)
+
+    blocks = hidden // LANES
+    spans = [(2 * j, min(2, blocks - 2 * j)) for j in range((blocks + 1) // 2)]
+    tiles = width // (2 * LANES)
+
+    def span(first, count):
+        return pl.ds(first * LANES, count * LANES)
+
+    def forward(k, carry):
+        at = pl.ds(pl.multiple_of(k * chunk, chunk), chunk)
 
         def tile(first, count):
-            gate_cols = pl.ds(pl.multiple_of(first * LANES, LANES), count * LANES)
-            up_cols = pl.ds(pl.multiple_of(hidden + first * LANES, LANES), count * LANES)
-            rows = rows_buf[0, base : base + chunk, :]
+            gate_cols, up_cols = span(first, count), span(blocks + first, count)
+            rows = rows_buf[0, at, :]
             if count == 1:
                 weights = jnp.concatenate([w_buf[:, gate_cols], w_buf[:, up_cols]], axis=1)
                 both = dot_nn(rows, weights)
-                gate = both[:, :LANES]
-                up = both[:, LANES:]
+                gate, up = both[:, :LANES], both[:, LANES:]
             else:
                 gate = dot_nn(rows, w_buf[:, gate_cols])
                 up = dot_nn(rows, w_buf[:, up_cols])
             sigmoid = 1.0 / (1.0 + jnp.exp(-gate))
-            gate_buf[base : base + chunk, gate_cols] = gate.astype(jnp.bfloat16)
-            gate_buf[base : base + chunk, up_cols] = up.astype(jnp.bfloat16)
-            act_buf[base : base + chunk, gate_cols] = (gate * sigmoid * up).astype(jnp.bfloat16)
-
-        def pair(j, carry):
-            tile(2 * j, 2)
-            return carry
-
-        blocks = hidden // LANES
-        lax.fori_loop(0, blocks // 2, pair, 0)
-        if blocks % 2:
-            tile(blocks - 1, 1)
-
-        def out_tile(j, carry):
-            cols = pl.ds(pl.multiple_of(j * 2 * LANES, 2 * LANES), 2 * LANES)
-            out = dot_nn(act_buf[base : base + chunk, :], down_buf[:, cols])
-            part_buf[0, base : base + chunk, cols] = out.astype(jnp.bfloat16)
-            return carry
-
-        lax.fori_loop(0, width // (2 * LANES), out_tile, 0)
-
-    def backward(k):
-        base = k * chunk
-
-        def tile(first, count):
-            rows = pl.ds(pl.multiple_of(first * LANES, LANES), count * LANES)
-            d_act = dot_nt(rows_buf[1, base : base + chunk, :], down_buf[rows, :])
-            up_rows = pl.ds(pl.multiple_of(hidden + first * LANES, LANES), count * LANES)
-            gate = gate_buf[base : base + chunk, rows].astype(jnp.float32)
-            up = gate_buf[base : base + chunk, up_rows].astype(jnp.float32)
+            gate_buf[at, gate_cols] = gate.astype(jnp.bfloat16)
+            gate_buf[at, up_cols] = up.astype(jnp.bfloat16)
+            act_buf[at, gate_cols] = (gate * sigmoid * up).astype(jnp.bfloat16)
+
+        take(forward_steps, k, 0)
+        for first, count in spans[:3]:
+            tile(first, count)
+        take(forward_steps, k, 1)
+        for first, count in spans[3:]:
+            tile(first, count)
+        take(forward_steps, k, 2)
+        for j in range(tiles):
+            cols = span(2 * j, 2)
+            out = dot_nn(act_buf[at, :], down_buf[:, cols])
+            part_buf[0, at, cols] = out.astype(jnp.bfloat16)
+        return carry
+
+    def backward(turn, carry):
+        k = (turn + 1) % group
+        at = pl.ds(pl.multiple_of(k * chunk, chunk), chunk)
+        take(backward_steps, k, 0)
+        for first, count in spans:
+            gate_cols, up_cols = span(first, count), span(blocks + first, count)
+            d_act = dot_nt(rows_buf[1, at, :], down_buf[gate_cols, :])
+            gate = gate_buf[at, gate_cols].astype(jnp.float32)
+            up = gate_buf[at, up_cols].astype(jnp.float32)
             sigmoid = 1.0 / (1.0 + jnp.exp(-gate))
             scaled = d_act * sigmoid
             d_gate = scaled * up * (1.0 + gate * (1.0 - sigmoid))
-            gate_buf[base : base + chunk, rows] = d_gate.astype(jnp.bfloat16)
-            gate_buf[base : base + chunk, up_rows] = (scaled * gate).astype(jnp.bfloat16)
-
-        def pair(j, carry):
-            tile(2 * j, 2)
-            return carry
-
-        blocks = hidden // LANES
-        lax.fori_loop(0, blocks // 2, pair, 0)
-        if blocks % 2:
-            tile(blocks - 1, 1)
-
-        def out_tile(j, carry):
-            cols = pl.ds(pl.multiple_of(j * 2 * LANES, 2 * LANES), 2 * LANES)
-            out = dot_nt(gate_buf[base : base + chunk, :], w_buf[cols, :])
-            part_buf[1, base : base + chunk, cols] = out.astype(jnp.bfloat16)
-            return carry
-
-        lax.fori_loop(0, width // (2 * LANES), out_tile, 0)
+            gate_buf[at, gate_cols] = d_gate.astype(jnp.bfloat16)
+            gate_buf[at, up_cols] = (scaled * gate).astype(jnp.bfloat16)
+        for side in range(2):
+            take(backward_steps, k, 1 + side)
+            for j in range(side * (tiles // 2), (side + 1) * (tiles // 2)):
+                cols = span(2 * j, 2)
+                out = dot_nt(gate_buf[at, :], w_buf[cols, :])
+                part_buf[1, at, cols] = out.astype(jnp.bfloat16)
+        return carry
+
+    forward_steps = {
+        (0, 0): [(spread, 0, 0), (spread, 1, 0), (spread, 0, 1), (relay_a, 0, 0), (relay_b, 0, 0), (relay_a, 1, 0), (relay_b, 1, 0), (spread, 0, 2), (relay_a, 0, 1), (relay_b, 0, 1), (arrived, 0, 0)],
+        (0, 2): [(spread, 0, 3)],
+        (1, 0): [(halves_out, 0, 0), (relay_a, 0, 2), (relay_b, 0, 2), (arrived, 0, 1)],
+        (1, 1): [(spread, 1, 1)],
+        (2, 0): [(relay_a, 0, 3), (relay_b, 0, 3), (halves_out, 0, 1), (spread, 1, 2), (arrived, 0, 2)],
+        (2, 2): [(spread, 1, 3)],
+        (3, 0): [(arrived, 0, 3)],
+        (3, 1): [(relay_a, 1, 1)],
+        (3, 2): [(relay_b, 1, 1), (full_y_out, 0, 0)],
+    }
+    backward_steps = {
+        (0, 0): [(arrived, 1, 0)],
+        (0, 1): [(full_y_out, 0, 3), (full_y_out, 1, 1)],
+        (0, 2): [(full_x_out, 1, 1)],
+        (1, 0): [(relay_a, 1, 2), (relay_b, 1, 2), (relay_a, 1, 3), (relay_b, 1, 3), (full_x_out, 0, 0), (full_y_out, 0, 1), (arrived, 1, 1)],
+        (1, 2): [(full_x_out, 0, 1), (halves_out, 0, 2)],
+        (2, 0): [(arrived, 1, 2)],
+        (2, 1): [(halves_out, 0, 3), (halves_out, 1, 1)],
+        (3, 0): [(home, 0, 0), (arrived, 1, 3)],
+        (3, 1): [(halves_out, 1, 2)],
+        (3, 2): [(full_x_out, 0, 2), (home, 0, 1), (full_y_out, 0, 2), (full_x_out, 0, 3)],
+    }
+    grad_steps = {
+        (0, 0): [(full_y_out, 1, 2)],
+        (1, 0): [(home, 0, 2), (full_x_out, 1, 2)],
+        (2, 0): [(halves_out, 1, 0), (halves_out, 1, 3)],
+        (2, 1): [(home, 0, 3)],
+        (2, 3): [(home, 1, 1)],
+        (4, 0): [(full_x_out, 1, 0), (full_y_out, 1, 0), (full_x_out, 1, 3), (home, 1, 2)],
+        (4, 1): [(full_y_out, 1, 3)],
+        (5, 0): [(home, 1, 0), (home, 1, 3)],
+    }
 
     own_copy(0).start()
     for k in range(1, group):
@@ -329,167 +374,92 @@
     down_keep.start()
     own_copy(1).start()
 
-    spread(0, 0)
-    spread(0, 1)
-    relay(0, 0)
     for k in range(1, group):
         z_copy(1, k).start()
-    spread(0, 2)
-    relay(0, 1)
-    arrived(0, 0)
-    for r in range(4):
-        for copy in w_keep(r):
-            copy.wait()
-        for copy in w_share(r, 1 - core):
-            copy.wait_recv()
-    down_keep.wait()
-    down_share().wait_recv()
-    forward(0)
-    spread(0, 3)
-    relay(0, 2)
-    arrived(0, 1)
-    forward(1)
-    spread(1, 0)
-    relay(0, 3)
-    arrived(0, 2)
-    forward(2)
-    spread(1, 1)
-    relay(1, 0)
-    arrived(0, 3)
-    forward(3)
-    spread(1, 2)
-    relay(1, 1)
-    arrived(1, 0)
-    backward(0)
-    spread(1, 3)
-    relay(1, 2)
-    arrived(1, 1)
-    halves_out(0, 0)
-    halves_out(0, 1)
-    backward(1)
-    relay(1, 3)
-    arrived(1, 2)
-    halves_out(0, 2)
-    halves_out(0, 3)
-    fulls_out(0, 0)
-    fulls_out(0, 1)
-    halves_out(1, 0)
-    backward(2)
-    arrived(1, 3)
-    fulls_out(0, 2)
-    fulls_out(0, 3)
-    halves_out(1, 1)
-    home(0, 0)
-    home(0, 1)
-    backward(3)
-    halves_out(1, 2)
-    halves_out(1, 3)
-    fulls_out(1, 0)
-    fulls_out(1, 1)
+
+    lax.fori_loop(0, group, forward, 0)
+    lax.fori_loop(0, group, backward, 0)
+    for event, t, which in grad_steps.get((0, 0), []):
+        event(t, which)
 
     act_t = down_buf.at[:, pl.ds(0, total)]
     rows_t = down_buf.at[pl.ds(0, piece), pl.ds(total, total)]
     send_down = w_buf.at[pl.ds(4 * piece, down_rows), pl.ds(0, width)]
 
     def send_gate(r):
-        return w_buf.at[pl.ds(r * piece, piece), :]
-
-    def turn(j, carry):
-        cols = pl.ds(pl.multiple_of(j * LANES, LANES), LANES)
-        act_t[cols, :] = act_buf[:, cols].T
-        return carry
-
-    lax.fori_loop(0, hidden // LANES, turn, 0)
+        return w_buf.at[pl.ds(pl.multiple_of(r * piece, piece), piece), :]
+
+    for j in range(blocks):
+        act_t[span(j, 1), :] = act_buf[:, span(j, 1)].T
 
     def down_grad(which, j):
-        cols = pl.ds(pl.multiple_of(j * 2 * LANES, 2 * LANES), 2 * LANES)
         rows = pl.ds(pl.multiple_of(which * down_rows, down_rows), down_rows)
-        return cols, dot_nn(act_t[rows, :], rows_buf[1, :, cols])
-
-    def down_for_partner(j, carry):
-        cols, value = down_grad(1 - core, j)
-        send_down[:, cols] = value.astype(jnp.bfloat16)
-        return carry
-
-    tiles = width // (2 * LANES)
-    lax.fori_loop(0, tiles, down_for_partner, 0)
+        return dot_nn(act_t[rows, :], rows_buf[1, :, span(2 * j, 2)])
+
+    def after(steps, number, r):
+        turns = {(turn, 0): events for (stage, turn), events in steps.items() if stage == number}
+        take(turns, r, 0)
+
+    after(grad_steps, 1, 0)
+    for j in range(tiles):
+        send_down[:, span(2 * j, 2)] = down_grad(1 - core, j).astype(jnp.bfloat16)
     down_send = remote(
         send_down, other_down, grad_sems.at[0, 4], grad_sems.at[1, 4], partner
     )
     down_send.start()
-    home(0, 2)
-    home(0, 3)
-    fulls_out(1, 2)
-    fulls_out(1, 3)
-
-    def gate_grad(r, which, store):
-        start = pl.multiple_of((chips[r] * 2 + which) * piece, piece)
+
+    def turned_rows(r, which):
+        step_y = r // 2
+        step_x = r % 2
+        chip = (at_y + step_y - 2 * at_y * step_y) * 2 + (at_x + step_x - 2 * at_x * step_x)
+        start = pl.multiple_of((chip * 2 + which) * piece, piece)
         rows_t[...] = rows_buf[0, :, pl.ds(start, piece)].T
-
-        def tile(j, carry):
-            cols = pl.ds(pl.multiple_of(j * 2 * LANES, 2 * LANES), 2 * LANES)
-            store(cols, dot_nn(rows_t[...], gate_buf[:, cols]))
-            return carry
-
-        lax.fori_loop(0, hidden2 // (2 * LANES), tile, 0)
 
     def gate_send(r):
         return remote(
             send_gate(r), other_gate.at[r], grad_sems.at[0, r], grad_sems.at[1, r], partner
         )
 
-    for r in range(4):
+    def gate_for_partner(r, carry):
+        after(grad_steps, 2, r)
+        turned_rows(r, 1 - core)
         target = send_gate(r)
-
-        def store(cols, value, target=target):
-            target[:, cols] = value.astype(jnp.bfloat16)
-
-        gate_grad(r, 1 - core, store)
+        for j in range(blocks):
+            cols = span(2 * j, 2)
+            target[:, cols] = dot_nn(rows_t[...], gate_buf[:, cols]).astype(jnp.bfloat16)
         gate_send(r).start()
-        if r == 0:
-            home(1, 0)
-            home(1, 1)
-        if r == 1:
-            home(1, 2)
-        if r == 2:
-            home(1, 3)
-
+        return carry
+
+    lax.fori_loop(0, 4, gate_for_partner, 0)
+    after(grad_steps, 3, 0)
     down_send.wait_recv()
 
-    def stage_copy(j):
-        cols = pl.ds(pl.multiple_of(j * 2 * LANES, 2 * LANES), 2 * LANES)
-        return pltpu.make_async_copy(
-            stage.at[j % 2], grad_down.at[:, cols], grad_sems.at[2, j % 2]
-        )
-
-    def down_for_self(j, carry):
-        cols, value = down_grad(core, j)
-
-        @pl.when(j >= 2)
-        def _():
-            stage_copy(j - 2).wait()
-
-        stage[j % 2] = value + other_down[:, cols].astype(jnp.float32)
-        stage_copy(j).start()
-        return carry
-
-    lax.fori_loop(0, tiles, down_for_self, 0)
+    for j in range(tiles):
+        cols = span(2 * j, 2)
+        value = down_grad(core, j) + other_down[:, cols].astype(jnp.float32)
+        other_down[:, cols] = value.astype(jnp.bfloat16)
+    down_out = pltpu.make_async_copy(other_down, grad_down, grad_sems.at[2, 0])
+    down_out.start()
 
     def gate_out(r):
         return pltpu.make_async_copy(other_gate.at[r], grad_gate_up.at[r], grad_sems.at[2, 2 + r])
 
-    for r in range(4):
+    def gate_for_self(r, carry):
+        after(grad_steps, 4, r)
         gate_send(r).wait_recv()
+        turned_rows(r, core)
         target = other_gate.at[r]
-
-        def store(cols, value, target=target):
+        for j in range(blocks):
+            cols = span(2 * j, 2)
+            value = dot_nn(rows_t[...], gate_buf[:, cols])
             target[:, cols] = (value + target[:, cols].astype(jnp.float32)).astype(jnp.bfloat16)
-
-        gate_grad(r, core, store)
         gate_out(r).start()
-
-    stage_copy(tiles - 2).wait()
-    stage_copy(tiles - 1).wait()
+        return carry
+
+    lax.fori_loop(0, 4, gate_for_self, 0)
+    after(grad_steps, 5, 0)
+
+    down_out.wait()
     for r in range(4):
         gate_out(r).wait()
         gate_send(r).wait_send()
@@ -531,7 +501,7 @@
             jax.ShapeDtypeStruct((group, cap, width), low),
             jax.ShapeDtypeStruct((group, cap, width), low),
             jax.ShapeDtypeStruct((4, piece, hidden2), low),
-            jax.ShapeDtypeStruct((down_rows, width), jnp.float32),
+            jax.ShapeDtypeStruct((down_rows, width), low),
         ),
         in_specs=[anywhere] * 5,
         out_specs=(anywhere,) * 4,
@@ -548,7 +518,6 @@
             pltpu.VMEM((2, group, cap, width), low),
             pltpu.VMEM((4, piece, hidden2), low),
             pltpu.VMEM((down_rows, width), low),
-            pltpu.VMEM((2, down_rows, 2 * LANES), jnp.float32),
             pltpu.SemaphoreType.DMA((2, 5, 2, group)),
             pltpu.SemaphoreType.DMA((2, 5, 2, group)),
             pltpu.SemaphoreType.DMA((2, 6)),
@@ -648,7 +617,15 @@
 def attention_back_kernel(
     heads,
     length,
-    d_attn,
+    returned,
+    d_sent,
+    resid,
+    inverse_two,
+    gates,
+    hits,
+    cotangent,
+    pair_cols,
+    small_full,
     tokens_all,
     inverse_all,
     whole,
@@ -661,12 +638,21 @@
     log_total,
     cosine,
     sine,
-    small_part,
     gate_grads,
-    grad_normed,
+    output,
+    grad_tokens,
     grad_weights,
     small_out,
     gate_got,
+    returned_buf,
+    d_sent_buf,
+    resid_buf,
+    inverse_two_buf,
+    gates_buf,
+    hits_buf,
+    cotangent_buf,
+    cols_buf,
+    small_full_buf,
     da_buf,
     tokens_buf,
     inverse_buf,
@@ -697,6 +683,7 @@
     small_recv,
     small_z,
     keep_buf,
+    sum_buf,
     load_sems,
     line_sems,
     sum_sems,
@@ -705,7 +692,7 @@
     small_sems,
     gate_sems,
 ):
-    tok, width = d_attn.shape
+    tok, width = cotangent.shape
     seq_len = tokens_all.shape[0]
     group = seq_len // tok
     local_width = w_out.shape[0]
@@ -743,6 +730,15 @@
         pltpu.make_async_copy(source, target, load_sems.at[number])
         for number, (source, target) in enumerate(
             [
+                (returned, returned_buf),
+                (hits, hits_buf),
+                (cotangent, cotangent_buf),
+                (resid, resid_buf),
+                (inverse_two, inverse_two_buf),
+                (gates, gates_buf),
+                (pair_cols, cols_buf),
+                (small_full, small_full_buf),
+                (d_sent, d_sent_buf),
                 (w_out, w_out_buf),
                 (query, query_buf),
                 (key_rows, key_buf),
@@ -755,12 +751,12 @@
                 (inverse_all, inverse_buf),
                 (whole, whole_buf),
                 (attended, attended_buf),
-                (small_part, small_buf),
                 (gate_grads.at[0], keep_buf),
             ]
         )
     ]
-    early = 7
+    first = 9
+    early = first + 7
     for load in loads[:early]:
         load.start()
 
@@ -768,19 +764,6 @@
 
     def rows_of(block):
         return pl.ds(pl.multiple_of(block * tok, tok), tok)
-
-    own_load = pltpu.make_async_copy(d_attn, da_buf.at[rows_of(place)], load_sems.at[14])
-    own_load.start()
-
-    def own_right():
-        return remote(
-            d_attn, da_buf.at[rows_of(place)], line_sems.at[0, place], line_sems.at[2, place], right
-        )
-
-    def own_left():
-        return remote(
-            d_attn, da_buf.at[rows_of(place)], line_sems.at[1, place], line_sems.at[2, place], left
-        )
 
     def pass_right(block):
         spot = da_buf.at[rows_of(block)]
@@ -789,14 +772,6 @@
     def pass_left(block):
         spot = da_buf.at[rows_of(block)]
         return remote(spot, spot, line_sems.at[1, block], line_sems.at[2, block], left)
-
-    @pl.when(place < group - 1)
-    def _():
-        own_right().start()
-
-    @pl.when(place > 0)
-    def _():
-        own_left().start()
 
     def gate_copy(r, peer):
         return remote(
@@ -808,6 +783,50 @@
         gate_copy(r, peers[r]).start()
     for load in loads[early:]:
         load.start()
+    for load in loads[:first]:
+        load.wait()
+
+    at = place * tok + lax.broadcasted_iota(jnp.int32, (tok, 1), 0)
+    live = jnp.where(at < length[0], 1.0, 0.0)
+    d_out = live * cotangent_buf[...].astype(jnp.float32)
+    total = resid_buf[...]
+    hhat = total * inverse_two_buf[...]
+    gate = [gates_buf[:, number : number + 1] for number in range(2)]
+    d_gate = []
+    for number in range(2):
+        picked = dot_nn(hits_buf[number].T, returned_buf[...])
+        d_gate.append(jnp.sum(d_out * picked, axis=-1, keepdims=True))
+        total = total + gate[number] * picked
+    output[...] = (live * total).astype(jnp.bfloat16)
+    mixed = gate[0] * d_gate[0] + gate[1] * d_gate[1]
+    d_chosen = [gate[number] * (d_gate[number] - mixed) for number in range(2)]
+    d_hidden = dot_nn((hits_buf[0] + hits_buf[1]).T, d_sent_buf[...])
+    gain_two = small_full_buf[1:2, :]
+    hidden_in = (hhat * gain_two).astype(jnp.bfloat16).astype(jnp.float32)
+    small_buf[...] = jnp.zeros_like(small_buf)
+    for expert in range(group):
+        d_logit = sum(
+            jnp.where(cols_buf[:, number : number + 1] == expert, d_chosen[number], 0.0)
+            for number in range(2)
+        )
+        row = slice(2 + expert, 3 + expert)
+        d_hidden = d_hidden + d_logit * small_full_buf[row, :]
+        small_buf[row, :] = jnp.sum(d_logit * hidden_in, axis=0, keepdims=True)
+    small_buf[1:2, :] = jnp.sum(d_hidden * hhat, axis=0, keepdims=True)
+    scaled = d_hidden * gain_two
+    shared = jnp.mean(scaled * hhat, axis=-1, keepdims=True)
+    d_resid = d_out + inverse_two_buf[...] * (scaled - hhat * shared)
+    resid_buf[...] = d_resid
+    da_buf[rows_of(place), :] = d_resid.astype(jnp.bfloat16)
+
+    @pl.when(place < group - 1)
+    def _():
+        pass_right(place).start()
+
+    @pl.when(place > 0)
+    def _():
+        pass_left(place).start()
+
     d_key_acc[...] = jnp.zeros_like(d_key_acc)
     d_value_acc[...] = jnp.zeros_like(d_value_acc)
 
@@ -835,9 +854,8 @@
                 jnp.bfloat16
             )
 
-    for load in loads[:early]:
+    for load in loads[first:early]:
         load.wait()
-    own_load.wait()
     attend_back(place)
 
     def arrive(step, carry):
@@ -858,7 +876,7 @@
     lax.fori_loop(0, group - 1, arrive, 0)
     for load in loads[early:]:
         load.wait()
-    keep = pltpu.make_async_copy(keep_buf, gate_got.at[0], load_sems.at[15])
+    keep = pltpu.make_async_copy(keep_buf, gate_got.at[0], load_sems.at[22])
     keep.start()
 
     for head in range(heads):
@@ -1050,17 +1068,25 @@
         total = total + small_z[k]
     small_out[...] = total
 
-    grad_normed[...] = normed_part[rows_of(place), :].astype(jnp.float32)
+    sum_buf[...] = normed_part[rows_of(place), :].astype(jnp.float32)
 
     @pl.when(place > 0)
     def _():
         go_right(place).wait_recv()
-        grad_normed[...] += from_left[place].astype(jnp.float32)
+        sum_buf[...] += from_left[place].astype(jnp.float32)
 
     @pl.when(place < group - 1)
     def _():
         go_left(place).wait_recv()
-        grad_normed[...] += from_right[place].astype(jnp.float32)
+        sum_buf[...] += from_right[place].astype(jnp.float32)
+
+    inverse_one = inverse_buf[rows_of(place), :]
+    hat = tokens_buf[rows_of(place), :].astype(jnp.float32) * inverse_one
+    scaled = sum_buf[...] * small_full_buf[0:1, :]
+    shared = jnp.mean(scaled * hat, axis=-1, keepdims=True)
+    grad_tokens[...] = (resid_buf[...] + inverse_one * (scaled - hat * shared)).astype(
+        jnp.bfloat16
+    )
 
     full_x_copy().wait_recv()
     full_y_copy().wait_recv()
@@ -1104,7 +1130,15 @@
 
 def attention_back_call(
     lengths,
-    d_attn,
+    returned,
+    d_sent,
+    resid,
+    inverse_two,
+    gates,
+    hits,
+    cotangent,
+    pair_cols,
+    small_full,
     tokens_all,
     inverse_all,
     whole,
@@ -1117,10 +1151,9 @@
     log_total,
     cosine,
     sine,
-    small_part,
     gate_grads,
 ):
-    tok, width = d_attn.shape
+    tok, width = cotangent.shape
     seq_len = tokens_all.shape[0]
     group = seq_len // tok
     local_width = w_out.shape[0]
@@ -1128,7 +1161,7 @@
     piece = gate_grads.shape[1]
     half = piece // 2
     parts = width // piece
-    small_rows = small_part.shape[0]
+    small_rows = small_full.shape[0]
     low, full = jnp.bfloat16, jnp.float32
     anywhere = pl.BlockSpec(memory_space=pl.ANY)
     inside = pl.BlockSpec(memory_space=pltpu.VMEM)
@@ -1140,14 +1173,24 @@
     return pl.pallas_call(
         functools.partial(attention_back_kernel, heads),
         out_shape=(
-            jax.ShapeDtypeStruct((tok, width), full),
+            jax.ShapeDtypeStruct((tok, width), low),
+            jax.ShapeDtypeStruct((tok, width), low),
             jax.ShapeDtypeStruct((piece, 4 * local_width), full),
             jax.ShapeDtypeStruct((small_rows, piece), full),
             jax.ShapeDtypeStruct(gate_grads.shape, low),
         ),
-        in_specs=[pl.BlockSpec(memory_space=pltpu.SMEM)] + [anywhere] * 15,
-        out_specs=(inside, inside, inside, anywhere),
+        in_specs=[pl.BlockSpec(memory_space=pltpu.SMEM)] + [anywhere] * 22,
+        out_specs=(inside, inside, inside, inside, anywhere),
         scratch_shapes=[
+            like(returned),
+            like(d_sent),
+            like(resid),
+            like(inverse_two),
+            like(gates),
+            like(hits),
+            like(cotangent),
+            like(pair_cols),
+            like(small_full),
             pltpu.VMEM((seq_len, width), low),
             like(tokens_all),
             like(inverse_all),
@@ -1174,11 +1217,12 @@
             pltpu.VMEM((half, 4 * local_width), low),
             pltpu.VMEM((piece, 4 * local_width), low),
             pltpu.VMEM((piece, 4 * local_width), low),
-            like(small_part),
+            like(small_full),
             pltpu.VMEM((parts, small_rows, piece), full),
             pltpu.VMEM((group, small_rows, piece), full),
             pltpu.VMEM(gate_grads.shape[1:], low),
-            pltpu.SemaphoreType.DMA((16,)),
+            like(resid),
+            pltpu.SemaphoreType.DMA((23,)),
             pltpu.SemaphoreType.DMA((3, group)),
             pltpu.SemaphoreType.DMA((3, group)),
             pltpu.SemaphoreType.DMA((2, 4)),
@@ -1193,7 +1237,15 @@
         name="attention_back",
     )(
         lengths,
-        d_attn,
+        returned,
+        d_sent,
+        resid,
+        inverse_two,
+        gates,
+        hits,
+        cotangent,
+        pair_cols,
+        small_full,
         tokens_all,
         inverse_all,
         whole,
@@ -1206,33 +1258,122 @@
         log_total,
         cosine,
         sine,
-        small_part,
         gate_grads,
     )
 
 
-def widen_slices(grads):
-    chips, rows, hidden2 = grads.shape
-    own = (lax.axis_index("dp") // 2).astype(jnp.int32).reshape(1)
-    size = hidden2 // 2
-
-    def body(own_ref, source, target):
-        target[...] = source[0].astype(jnp.float32)
-
-    wide = pl.pallas_call(
-        body,
-        out_shape=jax.ShapeDtypeStruct((rows, chips * hidden2), jnp.float32),
-        grid_spec=pltpu.PrefetchScalarGridSpec(
-            num_scalar_prefetch=1,
-            grid=(2, chips),
-            in_specs=[
-                pl.BlockSpec((1, rows, size), lambda part, at, own_ref: (at ^ own_ref[0], 0, part))
-            ],
-            out_specs=pl.BlockSpec((rows, size), lambda part, at, own_ref: (0, part * chips + at)),
+def finish_kernel(
+    gate_got,
+    grad_down_low,
+    grad_tokens_low,
+    output_low,
+    grad_weights,
+    grad_gate_up,
+    grad_down,
+    grad_tokens,
+    output,
+    grad_qkv,
+    grad_out,
+    got_buf,
+    wide_buf,
+    low_buf,
+    down_buf,
+    tokens_buf,
+    output_buf,
+    weights_buf,
+    out_buf,
+    load_sems,
+    store_sems,
+):
+    chips = gate_got.shape[0]
+    size = gate_got.shape[2] // 2
+    local_width = grad_qkv.shape[2]
+    index = lax.axis_index("dp")
+    at_x = (index // 2) % 2
+    at_y = index // 4
+
+    def load(number, source, target):
+        return pltpu.make_async_copy(source, target, load_sems.at[number])
+
+    loads = [load(r, gate_got.at[r], got_buf.at[r]) for r in range(chips)] + [
+        load(4, grad_down_low, low_buf),
+        load(5, grad_weights, weights_buf),
+        load(6, grad_tokens_low, tokens_buf),
+        load(7, output_low, output_buf),
+    ]
+    for copy in loads:
+        copy.start()
+    stores = []
+
+    def store(source, target):
+        copy = pltpu.make_async_copy(source, target, store_sems.at[len(stores)])
+        copy.start()
+        stores.append(copy)
+
+    for r in range(chips):
+        loads[r].wait()
+        step_y = r // 2
+        step_x = r % 2
+        chip = (at_y + step_y - 2 * at_y * step_y) * 2 + (at_x + step_x - 2 * at_x * step_x)
+        for part in range(2):
+            wide_buf[2 * r + part] = got_buf[r, :, part * size : (part + 1) * size].astype(
+                jnp.float32
+            )
+            lanes = pl.ds(pl.multiple_of((part * chips + chip) * size, LANES), size)
+            store(wide_buf.at[2 * r + part], grad_gate_up.at[0, :, lanes])
+    loads[4].wait()
+    down_buf[...] = low_buf[...].astype(jnp.float32)
+    store(down_buf, grad_down.at[0])
+    loads[5].wait()
+    out_buf[...] = weights_buf[:, 3 * local_width :].T
+    for c in range(3):
+        store(weights_buf.at[:, pl.ds(c * local_width, local_width)], grad_qkv.at[c])
+    store(out_buf, grad_out)
+    loads[6].wait()
+    store(tokens_buf, grad_tokens)
+    loads[7].wait()
+    store(output_buf, output)
+    for copy in stores:
+        copy.wait()
+
+
+def finish_call(gate_got, grad_down, grad_tokens, output, grad_weights):
+    chips, rows, hidden2 = gate_got.shape
+    local_width = grad_weights.shape[1] // 4
+    full = jnp.float32
+    anywhere = pl.BlockSpec(memory_space=pl.ANY)
+    out_t = (local_width, rows)
+
+    def like(array, kind=None):
+        return pltpu.VMEM(array.shape, kind or array.dtype)
+
+    return pl.pallas_call(
+        finish_kernel,
+        out_shape=(
+            jax.ShapeDtypeStruct((1, rows, chips * hidden2), full),
+            jax.ShapeDtypeStruct((1,) + grad_down.shape, full),
+            jax.ShapeDtypeStruct(grad_tokens.shape, grad_tokens.dtype),
+            jax.ShapeDtypeStruct(output.shape, output.dtype),
+            jax.ShapeDtypeStruct((3, rows, local_width), full),
+            jax.ShapeDtypeStruct(out_t, full),
         ),
-        name="widen",
-    )(own, grads)
-    return wide[None]
+        in_specs=[anywhere] * 5,
+        out_specs=(anywhere,) * 6,
+        scratch_shapes=[
+            like(gate_got),
+            pltpu.VMEM((2 * chips, rows, hidden2 // 2), full),
+            like(grad_down),
+            like(grad_down, full),
+            like(grad_tokens),
+            like(output),
+            like(grad_weights),
+            pltpu.VMEM(out_t, full),
+            pltpu.SemaphoreType.DMA((8,)),
+            pltpu.SemaphoreType.DMA((15,)),
+        ],
+        compiler_params=pltpu.CompilerParams(vmem_limit_bytes=67043328),
+        name="finish",
+    )(gate_got, grad_down, grad_tokens, output, grad_weights)
 
 
 def rotary_constants(length_total, head_size):
@@ -1730,16 +1871,15 @@
 
 
 def attention_call(
-    lengths, tokens, w_qkv, w_out, small, w_gate_up, routes, order, cosine, sine, cotangent, group
+    lengths, tokens, w_qkv, w_out, small, w_gate_up, pair_cols, cosine, sine, cotangent, group
 ):
     tok, width = tokens.shape
     seq_len = tok * group
     local_width = w_qkv.shape[2]
     heads = local_width // HEAD_DIM
-    slots = tok * routes.shape[1]
+    slots = tok * 2
     piece = w_qkv.shape[1]
     low, full = jnp.bfloat16, jnp.float32
-    pair_cols = jnp.concatenate([routes, order[:, None], jnp.zeros((tok, 5), jnp.int32)], axis=1)
     pair_rows = pair_cols.T
     anywhere = pl.BlockSpec(memory_space=pl.ANY)
     inside = pl.BlockSpec(memory_space=pltpu.VMEM)
@@ -2097,7 +2237,6 @@
     group = lax.axis_size("expert")
     tok, width = tokens.shape
     piece = w_router.shape[0]
-    local_width = w_qkv.shape[2]
     slots = tok * routes.shape[1]
     cosine, sine = rotary_constants(tok * group, HEAD_DIM)
     small = jnp.concatenate(
@@ -2109,6 +2248,7 @@
         ],
         axis=0,
     ).astype(jnp.float32)
+    pair_cols = jnp.concatenate([routes, order[:, None], jnp.zeros((tok, 5), jnp.int32)], axis=1)
     (
         tokens_all,
         whole,
@@ -2135,8 +2275,7 @@
         w_out,
         small,
         w_gate_up,
-        routes,
-        order,
+        pair_cols,
         cosine,
         sine,
         cotangent,
@@ -2146,51 +2285,17 @@
     returned, d_sent, grad_gate_up, grad_down = experts_call(
         sent.reshape(blocked), d_back.reshape(blocked), w_gate_up, w_got, w_down
     )
-    returned = returned.reshape(slots, width)
-    d_sent = d_sent.reshape(slots, width)
-
-    gain_one = small_full[0]
-    gain_two = small_full[1]
-    router_f = small_full[2 : 2 + group]
-    position = lax.axis_index("expert") * tok + jnp.arange(tok, dtype=jnp.int32)
-    live_rows = (position < lengths[0]).astype(jnp.float32)[:, None]
-    d_out = live_rows * cotangent.astype(jnp.float32)
-    hhat = resid * inverse_two
-    hidden_in = (hhat * gain_two).astype(jnp.bfloat16)
-    moe = jnp.zeros_like(resid)
-    d_gates_list = []
-    for index in range(2):
-        picked = contract_first(hits[index], returned)
-        d_gates_list.append(jnp.sum(d_out * picked, axis=-1))
-        moe = moe + gates[:, index : index + 1] * picked
-    output = (live_rows * (resid + moe)).astype(jnp.bfloat16)
-    d_gates = jnp.stack(d_gates_list, axis=1)
-    d_hidden = contract_first(hits[0] + hits[1], d_sent)
-    d_chosen = gates * (d_gates - jnp.sum(gates * d_gates, axis=1, keepdims=True))
-    expert_ids = jnp.arange(group, dtype=jnp.int32)
-    route_hits = (routes[:, :, None] == expert_ids[None, None, :]).astype(jnp.float32)
-    d_logits = jnp.sum(route_hits * d_chosen[:, :, None], axis=1)
-    d_hidden = d_hidden + jnp.dot(
-        d_logits, router_f, precision=HIGH, preferred_element_type=jnp.float32
-    )
-    router_part = jnp.dot(
-        d_logits.T,
-        hidden_in.astype(jnp.float32),
-        precision=HIGH,
-        preferred_element_type=jnp.float32,
-    )
-    gain_two_part = jnp.sum(d_hidden * hhat, axis=0)
-    scaled_two = d_hidden * gain_two
-    d_resid = d_out + inverse_two * (
-        scaled_two - hhat * jnp.mean(scaled_two * hhat, axis=-1, keepdims=True)
-    )
-    d_attn = d_resid.astype(jnp.bfloat16)
-    small_part = jnp.concatenate(
-        [jnp.zeros((1, width)), gain_two_part[None], router_part, jnp.zeros((2, width))], axis=0
-    )
-    grad_normalized, grad_weights, small_own, gate_got = attention_back_call(
+    output, grad_tokens, grad_weights, small_own, gate_got = attention_back_call(
         lengths,
-        d_attn,
+        returned.reshape(slots, width),
+        d_sent.reshape(slots, width),
+        resid,
+        inverse_two,
+        gates,
+        hits,
+        cotangent,
+        pair_cols,
+        small_full,
         tokens_all,
         inverse_all,
         whole,
@@ -2203,28 +2308,21 @@
         log_total,
         cosine,
         sine,
-        small_part,
         grad_gate_up,
     )
-    grad_qkv = jnp.stack(
-        [grad_weights[:, c * local_width : (c + 1) * local_width] for c in range(3)]
-    )
-    grad_out = grad_weights[:, 3 * local_width :].T
-    hat, inverse_one = normalize(tokens.astype(jnp.float32))
-    scaled_one = grad_normalized * gain_one
-    grad_tokens = d_resid + inverse_one * (
-        scaled_one - hat * jnp.mean(scaled_one * hat, axis=-1, keepdims=True)
+    grad_gate_up, grad_down, grad_tokens, output, grad_qkv, grad_out = finish_call(
+        gate_got, grad_down, grad_tokens, output, grad_weights
     )
     return (
         output,
-        grad_tokens.astype(jnp.bfloat16),
+        grad_tokens,
         grad_qkv,
         grad_out,
         small_own[0],
         small_own[1],
         small_own[2 : 2 + group].T,
-        widen_slices(gate_got),
-        grad_down[None],
+        grad_gate_up,
+        grad_down,
     )
 
 

time: 463 us -> 407 us (0.88)
  the two profiles are of different devices: /device:TPU:26 before, /device:TPU:0 now
where the time goes in v5:
time: 407 us; the launch traced here: 401 us
  Pallas kernels  392 us (96%)
  local copies, waits for them, and re-layouts  4.84 us (1%)
    pallas_call x1, Pallas kernels, experts_call(): pl.pallas_call(functools.partial(experts_kernel, group), out_shape=(jax.S...  163 us
    pallas_call x1, Pallas kernels, attention_call(): pl.pallas_call(functools.partial(attention_kernel, heads), out_shape=(jax...  113 us
    pallas_call x1, Pallas kernels, attention_back_call(): pl.pallas_call(functools.partial(attention_back_kernel, heads), out_shape...  105 us
    pallas_call x1, Pallas kernels, finish_call(): pl.pallas_call(finish_kernel, out_shape=(jax.ShapeDtypeStruct((1, rows, c...  10.3 us

profile of v5, /device:TPU:0, one launch (start us, length us, event | category | flops | bytes accessed | tf_op | source)
XLA Modules:
  0.0 401.5 jit_solution(10926700063845131471)
XLA Ops:
  1.3 0.1 pad.6.clone
  1.4 0.1 pad.2.clone
  1.5 0.7 broadcast_in_dim.15
  2.1 0.7 broadcast_in_dim.16
  2.8 1.3 maximum_convert_fusion.small
  4.1 1.4 fusion
  5.5 0.7 copy.26.pair_cols
  6.2 113.5 %attention.1 = (bf16[512,2048]{1,0:T(8,128)(2,1)}, bf16[512,2048]{1,0:T(8,128)(2,1)}, bf16[3,2048,512]{2,1,0:T(8,128)(2,1)}, bf16[512,2048]{1,0:T(8,128)(2,1)}, ...) custom-call(s32[1]{0:T(128)S(6)} %copy.28.length, ...), custom_call_target="tpu_custom_call" | custom-call | flops 4831838208 | bytes 40000000 | tf_op jit(solution)/shard_map/attention/pallas_call | solution.py:1888
  119.7 162.9 %experts.1 = (bf16[4,64,2048]{2,1,0:T(8,128)(2,1)}, bf16[4,64,2048]{2,1,0:T(8,128)(2,1)}, bf16[4,256,2816]{2,1,0:T(8,128)(2,1)}, bf16[704,2048]{1,0:T(8,128)(2,1)}) custom-call(bf16[4,64,2048]{2,1,0:T(8,128)(2,1)} %bitcast.18, bf16[4,64,2048]{2,1,0:T(8,128)(2,1)} %bitcast.19, bf16[1,256,11264]{2,1,0:T(8,128)(2,1)} %w_gate_up.3, ...), custom_call_target="tpu_custom_call" | custom-call | flops 53150220288 | bytes 20185088 | tf_op jit(solution)/shard_map/experts/pallas_call | solution.py:498
  282.6 105.3 %attention_back.1 = (bf16[128,2048]{1,0:T(8,128)(2,1)}, bf16[128,2048]{1,0:T(8,128)(2,1)}, f32[256,2048]{1,0:T(8,128)}, f32[8,256]{1,0:T(8,128)}, bf16[4,256,2816]{2,1,0:T(8,128)(2,1)}) custom-call(s32[1]{0:T(128)S(6)} %copy.28.length, bf16[256,2048]{1,0:T(8,128)(2,1)} %bitcast.16, bf16[256,2048]{1,0:T(8,128)(2,1)} %bitcast.17, ...), custom_call_target="tpu_custom_call" | custom-call | flops 9932111872 | bytes 40000000 | tf_op jit(solution)/shard_map/attention_back/pallas_call | solution.py:1173
  388.0 1.3 fusion.1
  389.3 1.3 slice_bitcast_fusion
  390.6 10.3 %finish.1 = (f32[1,256,11264]{2,1,0:T(8,128)}, f32[1,704,2048]{2,1,0:T(8,128)}, bf16[128,2048]{1,0:T(8,128)(2,1)}, bf16[128,2048]{1,0:T(8,128)(2,1)}, f32[3,256,512]{2,1,0:T(8,128)}, /*index=5*/f32[512,256]{1,0:T(8,128)}) custom-call(bf16[4,256,2816]{2,1,0:T(8,128)(2,1)} %get-tuple-element.63.gate_got, bf16[704,2048]{1,0:T(8,128)(2,1)} %get-tuple-element.64.grad_down_low, ...), custom_call_target="tpu_custom_call" | custom-call | tf_op jit(solution)/shard_map/finish/pallas_call | solution.py:1350
  (2 shorter events, 0.0 us)

commit v6 on v5

--- a/solution.py
+++ b/solution.py
@@ -624,7 +624,7 @@
     gates,
     hits,
     cotangent,
-    pair_cols,
+    pair_rows,
     small_full,
     tokens_all,
     inverse_all,
@@ -651,7 +651,7 @@
     gates_buf,
     hits_buf,
     cotangent_buf,
-    cols_buf,
+    rows_buf,
     small_full_buf,
     da_buf,
     tokens_buf,
@@ -736,7 +736,7 @@
                 (resid, resid_buf),
                 (inverse_two, inverse_two_buf),
                 (gates, gates_buf),
-                (pair_cols, cols_buf),
+                (pair_rows, rows_buf),
                 (small_full, small_full_buf),
                 (d_sent, d_sent_buf),
                 (w_out, w_out_buf),
@@ -804,9 +804,16 @@
     gain_two = small_full_buf[1:2, :]
     hidden_in = (hhat * gain_two).astype(jnp.bfloat16).astype(jnp.float32)
     small_buf[...] = jnp.zeros_like(small_buf)
+    square = (tok, tok)
+    same = lax.broadcasted_iota(jnp.int32, square, 0) == lax.broadcasted_iota(jnp.int32, square, 1)
+    named = []
+    for number in range(2):
+        row = rows_buf[number : number + 1, :].astype(jnp.float32)
+        kept = jnp.where(same, jnp.broadcast_to(row, square), 0.0)
+        named.append(jnp.sum(kept, axis=1, keepdims=True).astype(jnp.int32))
     for expert in range(group):
         d_logit = sum(
-            jnp.where(cols_buf[:, number : number + 1] == expert, d_chosen[number], 0.0)
+            jnp.where(named[number] == expert, d_chosen[number], 0.0)
             for number in range(2)
         )
         row = slice(2 + expert, 3 + expert)
@@ -1137,7 +1144,7 @@
     gates,
     hits,
     cotangent,
-    pair_cols,
+    pair_rows,
     small_full,
     tokens_all,
     inverse_all,
@@ -1189,7 +1196,7 @@
             like(gates),
             like(hits),
             like(cotangent),
-            like(pair_cols),
+            like(pair_rows),
             like(small_full),
             pltpu.VMEM((seq_len, width), low),
             like(tokens_all),
@@ -1244,7 +1251,7 @@
         gates,
         hits,
         cotangent,
-        pair_cols,
+        pair_rows,
         small_full,
         tokens_all,
         inverse_all,
@@ -1377,15 +1384,12 @@
 
 
 def rotary_constants(length_total, head_size):
-    position = np.arange(length_total, dtype=np.float32)
+    low = 32
     steps = np.arange(head_size // 2, dtype=np.float32) * np.float32(2.0) / np.float32(head_size)
-    frequency = np.power(np.float32(THETA), -steps).astype(np.float32)
-    angles = (position[:, None] * frequency[None, :]).astype(np.float32)
-    cosine, sine = np.cos(angles), np.sin(angles)
-    return (
-        np.concatenate([cosine, cosine], axis=1).astype(np.float32),
-        np.concatenate([-sine, sine], axis=1).astype(np.float32),
-    )
+    frequency = np.power(np.float32(THETA), -steps).astype(np.float32).astype(np.float64)
+    position = np.concatenate([np.arange(0, length_total, low), np.arange(low)])
+    angles = position[:, None] * np.concatenate([frequency, frequency])[None, :]
+    return np.stack([np.cos(angles), np.sin(angles)]).astype(np.float32)
 
 
 def attention_kernel(
@@ -1396,10 +1400,8 @@
     w_out,
     small,
     w_gate_up,
-    pair_cols,
     pair_rows,
-    cosine,
-    sine,
+    angles,
     cotangent,
     tokens_all,
     whole,
@@ -1413,6 +1415,8 @@
     attended,
     log_total,
     small_full,
+    cosine_buf,
+    sine_buf,
     resid,
     inverse_two,
     gates,
@@ -1426,10 +1430,8 @@
     part_buf,
     from_left,
     from_right,
-    cols_buf,
     rows_buf,
-    cosine_buf,
-    sine_buf,
+    angles_buf,
     cotangent_buf,
     load_sems,
     line_sems,
@@ -1564,10 +1566,8 @@
             [
                 (tokens, tokens_buf.at[rows_of(place)]),
                 (small, small_full.at[:, piece_of(index)]),
-                (pair_cols, cols_buf),
                 (pair_rows, rows_buf),
-                (cosine, cosine_buf),
-                (sine, sine_buf),
+                (angles, angles_buf),
                 (cotangent, cotangent_buf),
             ]
         )
@@ -1614,10 +1614,16 @@
     for load in loads:
         load.wait()
 
-    cols = cols_buf[...]
     rows = rows_buf[...]
-    first_col, second_col, order_col = cols[:, 0:1], cols[:, 1:2], cols[:, 2:3]
     first_row, second_row, order_row = rows[0:1], rows[1:2], rows[2:3]
+    square = (tok, tok)
+    same = lax.broadcasted_iota(jnp.int32, square, 0) == lax.broadcasted_iota(jnp.int32, square, 1)
+
+    def as_column(row):
+        kept = jnp.where(same, jnp.broadcast_to(row.astype(jnp.float32), square), 0.0)
+        return jnp.sum(kept, axis=1, keepdims=True).astype(jnp.int32)
+
+    first_col, second_col, order_col = [as_column(r) for r in (first_row, second_row, order_row)]
     start = place * tok
     live_col = (start + lax.broadcasted_iota(jnp.int32, (tok, 1), 0)) < length[0]
     live_row = (start + lax.broadcasted_iota(jnp.int32, (1, tok), 1)) < length[0]
@@ -1636,6 +1642,19 @@
         target = jnp.where(live_row & (slot < cap), step * cap + slot, -1)
         hits[number] = jnp.where(slot_ids == target, 1.0, 0.0).astype(jnp.bfloat16)
 
+    low = 32
+    highs = seq_len // low
+    sign = jnp.where(
+        lax.broadcasted_iota(jnp.int32, (low, head_size), 1) < head_size // 2, -1.0, 1.0
+    )
+    cosine_low, sine_low = angles_buf[0, highs:, :], angles_buf[1, highs:, :]
+    for number in range(highs):
+        at = slice(number * low, (number + 1) * low)
+        cosine_high = angles_buf[0, number : number + 1, :]
+        sine_high = angles_buf[1, number : number + 1, :]
+        cosine_buf[at, :] = cosine_high * cosine_low - sine_high * sine_low
+        sine_buf[at, :] = sign * (sine_high * cosine_low + cosine_high * sine_low)
+
     for k in range(1, parts):
         small_copy(k).wait_recv()
 
@@ -1659,6 +1678,18 @@
             pass_on(block, 1, left).start()
 
         normalize_block(block)
+
+    def slice_copy(r, turn):
+        number = (by_x // 2, by_y // 2, by_both // 2)[r - 1]
+        part = turn
+        lanes = pl.ds(pl.multiple_of(part * ff + number * hidden, LANES), hidden)
+        return remote(
+            w_gate_up.at[0, :, lanes],
+            w_got.at[r - 1, :, pl.ds(part * hidden, hidden)],
+            slice_sems.at[0, r - 1, turn],
+            slice_sems.at[1, r - 1, turn],
+            (along_x, along_y, over)[r - 1],
+        )
 
     normalize_block(place)
     arrive(0)
@@ -1692,21 +1723,11 @@
     upper = place // 2
     project(upper * tok, seq_len - tok)
     gather_out.relay()
-
-    def slice_copy(r, part):
-        number = (by_x // 2, by_y // 2, by_both // 2)[r - 1]
-        lanes = pl.ds(pl.multiple_of(part * ff + number * hidden, LANES), hidden)
-        return remote(
-            w_gate_up.at[0, :, lanes],
-            w_got.at[r - 1, :, pl.ds(part * hidden, hidden)],
-            slice_sems.at[0, r - 1, part],
-            slice_sems.at[1, r - 1, part],
-            (along_x, along_y, over)[r - 1],
-        )
-
-    for part in range(2):
-        for r in (3, 1, 2):
-            slice_copy(r, part).start()
+    for turn in range(2):
+        for r in (1, 2):
+            slice_copy(r, turn).start()
+    for turn in range(2):
+        slice_copy(3, turn).start()
     gather_out.finish()
     arrive(2)
     project((1 - upper) * (seq_len - tok), tok)
@@ -1865,13 +1886,13 @@
         def _():
             pass_on(block, 1, left).wait_send()
 
-    for part in range(2):
+    for turn in range(2):
         for r in (1, 2, 3):
-            slice_copy(r, part).wait()
+            slice_copy(r, turn).wait()
 
 
 def attention_call(
-    lengths, tokens, w_qkv, w_out, small, w_gate_up, pair_cols, cosine, sine, cotangent, group
+    lengths, tokens, w_qkv, w_out, small, w_gate_up, pair_rows, angles, cotangent, group
 ):
     tok, width = tokens.shape
     seq_len = tok * group
@@ -1880,7 +1901,6 @@
     slots = tok * 2
     piece = w_qkv.shape[1]
     low, full = jnp.bfloat16, jnp.float32
-    pair_rows = pair_cols.T
     anywhere = pl.BlockSpec(memory_space=pl.ANY)
     inside = pl.BlockSpec(memory_space=pltpu.VMEM)
     narrow = jax.ShapeDtypeStruct((seq_len, local_width), low)
@@ -1900,6 +1920,8 @@
             narrow,
             jax.ShapeDtypeStruct((seq_len, heads), full),
             jax.ShapeDtypeStruct((small.shape[0], width), full),
+            jax.ShapeDtypeStruct((seq_len, HEAD_DIM), full),
+            jax.ShapeDtypeStruct((seq_len, HEAD_DIM), full),
             jax.ShapeDtypeStruct((tok, width), full),
             jax.ShapeDtypeStruct((tok, 1), full),
             jax.ShapeDtypeStruct((tok, 2), full),
@@ -1907,8 +1929,8 @@
             jax.ShapeDtypeStruct((slots, width), low),
             jax.ShapeDtypeStruct((slots, width), low),
         ),
-        in_specs=[pl.BlockSpec(memory_space=pltpu.SMEM)] + [anywhere] * 10,
-        out_specs=(anywhere,) * 5 + (inside,) * 13,
+        in_specs=[pl.BlockSpec(memory_space=pltpu.SMEM)] + [anywhere] * 8,
+        out_specs=(anywhere,) * 5 + (inside,) * 15,
         scratch_shapes=[
             pltpu.VMEM((seq_len, width), low),
             pltpu.VMEM((seq_len, width), low),
@@ -1917,10 +1939,8 @@
             pltpu.VMEM((seq_len, width), low),
             pltpu.VMEM((group, tok, width), low),
             pltpu.VMEM((group, tok, width), low),
-            pltpu.VMEM((tok, 8), jnp.int32),
-            pltpu.VMEM((8, tok), jnp.int32),
-            pltpu.VMEM(cosine.shape, full),
-            pltpu.VMEM(sine.shape, full),
+            pltpu.VMEM(pair_rows.shape, jnp.int32),
+            pltpu.VMEM(angles.shape, full),
             pltpu.VMEM((tok, width), low),
             pltpu.SemaphoreType.DMA((14,)),
             pltpu.SemaphoreType.DMA((3, group)),
@@ -1941,10 +1961,8 @@
         w_out,
         small,
         w_gate_up,
-        pair_cols,
         pair_rows,
-        cosine,
-        sine,
+        angles,
         cotangent,
     )
 
@@ -2238,7 +2256,7 @@
     tok, width = tokens.shape
     piece = w_router.shape[0]
     slots = tok * routes.shape[1]
-    cosine, sine = rotary_constants(tok * group, HEAD_DIM)
+    angles = rotary_constants(tok * group, HEAD_DIM)
     small = jnp.concatenate(
         [
             attention_norm_gain[None],
@@ -2248,7 +2266,7 @@
         ],
         axis=0,
     ).astype(jnp.float32)
-    pair_cols = jnp.concatenate([routes, order[:, None], jnp.zeros((tok, 5), jnp.int32)], axis=1)
+    pair_rows = jnp.concatenate([routes.T, order[None]], axis=0)
     (
         tokens_all,
         whole,
@@ -2262,6 +2280,8 @@
         attended,
         log_total,
         small_full,
+        cosine,
+        sine,
         resid,
         inverse_two,
         gates,
@@ -2275,9 +2295,8 @@
         w_out,
         small,
         w_gate_up,
-        pair_cols,
-        cosine,
-        sine,
+        pair_rows,
+        angles,
         cotangent,
         group,
     )
@@ -2294,7 +2313,7 @@
         gates,
         hits,
         cotangent,
-        pair_cols,
+        pair_rows,
         small_full,
         tokens_all,
         inverse_all,

time: 407 us -> 392 us (0.963)
  Pallas kernels: 392 us -> 378 us
    pallas_call x1, Pallas kernels: 163 us -> 152 us  [experts_call(): pl.pallas_call(functools.partial(experts_kernel, group), out_shape=(jax.S...]
where the time goes in v6:
time: 392 us; the launch traced here: 386 us
  Pallas kernels  378 us (96%)
  local copies, waits for them, and re-layouts  4.03 us (1%)
    pallas_call x1, Pallas kernels, experts_call(): pl.pallas_call(functools.partial(experts_kernel, group), out_shape=(jax.S...  152 us
    pallas_call x1, Pallas kernels, attention_call(): pl.pallas_call(functools.partial(attention_kernel, heads), out_shape=(jax...  111 us
    pallas_call x1, Pallas kernels, attention_back_call(): pl.pallas_call(functools.partial(attention_back_kernel, heads), out_shape...  105 us
    pallas_call x1, Pallas kernels, finish_call(): pl.pallas_call(finish_kernel, out_shape=(jax.ShapeDtypeStruct((1, rows, c...  10.3 us

profile of v6, /device:TPU:0, one launch (start us, length us, event | category | flops | bytes accessed | tf_op | source)
XLA Modules:
  0.0 386.1 jit_solution(8854362905414586857)
XLA Ops:
  1.3 0.1 pad.5.clone
  1.4 0.7 broadcast_in_dim.12
  2.0 0.7 broadcast_in_dim.13
  2.7 1.3 pad_add_fusion.pair_rows
  4.0 1.3 maximum_convert_fusion.small
  5.3 111.1 %attention.1 = (bf16[512,2048]{1,0:T(8,128)(2,1)}, bf16[512,2048]{1,0:T(8,128)(2,1)}, bf16[3,2048,512]{2,1,0:T(8,128)(2,1)}, bf16[512,2048]{1,0:T(8,128)(2,1)}, ...) custom-call(s32[1]{0:T(128)S(6)} %copy.22.length, ...), custom_call_target="tpu_custom_call" | custom-call | flops 4831838208 | bytes 40000000 | tf_op jit(solution)/shard_map/attention/pallas_call | solution.py:1908
  116.5 151.5 %experts.1 = (bf16[4,64,2048]{2,1,0:T(8,128)(2,1)}, bf16[4,64,2048]{2,1,0:T(8,128)(2,1)}, bf16[4,256,2816]{2,1,0:T(8,128)(2,1)}, bf16[704,2048]{1,0:T(8,128)(2,1)}) custom-call(bf16[4,64,2048]{2,1,0:T(8,128)(2,1)} %bitcast.18, bf16[4,64,2048]{2,1,0:T(8,128)(2,1)} %bitcast.19, bf16[1,256,11264]{2,1,0:T(8,128)(2,1)} %w_gate_up.3, ...), custom_call_target="tpu_custom_call" | custom-call | flops 53150220288 | bytes 20185088 | tf_op jit(solution)/shard_map/experts/pallas_call | solution.py:498
  268.0 104.5 %attention_back.1 = (bf16[128,2048]{1,0:T(8,128)(2,1)}, bf16[128,2048]{1,0:T(8,128)(2,1)}, f32[256,2048]{1,0:T(8,128)}, f32[8,256]{1,0:T(8,128)}, bf16[4,256,2816]{2,1,0:T(8,128)(2,1)}) custom-call(s32[1]{0:T(128)S(6)} %copy.22.length, bf16[256,2048]{1,0:T(8,128)(2,1)} %bitcast.16, bf16[256,2048]{1,0:T(8,128)(2,1)} %bitcast.17, ...), custom_call_target="tpu_custom_call" | custom-call | flops 9932111872 | bytes 40000000 | tf_op jit(solution)/shard_map/attention_back/pallas_call | solution.py:1180
  372.6 1.3 fusion
  373.9 1.3 slice_bitcast_fusion
  375.2 10.3 %finish.1 = (f32[1,256,11264]{2,1,0:T(8,128)}, f32[1,704,2048]{2,1,0:T(8,128)}, bf16[128,2048]{1,0:T(8,128)(2,1)}, bf16[128,2048]{1,0:T(8,128)(2,1)}, f32[3,256,512]{2,1,0:T(8,128)}, /*index=5*/f32[512,256]{1,0:T(8,128)}) custom-call(bf16[4,256,2816]{2,1,0:T(8,128)(2,1)} %get-tuple-element.67.gate_got, bf16[704,2048]{1,0:T(8,128)(2,1)} %get-tuple-element.68.grad_down_low, ...), custom_call_target="tpu_custom_call" | custom-call | tf_op jit(solution)/shard_map/finish/pallas_call | solution.py:1357
  (1 shorter events, 0.0 us)

commit v7 on v6

--- a/solution.py
+++ b/solution.py
@@ -389,20 +389,30 @@
     def send_gate(r):
         return w_buf.at[pl.ds(pl.multiple_of(r * piece, piece), piece), :]
 
-    for j in range(blocks):
-        act_t[span(j, 1), :] = act_buf[:, span(j, 1)].T
+    def turn(j, carry):
+        lanes = pl.ds(pl.multiple_of(j * LANES, LANES), LANES)
+        act_t[lanes, :] = act_buf[:, lanes].T
+        return carry
+
+    lax.fori_loop(0, blocks, turn, 0)
+
+    def pair_span(j):
+        return pl.ds(pl.multiple_of(j * 2 * LANES, 2 * LANES), 2 * LANES)
 
     def down_grad(which, j):
         rows = pl.ds(pl.multiple_of(which * down_rows, down_rows), down_rows)
-        return dot_nn(act_t[rows, :], rows_buf[1, :, span(2 * j, 2)])
+        return dot_nn(act_t[rows, :], rows_buf[1, :, pair_span(j)])
 
     def after(steps, number, r):
         turns = {(turn, 0): events for (stage, turn), events in steps.items() if stage == number}
         take(turns, r, 0)
 
     after(grad_steps, 1, 0)
-    for j in range(tiles):
-        send_down[:, span(2 * j, 2)] = down_grad(1 - core, j).astype(jnp.bfloat16)
+    def down_for_partner(j, carry):
+        send_down[:, pair_span(j)] = down_grad(1 - core, j).astype(jnp.bfloat16)
+        return carry
+
+    lax.fori_loop(0, tiles, down_for_partner, 0)
     down_send = remote(
         send_down, other_down, grad_sems.at[0, 4], grad_sems.at[1, 4], partner
     )
@@ -434,10 +444,13 @@
     after(grad_steps, 3, 0)
     down_send.wait_recv()
 
-    for j in range(tiles):
-        cols = span(2 * j, 2)
+    def down_for_self(j, carry):
+        cols = pair_span(j)
         value = down_grad(core, j) + other_down[:, cols].astype(jnp.float32)
         other_down[:, cols] = value.astype(jnp.bfloat16)
+        return carry
+
+    lax.fori_loop(0, tiles, down_for_self, 0)
     down_out = pltpu.make_async_copy(other_down, grad_down, grad_sems.at[2, 0])
     down_out.start()
 
@@ -624,7 +637,7 @@
     gates,
     hits,
     cotangent,
-    pair_rows,
+    routes_t,
     small_full,
     tokens_all,
     inverse_all,
@@ -736,7 +749,7 @@
                 (resid, resid_buf),
                 (inverse_two, inverse_two_buf),
                 (gates, gates_buf),
-                (pair_rows, rows_buf),
+                (routes_t, rows_buf),
                 (small_full, small_full_buf),
                 (d_sent, d_sent_buf),
                 (w_out, w_out_buf),
@@ -863,11 +876,14 @@
 
     for load in loads[first:early]:
         load.wait()
-    attend_back(place)
 
     def arrive(step, carry):
-        block = line_order(place, step)
-        pass_right(block).wait_recv()
+        later = (step + group - 2) // (group - 1)
+        block = place * (1 - later) + line_order(place, step - later) * later
+
+        @pl.when(step > 0)
+        def _():
+            pass_right(block).wait_recv()
 
         @pl.when((block < place) & (place < group - 1))
         def _():
@@ -880,7 +896,7 @@
         attend_back(block)
         return carry
 
-    lax.fori_loop(0, group - 1, arrive, 0)
+    lax.fori_loop(0, group, arrive, 0)
     for load in loads[early:]:
         load.wait()
     keep = pltpu.make_async_copy(keep_buf, gate_got.at[0], load_sems.at[22])
@@ -1144,7 +1160,7 @@
     gates,
     hits,
     cotangent,
-    pair_rows,
+    routes_t,
     small_full,
     tokens_all,
     inverse_all,
@@ -1196,7 +1212,7 @@
             like(gates),
             like(hits),
             like(cotangent),
-            like(pair_rows),
+            like(routes_t),
             like(small_full),
             pltpu.VMEM((seq_len, width), low),
             like(tokens_all),
@@ -1251,7 +1267,7 @@
         gates,
         hits,
         cotangent,
-        pair_rows,
+        routes_t,
         small_full,
         tokens_all,
         inverse_all,
@@ -1275,12 +1291,16 @@
     grad_tokens_low,
     output_low,
     grad_weights,
+    small,
     grad_gate_up,
     grad_down,
     grad_tokens,
     output,
     grad_qkv,
     grad_out,
+    gain_one,
+    gain_two,
+    router,
     got_buf,
     wide_buf,
     low_buf,
@@ -1289,6 +1309,7 @@
     output_buf,
     weights_buf,
     out_buf,
+    small_buf,
     load_sems,
     store_sems,
 ):
@@ -1307,6 +1328,7 @@
         load(5, grad_weights, weights_buf),
         load(6, grad_tokens_low, tokens_buf),
         load(7, output_low, output_buf),
+        load(8, small, small_buf),
     ]
     for copy in loads:
         copy.start()
@@ -1340,11 +1362,15 @@
     store(tokens_buf, grad_tokens)
     loads[7].wait()
     store(output_buf, output)
+    loads[8].wait()
+    gain_one[...] = small_buf[0:1, :]
+    gain_two[...] = small_buf[1:2, :]
+    router[...] = small_buf[2 : 2 + router.shape[0], :]
     for copy in stores:
         copy.wait()
 
 
-def finish_call(gate_got, grad_down, grad_tokens, output, grad_weights):
+def finish_call(gate_got, grad_down, grad_tokens, output, grad_weights, small, experts):
     chips, rows, hidden2 = gate_got.shape
     local_width = grad_weights.shape[1] // 4
     full = jnp.float32
@@ -1363,9 +1389,12 @@
             jax.ShapeDtypeStruct(output.shape, output.dtype),
             jax.ShapeDtypeStruct((3, rows, local_width), full),
             jax.ShapeDtypeStruct(out_t, full),
+            jax.ShapeDtypeStruct((1, rows), full),
+            jax.ShapeDtypeStruct((1, rows), full),
+            jax.ShapeDtypeStruct((experts, rows), full),
         ),
-        in_specs=[anywhere] * 5,
-        out_specs=(anywhere,) * 6,
+        in_specs=[anywhere] * 6,
+        out_specs=(anywhere,) * 6 + (pl.BlockSpec(memory_space=pltpu.VMEM),) * 3,
         scratch_shapes=[
             like(gate_got),
             pltpu.VMEM((2 * chips, rows, hidden2 // 2), full),
@@ -1375,12 +1404,13 @@
             like(output),
             like(grad_weights),
             pltpu.VMEM(out_t, full),
-            pltpu.SemaphoreType.DMA((8,)),
+            like(small),
+            pltpu.SemaphoreType.DMA((9,)),
             pltpu.SemaphoreType.DMA((15,)),
         ],
         compiler_params=pltpu.CompilerParams(vmem_limit_bytes=67043328),
         name="finish",
-    )(gate_got, grad_down, grad_tokens, output, grad_weights)
+    )(gate_got, grad_down, grad_tokens, output, grad_weights, small)
 
 
 def rotary_constants(length_total, head_size):
@@ -1398,9 +1428,12 @@
     tokens,
     w_qkv,
     w_out,
-    small,
+    gain_one,
+    gain_two,
+    router_t,
     w_gate_up,
-    pair_rows,
+    routes_t,
+    order_row,
     angles,
     cotangent,
     tokens_all,
@@ -1431,8 +1464,13 @@
     from_left,
     from_right,
     rows_buf,
+    order_buf,
     angles_buf,
     cotangent_buf,
+    gain_one_buf,
+    gain_two_buf,
+    router_buf,
+    small,
     load_sems,
     line_sems,
     sum_sems,
@@ -1505,7 +1543,7 @@
 
         def keep(self):
             return pltpu.make_async_copy(
-                self.source, self.spot(index), load_sems.at[8 + self.number]
+                self.source, self.spot(index), load_sems.at[16 + self.number]
             )
 
         def relay_x(self):
@@ -1565,8 +1603,11 @@
         for number, (source, target) in enumerate(
             [
                 (tokens, tokens_buf.at[rows_of(place)]),
-                (small, small_full.at[:, piece_of(index)]),
-                (pair_rows, rows_buf),
+                (gain_one, gain_one_buf),
+                (gain_two, gain_two_buf),
+                (router_t, router_buf),
+                (routes_t, rows_buf),
+                (order_row, order_buf),
                 (angles, angles_buf),
                 (cotangent, cotangent_buf),
             ]
@@ -1607,15 +1648,21 @@
             ring_peer(k),
         )
 
+    gather_qkv.begin()
+
+    for load in loads:
+        load.wait()
+    experts = router_t.shape[0]
+    small[...] = jnp.zeros_like(small)
+    small[0:1, :] = gain_one_buf[...].astype(jnp.float32)
+    small[1:2, :] = gain_two_buf[...].astype(jnp.float32)
+    small[2 : 2 + experts, :] = router_buf[...].astype(jnp.float32)
+    small_full[:, piece_of(index)] = small[...]
     for k in range(1, parts):
         small_copy(k).start()
-    gather_qkv.begin()
-
-    for load in loads:
-        load.wait()
 
     rows = rows_buf[...]
-    first_row, second_row, order_row = rows[0:1], rows[1:2], rows[2:3]
+    first_row, second_row, order_at = rows[0:1], rows[1:2], order_buf[...]
     square = (tok, tok)
     same = lax.broadcasted_iota(jnp.int32, square, 0) == lax.broadcasted_iota(jnp.int32, square, 1)
 
@@ -1623,11 +1670,11 @@
         kept = jnp.where(same, jnp.broadcast_to(row.astype(jnp.float32), square), 0.0)
         return jnp.sum(kept, axis=1, keepdims=True).astype(jnp.int32)
 
-    first_col, second_col, order_col = [as_column(r) for r in (first_row, second_row, order_row)]
+    first_col, second_col, order_col = [as_column(r) for r in (first_row, second_row, order_at)]
     start = place * tok
     live_col = (start + lax.broadcasted_iota(jnp.int32, (tok, 1), 0)) < length[0]
     live_row = (start + lax.broadcasted_iota(jnp.int32, (1, tok), 1)) < length[0]
-    before = order_col < order_row
+    before = order_col < order_at
 
     def count(mask):
         return jnp.sum(jnp.where(mask & live_col, 1.0, 0.0), axis=0, keepdims=True)
@@ -1892,7 +1939,19 @@
 
 
 def attention_call(
-    lengths, tokens, w_qkv, w_out, small, w_gate_up, pair_rows, angles, cotangent, group
+    lengths,
+    tokens,
+    w_qkv,
+    w_out,
+    gain_one,
+    gain_two,
+    router_t,
+    w_gate_up,
+    routes_t,
+    order_row,
+    angles,
+    cotangent,
+    group,
 ):
     tok, width = tokens.shape
     seq_len = tok * group
@@ -1919,7 +1978,7 @@
             narrow,
             narrow,
             jax.ShapeDtypeStruct((seq_len, heads), full),
-            jax.ShapeDtypeStruct((small.shape[0], width), full),
+            jax.ShapeDtypeStruct((8, width), full),
             jax.ShapeDtypeStruct((seq_len, HEAD_DIM), full),
             jax.ShapeDtypeStruct((seq_len, HEAD_DIM), full),
             jax.ShapeDtypeStruct((tok, width), full),
@@ -1929,7 +1988,7 @@
             jax.ShapeDtypeStruct((slots, width), low),
             jax.ShapeDtypeStruct((slots, width), low),
         ),
-        in_specs=[pl.BlockSpec(memory_space=pltpu.SMEM)] + [anywhere] * 8,
+        in_specs=[pl.BlockSpec(memory_space=pltpu.SMEM)] + [anywhere] * 11,
         out_specs=(anywhere,) * 5 + (inside,) * 15,
         scratch_shapes=[
             pltpu.VMEM((seq_len, width), low),
@@ -1939,10 +1998,15 @@
             pltpu.VMEM((seq_len, width), low),
             pltpu.VMEM((group, tok, width), low),
             pltpu.VMEM((group, tok, width), low),
-            pltpu.VMEM(pair_rows.shape, jnp.int32),
+            pltpu.VMEM(routes_t.shape, jnp.int32),
+            pltpu.VMEM(order_row.shape, jnp.int32),
             pltpu.VMEM(angles.shape, full),
             pltpu.VMEM((tok, width), low),
-            pltpu.SemaphoreType.DMA((14,)),
+            pltpu.VMEM(gain_one.shape, low),
+            pltpu.VMEM(gain_two.shape, low),
+            pltpu.VMEM(router_t.shape, low),
+            pltpu.VMEM((8, piece), full),
+            pltpu.SemaphoreType.DMA((18,)),
             pltpu.SemaphoreType.DMA((3, group)),
             pltpu.SemaphoreType.DMA((3, group)),
             pltpu.SemaphoreType.DMA((2, 2, 9)),
@@ -1959,9 +2023,12 @@
         tokens,
         w_qkv,
         w_out,
-        small,
+        gain_one,
+        gain_two,
+        router_t,
         w_gate_up,
-        pair_rows,
+        routes_t,
+        order_row,
         angles,
         cotangent,
     )
@@ -2257,16 +2324,7 @@
     piece = w_router.shape[0]
     slots = tok * routes.shape[1]
     angles = rotary_constants(tok * group, HEAD_DIM)
-    small = jnp.concatenate(
-        [
-            attention_norm_gain[None],
-            gain_ffn[None],
-            w_router.T,
-            jnp.zeros((2, piece), jnp.bfloat16),
-        ],
-        axis=0,
-    ).astype(jnp.float32)
-    pair_rows = jnp.concatenate([routes.T, order[None]], axis=0)
+    routes_t = routes.T
     (
         tokens_all,
         whole,
@@ -2293,9 +2351,12 @@
         tokens,
         w_qkv,
         w_out,
-        small,
+        attention_norm_gain[None],
+        gain_ffn[None],
+        w_router.T,
         w_gate_up,
-        pair_rows,
+        routes_t,
+        order.reshape(1, tok),
         angles,
         cotangent,
         group,
@@ -2313,7 +2374,7 @@
         gates,
         hits,
         cotangent,
-        pair_rows,
+        routes_t,
         small_full,
         tokens_all,
         inverse_all,
@@ -2329,17 +2390,25 @@
         sine,
         grad_gate_up,
     )
-    grad_gate_up, grad_down, grad_tokens, output, grad_qkv, grad_out = finish_call(
-        gate_got, grad_down, grad_tokens, output, grad_weights
-    )
+    (
+        grad_gate_up,
+        grad_down,
+        grad_tokens,
+        output,
+        grad_qkv,
+        grad_out,
+        gain_one,
+        gain_two,
+        router,
+    ) = finish_call(gate_got, grad_down, grad_tokens, output, grad_weights, small_own, group)
     return (
         output,
         grad_tokens,
         grad_qkv,
         grad_out,
-        small_own[0],
-        small_own[1],
-        small_own[2 : 2 + group].T,
+        gain_one.reshape(piece),
+        gain_two.reshape(piece),
+        router.T,
         grad_gate_up,
         grad_down,
     )

time: 392 us -> 383 us (0.977); the launches traced: 386 us -> 383 us
    pallas_call x1, Pallas kernels: 152 us -> 147 us  [experts_call(): pl.pallas_call(functools.partial(experts_kernel, group), out_shape=(jax.S...]
    pallas_call x1, Pallas kernels: 111 us -> 115 us  [attention_call(): pl.pallas_call(functools.partial(attention_kernel, heads), out_shape=(jax...]
where the time goes in v7:
time: 383 us
  Pallas kernels  379 us (99%)
    pallas_call x1, Pallas kernels, experts_call(): pl.pallas_call(functools.partial(experts_kernel, group), out_shape=(jax.S...  147 us
    pallas_call x1, Pallas kernels, attention_call(): pl.pallas_call(functools.partial(attention_kernel, heads), out_shape=(jax...  115 us
    pallas_call x1, Pallas kernels, attention_back_call(): pl.pallas_call(functools.partial(attention_back_kernel, heads), out_shape...  105 us
    pallas_call x1, Pallas kernels, finish_call(): pl.pallas_call(finish_kernel, out_shape=(jax.ShapeDtypeStruct((1, rows, c...  11 us

profile of v7, /device:TPU:0, one launch (start us, length us, event | category | flops | bytes accessed | tf_op | source)
XLA Modules:
  0.0 382.9 jit_solution(5001259482620923071)
XLA Ops:
  1.3 1.2 broadcast_in_dim.6.gain_one
  2.5 1.2 broadcast_in_dim.7.gain_two
  3.7 115.3 %attention.1 = (bf16[512,2048]{1,0:T(8,128)(2,1)}, bf16[512,2048]{1,0:T(8,128)(2,1)}, bf16[3,2048,512]{2,1,0:T(8,128)(2,1)}, bf16[512,2048]{1,0:T(8,128)(2,1)}, ...) custom-call(s32[1]{0:T(128)S(6)} %copy.22.length, ...), custom_call_target="tpu_custom_call" | custom-call | flops 4831838208 | bytes 40000000 | tf_op jit(solution)/shard_map/attention/pallas_call | solution.py:1967
  119.0 147.2 %experts.1 = (bf16[4,64,2048]{2,1,0:T(8,128)(2,1)}, bf16[4,64,2048]{2,1,0:T(8,128)(2,1)}, bf16[4,256,2816]{2,1,0:T(8,128)(2,1)}, bf16[704,2048]{1,0:T(8,128)(2,1)}) custom-call(bf16[4,64,2048]{2,1,0:T(8,128)(2,1)} %bitcast.19, bf16[4,64,2048]{2,1,0:T(8,128)(2,1)} %bitcast.20, bf16[1,256,11264]{2,1,0:T(8,128)(2,1)} %w_gate_up.3, ...), custom_call_target="tpu_custom_call" | custom-call | flops 53150220288 | bytes 20185088 | tf_op jit(solution)/shard_map/experts/pallas_call | solution.py:511
  266.2 105.5 %attention_back.1 = (bf16[128,2048]{1,0:T(8,128)(2,1)}, bf16[128,2048]{1,0:T(8,128)(2,1)}, f32[256,2048]{1,0:T(8,128)}, f32[8,256]{1,0:T(8,128)}, bf16[4,256,2816]{2,1,0:T(8,128)(2,1)}) custom-call(s32[1]{0:T(128)S(6)} %copy.22.length, bf16[256,2048]{1,0:T(8,128)(2,1)} %bitcast.17, bf16[256,2048]{1,0:T(8,128)(2,1)} %bitcast.18, ...), custom_call_target="tpu_custom_call" | custom-call | flops 9932111872 | bytes 40000000 | tf_op jit(solution)/shard_map/attention_back/pallas_call | solution.py:1196
  371.7 11.0 %finish.1 = (f32[1,256,11264]{2,1,0:T(8,128)}, f32[1,704,2048]{2,1,0:T(8,128)}, bf16[128,2048]{1,0:T(8,128)(2,1)}, bf16[128,2048]{1,0:T(8,128)(2,1)}, f32[3,256,...) custom-call(bf16[4,256,2816]{2,1,0:T(8,128)(2,1)} %get-tuple-element.70.gate_g, ...), custom_call_target="tpu_custom_call" | custom-call | tf_op jit(solution)/shard_map/finish/pallas_call | solution.py:1383

commit v8 on v7

--- a/solution.py
+++ b/solution.py
@@ -331,37 +331,33 @@
         return carry
 
     forward_steps = {
-        (0, 0): [(spread, 0, 0), (spread, 1, 0), (spread, 0, 1), (relay_a, 0, 0), (relay_b, 0, 0), (relay_a, 1, 0), (relay_b, 1, 0), (spread, 0, 2), (relay_a, 0, 1), (relay_b, 0, 1), (arrived, 0, 0)],
-        (0, 2): [(spread, 0, 3)],
-        (1, 0): [(halves_out, 0, 0), (relay_a, 0, 2), (relay_b, 0, 2), (arrived, 0, 1)],
-        (1, 1): [(spread, 1, 1)],
+        (0, 0): [(spread, 0, 0), (spread, 1, 0), (relay_a, 0, 0), (relay_b, 0, 0), (spread, 0, 1), (relay_a, 1, 0), (relay_b, 1, 0), (arrived, 0, 0)],
+        (0, 2): [(spread, 0, 2)],
+        (1, 0): [(relay_a, 0, 1), (relay_b, 0, 1), (spread, 0, 3), (halves_out, 0, 0), (relay_a, 0, 2), (relay_b, 0, 2), (spread, 1, 1), (arrived, 0, 1)],
         (2, 0): [(relay_a, 0, 3), (relay_b, 0, 3), (halves_out, 0, 1), (spread, 1, 2), (arrived, 0, 2)],
-        (2, 2): [(spread, 1, 3)],
-        (3, 0): [(arrived, 0, 3)],
-        (3, 1): [(relay_a, 1, 1)],
-        (3, 2): [(relay_b, 1, 1), (full_y_out, 0, 0)],
+        (2, 1): [(spread, 1, 3)],
+        (3, 0): [(relay_a, 1, 1), (arrived, 0, 3)],
+        (3, 1): [(relay_b, 1, 1), (full_y_out, 0, 0)],
     }
     backward_steps = {
-        (0, 0): [(arrived, 1, 0)],
-        (0, 1): [(full_y_out, 0, 3), (full_y_out, 1, 1)],
-        (0, 2): [(full_x_out, 1, 1)],
-        (1, 0): [(relay_a, 1, 2), (relay_b, 1, 2), (relay_a, 1, 3), (relay_b, 1, 3), (full_x_out, 0, 0), (full_y_out, 0, 1), (arrived, 1, 1)],
-        (1, 2): [(full_x_out, 0, 1), (halves_out, 0, 2)],
-        (2, 0): [(arrived, 1, 2)],
-        (2, 1): [(halves_out, 0, 3), (halves_out, 1, 1)],
-        (3, 0): [(home, 0, 0), (arrived, 1, 3)],
-        (3, 1): [(halves_out, 1, 2)],
-        (3, 2): [(full_x_out, 0, 2), (home, 0, 1), (full_y_out, 0, 2), (full_x_out, 0, 3)],
+        (0, 0): [(home, 0, 2), (halves_out, 1, 3), (arrived, 1, 0)],
+        (0, 2): [(home, 0, 3), (full_y_out, 1, 2), (full_x_out, 1, 2)],
+        (1, 0): [(full_x_out, 0, 0), (full_y_out, 0, 1), (relay_a, 1, 2), (relay_b, 1, 2), (relay_a, 1, 3), (relay_b, 1, 3), (arrived, 1, 1)],
+        (1, 1): [(full_x_out, 0, 1), (halves_out, 0, 2)],
+        (1, 2): [(halves_out, 0, 3), (home, 0, 0)],
+        (2, 0): [(halves_out, 1, 1), (arrived, 1, 2)],
+        (2, 2): [(home, 0, 1), (full_y_out, 0, 2), (full_x_out, 0, 2)],
+        (3, 0): [(full_y_out, 0, 3), (full_x_out, 0, 3), (halves_out, 1, 2), (arrived, 1, 3)],
+        (3, 1): [(full_y_out, 1, 1)],
+        (3, 2): [(full_x_out, 1, 1)],
     }
     grad_steps = {
-        (0, 0): [(full_y_out, 1, 2)],
-        (1, 0): [(home, 0, 2), (full_x_out, 1, 2)],
-        (2, 0): [(halves_out, 1, 0), (halves_out, 1, 3)],
-        (2, 1): [(home, 0, 3)],
-        (2, 3): [(home, 1, 1)],
-        (4, 0): [(full_x_out, 1, 0), (full_y_out, 1, 0), (full_x_out, 1, 3), (home, 1, 2)],
-        (4, 1): [(full_y_out, 1, 3)],
-        (5, 0): [(home, 1, 0), (home, 1, 3)],
+        (1, 0): [(halves_out, 1, 0)],
+        (2, 0): [(full_y_out, 1, 3), (full_x_out, 1, 3), (home, 1, 1)],
+        (2, 2): [(home, 1, 2)],
+        (2, 3): [(full_y_out, 1, 0), (full_x_out, 1, 0)],
+        (4, 0): [(home, 1, 3)],
+        (4, 2): [(home, 1, 0)],
     }
 
     own_copy(0).start()
@@ -1726,13 +1722,16 @@
 
         normalize_block(block)
 
+    early = piece // 4
+
     def slice_copy(r, turn):
         number = (by_x // 2, by_y // 2, by_both // 2)[r - 1]
-        part = turn
+        part = turn // 2
         lanes = pl.ds(pl.multiple_of(part * ff + number * hidden, LANES), hidden)
+        at = (pl.ds(0, early), pl.ds(early, piece - early), pl.ds(0, piece))[turn]
         return remote(
-            w_gate_up.at[0, :, lanes],
-            w_got.at[r - 1, :, pl.ds(part * hidden, hidden)],
+            w_gate_up.at[0, at, lanes],
+            w_got.at[r - 1, at, pl.ds(part * hidden, hidden)],
             slice_sems.at[0, r - 1, turn],
             slice_sems.at[1, r - 1, turn],
             (along_x, along_y, over)[r - 1],
@@ -1742,6 +1741,8 @@
     arrive(0)
     gather_qkv.relay()
     gather_out.begin()
+    for r in (1, 2):
+        slice_copy(r, 0).start()
     arrive(1)
     gather_qkv.finish()
 
@@ -1770,12 +1771,11 @@
     upper = place // 2
     project(upper * tok, seq_len - tok)
     gather_out.relay()
-    for turn in range(2):
+    for turn in (1, 2):
         for r in (1, 2):
             slice_copy(r, turn).start()
-    for turn in range(2):
+    for turn in range(3):
         slice_copy(3, turn).start()
-    gather_out.finish()
     arrive(2)
     project((1 - upper) * (seq_len - tok), tok)
 
@@ -1784,13 +1784,13 @@
         for number, (source, target) in enumerate(
             [
                 (w_qkv_buf, qkv_full),
-                (w_out_buf, out_full),
                 (tokens_buf, tokens_all),
                 (whole_buf, whole),
+                (w_out_buf, out_full),
             ]
         )
     ]
-    for store in stores:
+    for store in stores[:3]:
         store.start()
 
     for number in range(group):
@@ -1810,6 +1810,9 @@
             probs = (exponent / row_total).astype(jnp.bfloat16)
             attended[at, lanes] = dot_nn(probs, value[0:extent, lanes]).astype(jnp.bfloat16)
             log_total[at, head : head + 1] = top + jnp.log(row_total)
+
+    gather_out.finish()
+    stores[3].start()
 
     def out_tile(j, carry):
         lanes = piece_of(j)
@@ -1933,7 +1936,7 @@
         def _():
             pass_on(block, 1, left).wait_send()
 
-    for turn in range(2):
+    for turn in range(3):
         for r in (1, 2, 3):
             slice_copy(r, turn).wait()
 
@@ -2011,7 +2014,7 @@
             pltpu.SemaphoreType.DMA((3, group)),
             pltpu.SemaphoreType.DMA((2, 2, 9)),
             pltpu.SemaphoreType.DMA((2, width // piece)),
-            pltpu.SemaphoreType.DMA((2, 3, 2)),
+            pltpu.SemaphoreType.DMA((2, 3, 3)),
         ],
         compiler_params=pltpu.CompilerParams(
             collective_id=3, has_side_effects=True, vmem_limit_bytes=67043328

time: 383 us -> 378 us (0.987)
  Pallas kernels: 379 us -> 374 us
    pallas_call x1, Pallas kernels: 115 us -> 110 us  [attention_call(): pl.pallas_call(functools.partial(attention_kernel, heads), out_shape=(jax...]
where the time goes in v8:
time: 378 us
  Pallas kernels  374 us (99%)
    pallas_call x1, Pallas kernels, experts_call(): pl.pallas_call(functools.partial(experts_kernel, group), out_shape=(jax.S...  147 us
    pallas_call x1, Pallas kernels, attention_call(): pl.pallas_call(functools.partial(attention_kernel, heads), out_shape=(jax...  110 us
    pallas_call x1, Pallas kernels, attention_back_call(): pl.pallas_call(functools.partial(attention_back_kernel, heads), out_shape...  106 us
    pallas_call x1, Pallas kernels, finish_call(): pl.pallas_call(finish_kernel, out_shape=(jax.ShapeDtypeStruct((1, rows, c...  11 us

profile of v8, /device:TPU:0, one launch (start us, length us, event | category | flops | bytes accessed | tf_op | source)
XLA Modules:
  0.0 377.8 jit_solution(4992329605220169524)
XLA Ops:
  1.3 1.2 broadcast_in_dim.6.gain_one
  2.5 1.2 broadcast_in_dim.7.gain_two
  3.7 110.4 %attention.1 = (bf16[512,2048]{1,0:T(8,128)(2,1)}, bf16[512,2048]{1,0:T(8,128)(2,1)}, bf16[3,2048,512]{2,1,0:T(8,128)(2,1)}, bf16[512,2048]{1,0:T(8,128)(2,1)}, ...) custom-call(s32[1]{0:T(128)S(6)} %copy.22.length, ...), custom_call_target="tpu_custom_call" | custom-call | flops 4831838208 | bytes 40000000 | tf_op jit(solution)/shard_map/attention/pallas_call | solution.py:1970
  114.2 146.5 %experts.1 = (bf16[4,64,2048]{2,1,0:T(8,128)(2,1)}, bf16[4,64,2048]{2,1,0:T(8,128)(2,1)}, bf16[4,256,2816]{2,1,0:T(8,128)(2,1)}, bf16[704,2048]{1,0:T(8,128)(2,1)}) custom-call(bf16[4,64,2048]{2,1,0:T(8,128)(2,1)} %bitcast.19, bf16[4,64,2048]{2,1,0:T(8,128)(2,1)} %bitcast.20, bf16[1,256,11264]{2,1,0:T(8,128)(2,1)} %w_gate_up.3, ...), custom_call_target="tpu_custom_call" | custom-call | flops 53150220288 | bytes 20185088 | tf_op jit(solution)/shard_map/experts/pallas_call | solution.py:507
  260.7 106.0 %attention_back.1 = (bf16[128,2048]{1,0:T(8,128)(2,1)}, bf16[128,2048]{1,0:T(8,128)(2,1)}, f32[256,2048]{1,0:T(8,128)}, f32[8,256]{1,0:T(8,128)}, bf16[4,256,2816]{2,1,0:T(8,128)(2,1)}) custom-call(s32[1]{0:T(128)S(6)} %copy.22.length, bf16[256,2048]{1,0:T(8,128)(2,1)} %bitcast.17, bf16[256,2048]{1,0:T(8,128)(2,1)} %bitcast.18, ...), custom_call_target="tpu_custom_call" | custom-call | flops 9932111872 | bytes 40000000 | tf_op jit(solution)/shard_map/attention_back/pallas_call | solution.py:1192
  366.7 11.0 %finish.1 = (f32[1,256,11264]{2,1,0:T(8,128)}, f32[1,704,2048]{2,1,0:T(8,128)}, bf16[128,2048]{1,0:T(8,128)(2,1)}, bf16[128,2048]{1,0:T(8,128)(2,1)}, f32[3,256,...) custom-call(bf16[4,256,2816]{2,1,0:T(8,128)(2,1)} %get-tuple-element.70.gate_g, ...), custom_call_target="tpu_custom_call" | custom-call | tf_op jit(solution)/shard_map/finish/pallas_call | solution.py:1379

commit v9 on v8

--- a/solution.py
+++ b/solution.py
@@ -1004,25 +1004,30 @@
     def _():
         on_left(0)
 
-    def half_x_copy():
-        return remote(
-            own_part.at[3, pl.ds(0, half)], half_x, ring_sems.at[0, 0], ring_sems.at[1, 0], along_x
+    def lanes_of(c):
+        return pl.ds(c * (2 * local_width), 2 * local_width)
+
+    def ring_copy(number, c, source, target, peer):
+        sem = 4 * c + number
+        return remote(source, target, ring_sems.at[0, sem], ring_sems.at[1, sem], peer)
+
+    def half_x_copy(c):
+        source = own_part.at[3, pl.ds(0, half), lanes_of(c)]
+        return ring_copy(0, c, source, half_x.at[:, lanes_of(c)], along_x)
+
+    def half_y_copy(c):
+        source = own_part.at[3, pl.ds(half, half), lanes_of(c)]
+        return ring_copy(1, c, source, half_y.at[:, lanes_of(c)], along_y)
+
+    def full_x_copy(c):
+        return ring_copy(
+            2, c, own_part.at[1, :, lanes_of(c)], full_x.at[:, lanes_of(c)], along_x
         )
 
-    def half_y_copy():
-        return remote(
-            own_part.at[3, pl.ds(half, half)],
-            half_y,
-            ring_sems.at[0, 1],
-            ring_sems.at[1, 1],
-            along_y,
+    def full_y_copy(c):
+        return ring_copy(
+            3, c, own_part.at[2, :, lanes_of(c)], full_y.at[:, lanes_of(c)], along_y
         )
-
-    def full_x_copy():
-        return remote(own_part.at[1], full_x, ring_sems.at[0, 2], ring_sems.at[1, 2], along_x)
-
-    def full_y_copy():
-        return remote(own_part.at[2], full_y, ring_sems.at[0, 3], ring_sems.at[1, 3], along_y)
 
     def for_self(i, carry):
         r = 3 - i
@@ -1033,8 +1038,9 @@
 
         @pl.when(i == 0)
         def _():
-            half_x_copy().start()
-            half_y_copy().start()
+            for c in range(2):
+                half_x_copy(c).start()
+                half_y_copy(c).start()
 
         return carry
 
@@ -1066,12 +1072,13 @@
     for k in range(1, group):
         small_line_copy(k).start()
 
-    half_x_copy().wait_recv()
-    add_into(own_part.at[2, pl.ds(0, half)], half_x)
-    full_y_copy().start()
-    half_y_copy().wait_recv()
-    add_into(own_part.at[1, pl.ds(half, half)], half_y)
-    full_x_copy().start()
+    for c in range(2):
+        half_x_copy(c).wait_recv()
+        add_into(own_part.at[2, pl.ds(0, half), lanes_of(c)], half_x.at[:, lanes_of(c)])
+        full_y_copy(c).start()
+        half_y_copy(c).wait_recv()
+        add_into(own_part.at[1, pl.ds(half, half), lanes_of(c)], half_y.at[:, lanes_of(c)])
+        full_x_copy(c).start()
 
     @pl.when(place == 1)
     def _():
@@ -1107,21 +1114,23 @@
         jnp.bfloat16
     )
 
-    full_x_copy().wait_recv()
-    full_y_copy().wait_recv()
-    grad_weights[...] = (
-        own_part[0].astype(jnp.float32)
-        + full_x[...].astype(jnp.float32)
-        + full_y[...].astype(jnp.float32)
-    )
+    for c in range(2):
+        full_x_copy(c).wait_recv()
+        full_y_copy(c).wait_recv()
+        grad_weights[:, lanes_of(c)] = (
+            own_part[0, :, lanes_of(c)].astype(jnp.float32)
+            + full_x[:, lanes_of(c)].astype(jnp.float32)
+            + full_y[:, lanes_of(c)].astype(jnp.float32)
+        )
 
     for r in (1, 2, 3):
         gate_copy(r, peers[r]).wait()
     keep.wait()
-    half_x_copy().wait_send()
-    half_y_copy().wait_send()
-    full_x_copy().wait_send()
-    full_y_copy().wait_send()
+    for c in range(2):
+        half_x_copy(c).wait_send()
+        half_y_copy(c).wait_send()
+        full_x_copy(c).wait_send()
+        full_y_copy(c).wait_send()
     for r in range(4):
         pair_copy(r).wait_send()
     for k in range(1, parts):
@@ -1245,7 +1254,7 @@
             pltpu.SemaphoreType.DMA((3, group)),
             pltpu.SemaphoreType.DMA((3, group)),
             pltpu.SemaphoreType.DMA((2, 4)),
-            pltpu.SemaphoreType.DMA((2, 4)),
+            pltpu.SemaphoreType.DMA((2, 8)),
             pltpu.SemaphoreType.DMA((2, parts + group)),
             pltpu.SemaphoreType.DMA((2, 4)),
         ],
@@ -1650,8 +1659,10 @@
         load.wait()
     experts = router_t.shape[0]
     small[...] = jnp.zeros_like(small)
-    small[0:1, :] = gain_one_buf[...].astype(jnp.float32)
-    small[1:2, :] = gain_two_buf[...].astype(jnp.float32)
+    for number in range(piece // LANES):
+        lanes = slice(number * LANES, (number + 1) * LANES)
+        small[0:1, lanes] = gain_one_buf[number : number + 1, :].astype(jnp.float32)
+        small[1:2, lanes] = gain_two_buf[number : number + 1, :].astype(jnp.float32)
     small[2 : 2 + experts, :] = router_buf[...].astype(jnp.float32)
     small_full[:, piece_of(index)] = small[...]
     for k in range(1, parts):
@@ -2354,8 +2365,8 @@
         tokens,
         w_qkv,
         w_out,
-        attention_norm_gain[None],
-        gain_ffn[None],
+        attention_norm_gain.reshape(-1, LANES),
+        gain_ffn.reshape(-1, LANES),
         w_router.T,
         w_gate_up,
         routes_t,

time: 378 us -> 375 us (level)
  no operation moved by 1% of the time
where the time goes in v9:
time: 375 us
  Pallas kernels  373 us (99%)
    pallas_call x1, Pallas kernels, experts_call(): pl.pallas_call(functools.partial(experts_kernel, group), out_shape=(jax.S...  147 us
    pallas_call x1, Pallas kernels, attention_call(): pl.pallas_call(functools.partial(attention_kernel, heads), out_shape=(jax...  111 us
    pallas_call x1, Pallas kernels, attention_back_call(): pl.pallas_call(functools.partial(attention_back_kernel, heads), out_shape...  105 us
    pallas_call x1, Pallas kernels, finish_call(): pl.pallas_call(finish_kernel, out_shape=(jax.ShapeDtypeStruct((1, rows, c...  11 us

profile of v9, /device:TPU:0, one launch (start us, length us, event | category | flops | bytes accessed | tf_op | source)
XLA Modules:
  0.0 374.9 jit_solution(3915134425621022798)
XLA Ops:
  1.3 110.6 %attention.1 = (bf16[512,2048]{1,0:T(8,128)(2,1)}, bf16[512,2048]{1,0:T(8,128)(2,1)}, bf16[3,2048,512]{2,1,0:T(8,128)(2,1)}, bf16[512,2048]{1,0:T(8,128)(2,1)}, ...) custom-call(s32[1]{0:T(128)S(6)} %copy.22.length, ...), custom_call_target="tpu_custom_call" | custom-call | flops 4831838208 | bytes 40000000 | tf_op jit(solution)/shard_map/attention/pallas_call | solution.py:1981
  111.9 146.5 %experts.1 = (bf16[4,64,2048]{2,1,0:T(8,128)(2,1)}, bf16[4,64,2048]{2,1,0:T(8,128)(2,1)}, bf16[4,256,2816]{2,1,0:T(8,128)(2,1)}, bf16[704,2048]{1,0:T(8,128)(2,1)}) custom-call(bf16[4,64,2048]{2,1,0:T(8,128)(2,1)} %bitcast.23, bf16[4,64,2048]{2,1,0:T(8,128)(2,1)} %bitcast.24, bf16[1,256,11264]{2,1,0:T(8,128)(2,1)} %w_gate_up.3, ...), custom_call_target="tpu_custom_call" | custom-call | flops 53150220288 | bytes 20185088 | tf_op jit(solution)/shard_map/experts/pallas_call | solution.py:507
  258.4 105.4 %attention_back.1 = (bf16[128,2048]{1,0:T(8,128)(2,1)}, bf16[128,2048]{1,0:T(8,128)(2,1)}, f32[256,2048]{1,0:T(8,128)}, f32[8,256]{1,0:T(8,128)}, bf16[4,256,2816]{2,1,0:T(8,128)(2,1)}) custom-call(s32[1]{0:T(128)S(6)} %copy.22.length, bf16[256,2048]{1,0:T(8,128)(2,1)} %bitcast.21, bf16[256,2048]{1,0:T(8,128)(2,1)} %bitcast.22, ...), custom_call_target="tpu_custom_call" | custom-call | flops 9932111872 | bytes 40000000 | tf_op jit(solution)/shard_map/attention_back/pallas_call | solution.py:1201
  363.8 11.0 %finish.1 = (f32[1,256,11264]{2,1,0:T(8,128)}, f32[1,704,2048]{2,1,0:T(8,128)}, bf16[128,2048]{1,0:T(8,128)(2,1)}, bf16[128,2048]{1,0:T(8,128)(2,1)}, f32[3,256,...) custom-call(bf16[4,256,2816]{2,1,0:T(8,128)(2,1)} %get-tuple-element.70.gate_g, ...), custom_call_target="tpu_custom_call" | custom-call | tf_op jit(solution)/shard_map/finish/pallas_call | solution.py:1388

commit v10 on v9

--- a/solution.py
+++ b/solution.py
@@ -408,7 +408,7 @@
         send_down[:, pair_span(j)] = down_grad(1 - core, j).astype(jnp.bfloat16)
         return carry
 
-    lax.fori_loop(0, tiles, down_for_partner, 0)
+    lax.fori_loop(0, tiles, down_for_partner, 0, unroll=2)
     down_send = remote(
         send_down, other_down, grad_sems.at[0, 4], grad_sems.at[1, 4], partner
     )
@@ -446,7 +446,7 @@
         other_down[:, cols] = value.astype(jnp.bfloat16)
         return carry
 
-    lax.fori_loop(0, tiles, down_for_self, 0)
+    lax.fori_loop(0, tiles, down_for_self, 0, unroll=2)
     down_out = pltpu.make_async_copy(other_down, grad_down, grad_sems.at[2, 0])
     down_out.start()
 

time: 375 us -> 375 us (level)
  no operation moved by 1% of the time
where the time goes in v10:
time: 375 us
  Pallas kernels  373 us (99%)
    pallas_call x1, Pallas kernels, experts_call(): pl.pallas_call(functools.partial(experts_kernel, group), out_shape=(jax.S...  146 us
    pallas_call x1, Pallas kernels, attention_call(): pl.pallas_call(functools.partial(attention_kernel, heads), out_shape=(jax...  111 us
    pallas_call x1, Pallas kernels, attention_back_call(): pl.pallas_call(functools.partial(attention_back_kernel, heads), out_shape...  105 us
    pallas_call x1, Pallas kernels, finish_call(): pl.pallas_call(finish_kernel, out_shape=(jax.ShapeDtypeStruct((1, rows, c...  11 us

profile of v10, /device:TPU:0, one launch (start us, length us, event | category | flops | bytes accessed | tf_op | source)
XLA Modules:
  0.0 374.6 jit_solution(7770772346515599902)
XLA Ops:
  1.3 110.6 %attention.1 = (bf16[512,2048]{1,0:T(8,128)(2,1)}, bf16[512,2048]{1,0:T(8,128)(2,1)}, bf16[3,2048,512]{2,1,0:T(8,128)(2,1)}, bf16[512,2048]{1,0:T(8,128)(2,1)}, ...) custom-call(s32[1]{0:T(128)S(6)} %copy.22.length, ...), custom_call_target="tpu_custom_call" | custom-call | flops 4831838208 | bytes 40000000 | tf_op jit(solution)/shard_map/attention/pallas_call | solution.py:1981
  111.9 146.2 %experts.1 = (bf16[4,64,2048]{2,1,0:T(8,128)(2,1)}, bf16[4,64,2048]{2,1,0:T(8,128)(2,1)}, bf16[4,256,2816]{2,1,0:T(8,128)(2,1)}, bf16[704,2048]{1,0:T(8,128)(2,1)}) custom-call(bf16[4,64,2048]{2,1,0:T(8,128)(2,1)} %bitcast.23, bf16[4,64,2048]{2,1,0:T(8,128)(2,1)} %bitcast.24, bf16[1,256,11264]{2,1,0:T(8,128)(2,1)} %w_gate_up.3, ...), custom_call_target="tpu_custom_call" | custom-call | flops 53150220288 | bytes 20185088 | tf_op jit(solution)/shard_map/experts/pallas_call | solution.py:507
  258.1 105.4 %attention_back.1 = (bf16[128,2048]{1,0:T(8,128)(2,1)}, bf16[128,2048]{1,0:T(8,128)(2,1)}, f32[256,2048]{1,0:T(8,128)}, f32[8,256]{1,0:T(8,128)}, bf16[4,256,2816]{2,1,0:T(8,128)(2,1)}) custom-call(s32[1]{0:T(128)S(6)} %copy.22.length, bf16[256,2048]{1,0:T(8,128)(2,1)} %bitcast.21, bf16[256,2048]{1,0:T(8,128)(2,1)} %bitcast.22, ...), custom_call_target="tpu_custom_call" | custom-call | flops 9932111872 | bytes 40000000 | tf_op jit(solution)/shard_map/attention_back/pallas_call | solution.py:1201
  363.4 11.0 %finish.1 = (f32[1,256,11264]{2,1,0:T(8,128)}, f32[1,704,2048]{2,1,0:T(8,128)}, bf16[128,2048]{1,0:T(8,128)(2,1)}, bf16[128,2048]{1,0:T(8,128)(2,1)}, f32[3,256,...) custom-call(bf16[4,256,2816]{2,1,0:T(8,128)(2,1)} %get-tuple-element.70.gate_g, ...), custom_call_target="tpu_custom_call" | custom-call | tf_op jit(solution)/shard_map/finish/pallas_call | solution.py:1388
